TPU v7x, 32 devices: a whole 2x2x4 slice. The times are simulated.
32 devices in a mesh: dp: 4 (over y, core), expert: 8 (over z, x).
Axes of the slice: x: 2, y: 2, z: 4, core: 2. Of those that a mesh axis runs over, the one named last changes fastest.
Arguments:
- tokens: bfloat16 [4096, 2048], P(('dp', 'expert')), may hold values from -6 to 6
- d_mixed: bfloat16 [4096, 2048], P(('dp', 'expert')), may hold values from -6 to 6
- w_in: bfloat16 [32, 2048, 768], P('expert'), may hold values from -0.125 to 0.125
- w_out: bfloat16 [32, 384, 2048], P('expert'), may hold values from -0.3125 to 0.3125
- expert_ids: int32 [4096, 8], P(('dp', 'expert')), may hold values from 0 to 31, all different within a row; in each aligned block of 128 rows (0 to 127, 128 to 255, ...) at most 40 rows name the same one
- gate_fixed: int32 [4096, 8], P(('dp', 'expert')), may hold values from 1 to 65535
- placement: int32 [32], replicated, may hold values from 0 to 31, each once
Outputs:
- mixed: bfloat16 [4096, 2048], P(('dp', 'expert'))
- d_tokens: bfloat16 [4096, 2048], P(('dp', 'expert'))
- grad_in: bfloat16 [32, 2048, 768], P('expert', 'dp')
- grad_out: bfloat16 [32, 384, 2048], P('expert', None, 'dp')
Inputs may be any that keep to these rules, and one draw needn't show every extreme that they name: `expert_ids`: each row names 8 different experts. Among the rows of one device no expert is named more than 40 times, and in every draw some expert is named exactly 40 times by the rows of some device. Each number appears once: expert e's weights are in slot placement[e], held by expert-axis index placement[e] // 4.
All inputs are finite; a program needn't handle non-finite values.
Results may differ from a plain program's by a relative error of at most 0.009.
Values may be sent and summed in bfloat16 or wider, within the bound.
No kernel may reach another device: no remote copies, remote signals or barrier semaphores. Data moves between devices by JAX's collectives and lax.ppermute only.
A program may use at most 192 MiB of HBM per device.

v0:
```python
import jax
import jax.numpy as jnp
from jax import lax
from jax.sharding import PartitionSpec as P


def gather_routes(rows, position, scales):
    total = jnp.zeros((position.shape[0], rows.shape[1]), jnp.float32)
    for k in range(position.shape[1]):
        picked = jnp.take(rows, position[:, k], axis=0).astype(jnp.float32)
        total = total + scales[:, k : k + 1] * picked
    return total


def body(tokens, d_mixed, w_in, w_out, expert_ids, gate_fixed, placement):
    tok_rows, width = tokens.shape
    local_count = w_in.shape[0]
    hidden = w_out.shape[1]
    axis_count = lax.axis_size("expert")
    experts_all = local_count * axis_count
    top = expert_ids.shape[1]
    capacity = max(2, 5 * tok_rows * top // (4 * experts_all))
    slots = experts_all * capacity
    gates = gate_fixed.astype(jnp.float32)
    gates = gates / jnp.sum(gates, axis=1, keepdims=True)
    catalog = jnp.arange(experts_all, dtype=jnp.int32)
    slot_of = jnp.sum(jnp.where(expert_ids[:, :, None] == catalog, placement, 0), axis=2)
    flat_slot = slot_of.reshape(-1)
    onehot = (flat_slot[:, None] == catalog).astype(jnp.int32)
    rank = jnp.sum(jnp.cumsum(onehot, axis=0) * onehot, axis=1) - 1
    position = (flat_slot * capacity + rank).reshape(tok_rows, top)
    places = jnp.arange(slots, dtype=jnp.int32)
    match = position[:, :, None] == places
    dispatch = jnp.any(match, axis=1).astype(jnp.bfloat16)
    slot_gate = jnp.sum(jnp.where(match, gates[:, :, None], 0.0), axis=(0, 1))
    blocked = (axis_count, local_count, capacity, width)

    def to_slots(rows):
        return jnp.einsum("ts,td->sd", dispatch, rows, preferred_element_type=jnp.float32)

    x_send = to_slots(tokens).astype(jnp.bfloat16).reshape(blocked)
    x_recv = lax.all_to_all(x_send, "expert", split_axis=0, concat_axis=0, tiled=True)
    pre = jnp.einsum("secd,edf->secf", x_recv, w_in, preferred_element_type=jnp.float32)
    gate_part = pre[..., :hidden]
    up_part = pre[..., hidden:]
    sig = jax.nn.sigmoid(gate_part)
    silu = gate_part * sig
    act = (silu * up_part).astype(jnp.bfloat16)
    expert_out = jnp.einsum(
        "secf,efd->secd", act, w_out, preferred_element_type=jnp.float32
    ).astype(jnp.bfloat16)
    came_back = lax.all_to_all(
        expert_out, "expert", split_axis=0, concat_axis=0, tiled=True
    ).reshape(slots, width)
    mixed = gather_routes(came_back, position, gates).astype(jnp.bfloat16)
    d_recv = lax.all_to_all(
        (to_slots(d_mixed) * slot_gate[:, None]).astype(jnp.bfloat16).reshape(blocked),
        "expert",
        split_axis=0,
        concat_axis=0,
        tiled=True,
    )
    d_act = jnp.einsum("secd,efd->secf", d_recv, w_out, preferred_element_type=jnp.float32)
    d_gate = d_act * up_part * sig * (1.0 + gate_part * (1.0 - sig))
    d_up = d_act * silu
    d_pre = jnp.concatenate([d_gate, d_up], axis=3).astype(jnp.bfloat16)
    d_rows = jnp.einsum("secf,edf->secd", d_pre, w_in, preferred_element_type=jnp.float32).astype(
        jnp.bfloat16
    )
    returned = lax.all_to_all(d_rows, "expert", split_axis=0, concat_axis=0, tiled=True).reshape(
        slots, width
    )
    unit = jnp.ones((tok_rows, top), jnp.float32)
    d_tokens = gather_routes(returned, position, unit).astype(jnp.bfloat16)
    in_term = jnp.einsum("secd,secf->edf", x_recv, d_pre, preferred_element_type=jnp.float32)
    down_term = jnp.einsum("secf,secd->efd", act, d_recv, preferred_element_type=jnp.float32)
    summed_in, summed_out = (
        lax.psum_scatter(
            in_term.astype(jnp.bfloat16), "dp", scatter_dimension=1, tiled=True
        ).astype(jnp.float32),
        lax.psum_scatter(
            down_term.astype(jnp.bfloat16), "dp", scatter_dimension=2, tiled=True
        ).astype(jnp.float32),
    )
    grad_in = summed_in.astype(jnp.bfloat16)
    grad_out = summed_out.astype(jnp.bfloat16)
    return (mixed, d_tokens, grad_in, grad_out)


def solution(mesh):
    in_specs = (
        P(("dp", "expert"), None),
        P(("dp", "expert"), None),
        P("expert", None, None),
        P("expert", None, None),
        P(("dp", "expert"), None),
        P(("dp", "expert"), None),
        P(),
    )
    out_specs = (
        P(("dp", "expert"), None),
        P(("dp", "expert"), None),
        P("expert", "dp", None),
        P("expert", None, "dp"),
    )
    return jax.shard_map(body, mesh=mesh, in_specs=in_specs, out_specs=out_specs, check_vma=False)
```

profile of v0, /device:TPU:0, one launch (start us, length us, event | category | flops | bytes accessed | tf_op | source)
XLA Modules:
  0.0 633.6 jit_solution(1214796687438871560)
XLA Ops:
  8.3 9.0 %reduce-window.6 = s32[32,8,128]{2,1,0:T(8,128)S(1)} reduce-window(s32[32,8,128]{2,1,0:T(8,128)S(1)} %fusion.29, s32[]{:T(128)} %constant.5.clone.1), window={size=1x1x128 pad=0_0x0_0x127_0}, to_apply=%region_2.3 | reduce-window | flops 4161536 | bytes 262148 | tf_op jit(solution)/shard_map/reduce-window
  23.7 7.4 %all-to-all-start = ((bf16[8,4,40,2048]{3,2,1,0:T(8,128)(2,1)}), bf16[8,4,40,2048]{3,2,1,0:T(8,128)(2,1)}, u32[]{:S(2)}, u32[]{:S(2)}) async-start(bf16[8,4,40,2048]{3,2,1,0:T(8,128)(2,1)} %bitcast.110), calls=%async_computation | async-start | bytes 10485760 | tf_op jit(solution)/shard_map/all_to_all | solution.py:42
  35.8 111.0 %all-to-all-done = bf16[8,4,40,2048]{3,2,1,0:T(8,128)(2,1)} async-done(((bf16[8,4,40,2048]{3,2,1,0:T(8,128)(2,1)}), bf16[8,4,40,2048]{3,2,1,0:T(8,128)(2,1)}, u32[]{:S(2)}, u32[]{:S(2)}) %all-to-all-start) | async-done | bytes 5242912 | tf_op jit(solution)/shard_map/all_to_all | solution.py:42
  146.8 4.6 all-to-all-start.2
  152.1 12.4 %fusion.16 = f32[8,4,40,768]{3,2,0,1:T(8,128)} fusion(bf16[4,2048,768]{2,1,0:T(8,128)(2,1)} %param.11, bf16[8,4,40,2048]{3,2,1,0:T(8,128)(2,1)} %all-to-all-done), kind=kOutput, calls=%fused_computation.36 | convolution fusion | flops 4026531840 | bytes 21757952 | tf_op jit(solution)/shard_map/secd,edf->secf/dot_general | solution.py:43
  164.4 102.0 %all-to-all-done.2 = bf16[8,4,40,2048]{3,2,1,0:T(8,128)(2,1)} async-done(((bf16[8,4,40,2048]{3,2,1,0:T(8,128)(2,1)}), bf16[8,4,40,2048]{3,2,1,0:T(8,128)(2,1)}, u32[]{:S(2)}, u32[]{:S(2)}) %all-to-all-start.2) | async-done | bytes 5242912 | tf_op jit(solution)/shard_map/all_to_all | solution.py:56
  266.4 8.8 %fusion.23 = (bf16[8,4,40,384]{3,2,0,1:T(8,128)(2,1)S(1)}, bf16[8,4,40,384]{3,2,0,1:T(8,128)(2,1)S(1)}, bf16[8,4,40,384]{3,2,0,1:T(8,128)(2,1)S(1)}) fusion(f32[8,4,40,768]{3,2,0,1:T(8,128)} %fusion.16, bf16[4,384,2048]{2,1,0:T(8,128)(2,1)} %param.12, bf16[8,4,40,2048]{3,2,1,0:T(8,128)(2,1)} %all-to-all-done.2), kind=kOutput, calls=%fused_computation.42 | convolution fusion | flops 2020638720 | bytes 18415616 | tf_op jit(solution)/shard_map/secd,efd->secf/dot_general | solution.py:63
  275.2 8.6 %bitcast_convert_fusion.1 = bf16[4,384,2048]{2,1,0:T(8,128)(2,1)} fusion(bf16[8,4,40,384]{3,2,0,1:T(8,128)(2,1)S(1)} %get-tuple-element.23, bf16[8,4,40,2048]{3,2,1,0:T(8,128)(2,1)} %all-to-all-done.2), kind=kOutput, calls=%fused_computation.17 | convolution fusion | flops 2016411648 | bytes 12517376 | tf_op jit(solution)/shard_map/secf,secd->efd/dot_general | solution.py:76
  284.0 13.3 %bitcast_convert_fusion = bf16[4,2048,768]{2,1,0:T(8,128)(2,1)} fusion(bf16[8,4,40,2048]{3,2,1,0:T(8,128)(2,1)} %all-to-all-done, bf16[8,4,40,384]{3,2,0,1:T(8,128)(2,1)S(1)} %get-tuple-element.22, bf16[8,4,40,384]{3,2,0,1:T(8,128)(2,1)S(1)} %get-tuple-element.21), kind=kOutput, calls=%fused_computation.16 | convolution fusion | flops 4036755456 | bytes 19791872 | tf_op jit(solution)/shard_map/secd,secf->edf/dot_general | solution.py:75
  297.3 5.9 convert_bitcast_fusion.1
  306.0 4.6 all-to-all-start.1
  310.7 14.5 %convert_bitcast_fusion = bf16[8,4,40,2048]{3,2,0,1:T(8,128)(2,1)} fusion(bf16[4,2048,768]{2,1,0:T(8,128)(2,1)} %param.11, bf16[8,4,40,384]{3,2,0,1:T(8,128)(2,1)S(1)} %get-tuple-element.22, bf16[8,4,40,384]{3,2,0,1:T(8,128)(2,1)S(1)} %get-tuple-element.21), kind=kOutput, calls=%fused_computation.29 | convolution fusion | flops 4033085440 | bytes 19791872 | tf_op jit(solution)/shard_map/secf,edf->secd/dot_general | solution.py:67
  325.1 5.6 copy.52
  330.8 95.3 %all-to-all-done.1 = bf16[8,4,40,2048]{3,2,1,0:T(8,128)(2,1)} async-done(((bf16[8,4,40,2048]{3,2,1,0:T(8,128)(2,1)}), bf16[8,4,40,2048]{3,2,1,0:T(8,128)(2,1)}, u32[]{:S(2)}, u32[]{:S(2)}) %all-to-all-start.1) | async-done | bytes 5242912 | tf_op jit(solution)/shard_map/all_to_all | solution.py:52
  426.1 4.8 all-to-all-start.3
  431.0 4.6 gather_fusion.7
  435.6 4.6 gather_fusion.6
  440.3 105.4 %all-to-all-done.3 = bf16[8,4,40,2048]{3,2,1,0:T(8,128)(2,1)} async-done(((bf16[8,4,40,2048]{3,2,1,0:T(8,128)(2,1)}), bf16[8,4,40,2048]{3,2,1,0:T(8,128)(2,1)}, u32[]{:S(2)}, u32[]{:S(2)}) %all-to-all-start.3) | async-done | bytes 5242912 | tf_op jit(solution)/shard_map/all_to_all | solution.py:70
  545.6 5.4 gather_fusion.15
  551.0 5.4 gather_fusion.14
  556.4 4.6 gather_fusion.5
  561.0 5.4 gather_fusion.13
  566.4 4.6 gather_fusion.4
  571.0 5.8 gather_fusion.12
  576.8 4.6 gather_fusion.3
  581.4 5.4 gather_fusion.11
  586.8 5.4 gather_fusion.2
  592.2 5.4 gather_fusion.10
  597.6 5.4 gather_fusion.1
  603.0 5.4 gather_fusion.9
  608.4 5.6 gather_fusion
  614.1 5.4 gather_fusion.8
  (47 shorter events, 22.8 us)
Async XLA Ops:
  7.2 12.6 %copy-start = (bf16[128,2048]{1,0:T(8,128)(2,1)S(1)}, bf16[128,2048]{1,0:T(8,128)(2,1)}, u32[]{:S(2)}) copy-start(bf16[128,2048]{1,0:T(8,128)(2,1)} %param.9) | copy-start | bytes 1572868
  23.7 7.4 %copy-start.3 = (s32[128,8]{0,1:T(8,128)S(1)}, s32[128,8]{0,1:T(8,128)}, u32[]{:S(2)}) copy-start(s32[128,8]{0,1:T(8,128)} %param.14) | copy-start | bytes 12292
  23.7 8.2 %copy-start.2 = (bf16[128,2048]{1,0:T(8,128)(2,1)S(1)}, bf16[128,2048]{1,0:T(8,128)(2,1)}, u32[]{:S(2)}) copy-start(bf16[128,2048]{1,0:T(8,128)(2,1)} %param.10) | copy-start | bytes 1572868
  23.7 123.2 %all-to-all-start = ((bf16[8,4,40,2048]{3,2,1,0:T(8,128)(2,1)}), bf16[8,4,40,2048]{3,2,1,0:T(8,128)(2,1)}, u32[]{:S(2)}, u32[]{:S(2)}) async-start(bf16[8,4,40,2048]{3,2,1,0:T(8,128)(2,1)} %bitcast.110), calls=%async_computation | async-start | bytes 10485760 | tf_op jit(solution)/shard_map/all_to_all | solution.py:42
  146.8 119.6 %all-to-all-start.2 = ((bf16[8,4,40,2048]{3,2,1,0:T(8,128)(2,1)}), bf16[8,4,40,2048]{3,2,1,0:T(8,128)(2,1)}, u32[]{:S(2)}, u32[]{:S(2)}) async-start(bf16[8,4,40,2048]{3,2,1,0:T(8,128)(2,1)} %bitcast.109), calls=%async_computation.2 | async-start | bytes 10485760 | tf_op jit(solution)/shard_map/all_to_all | solution.py:56
  151.5 475.0 %reduce-scatter.5.cloned.1.call-start = ((), (), s32[]{:S(2)}) async-start(), calls=%async_computation.7 | async-start | bytes 7864320 | tf_op jit(solution)/shard_map/reduce_scatter | solution.py:81
  283.8 342.7 %reduce-scatter.3.cloned.1.call-start = ((), (), s32[]{:S(2)}) async-start(), calls=%async_computation.6 | async-start | bytes 15728640 | tf_op jit(solution)/shard_map/reduce_scatter | solution.py:78
  306.0 120.1 %all-to-all-start.1 = ((bf16[8,4,40,2048]{3,2,1,0:T(8,128)(2,1)}), bf16[8,4,40,2048]{3,2,1,0:T(8,128)(2,1)}, u32[]{:S(2)}, u32[]{:S(2)}) async-start(bf16[8,4,40,2048]{3,2,1,0:T(8,128)(2,1)} %copy.49), calls=%async_computation.1 | async-start | bytes 10485760 | tf_op jit(solution)/shard_map/all_to_all | solution.py:52
  426.1 119.5 %all-to-all-start.3 = ((bf16[8,4,40,2048]{3,2,1,0:T(8,128)(2,1)}), bf16[8,4,40,2048]{3,2,1,0:T(8,128)(2,1)}, u32[]{:S(2)}, u32[]{:S(2)}) async-start(bf16[8,4,40,2048]{3,2,1,0:T(8,128)(2,1)} %copy.52), calls=%async_computation.3 | async-start | bytes 10485760 | tf_op jit(solution)/shard_map/all_to_all | solution.py:70
  614.1 12.5 %copy-start.1 = (bf16[128,2048]{1,0:T(8,128)(2,1)S(1)}, bf16[128,2048]{1,0:T(8,128)(2,1)}, u32[]{:S(2)}) copy-start(bf16[128,2048]{1,0:T(8,128)(2,1)} %param.9) | copy-start | bytes 1572868
Sparse Core Ops, SparseCore 0:
  283.9 56.9 reduce-scatter.4
  344.1 99.8 reduce-scatter.2
where the time goes:
time: 640 us; the launch traced here: 634 us
  waiting for transfers between devices  414 us (65%)
  local copies, waits for them, and re-layouts  92.4 us (14%)
  matrix products  71.2 us (11%)
  starting transfers between devices  22.3 us (3%)
  other arithmetic  19.4 us (3%)
  between operations  14.5 us (2%)
    all_to_all x1, waiting for transfers between devices, body(): lax.all_to_all(x_send, 'expert', split_axis=0, concat_axis=0, tiled=True)  111 us
    all_to_all x1, waiting for transfers between devices, body(): lax.all_to_all(d_rows, 'expert', split_axis=0, concat_axis=0, tiled=True)  105 us
    all_to_all x1, waiting for transfers between devices, body(): lax.all_to_all((to_slots(d_mixed) * slot_gate[:, None]).astype(jnp.bfloat...  102 us
    all_to_all x1, waiting for transfers between devices, body(): lax.all_to_all(expert_out, 'expert', split_axis=0, concat_axis=0, tiled=T...  95.3 us
    gather x16, local copies, waits for them, and re-layouts, gather_routes(): picked = jnp.take(rows, position[:, k], axis=0).astype(jnp.float32)  83.1 us
    dot_general x1, matrix products, body(): jnp.einsum('secf,edf->secd', d_pre, w_in, preferred_element_type=jnp.floa...  14.5 us
    dot_general x1, matrix products, body(): jnp.einsum('secd,secf->edf', x_recv, d_pre, preferred_element_type=jnp.fl...  13.3 us
  transfers between devices with their start and end apart: 6, of which 4 were waited for; matrix products, arithmetic and copies ran while one was open for 24% of the time, Pallas kernels for 0%

commit v1 on v0

v1 whole, which is shorter than its diff:
```python
import jax
import jax.numpy as jnp
from jax import lax
from jax.experimental import pallas as pl
from jax.experimental.pallas import tpu as pltpu
from jax.sharding import PartitionSpec as P

F32, BF16 = jnp.float32, jnp.bfloat16
LIMIT = 48 << 20


def ring_pairs(count):
    order = list(range(0, count, 2)) + list(range(count - 1 - count % 2, 0, -2))
    ahead = [(order[i], order[(i + 1) % count]) for i in range(count)]
    return ahead, [(b, a) for a, b in ahead]


def narrow(a):
    return a.astype(BF16)


def wide(a):
    return a.astype(F32)


def ring_gather(block, pairs):
    ahead, back = pairs
    half = block.shape[0] // 2
    f = g = block
    blocks = [block]
    for _ in range(1, len(ahead) // 2):
        f = lax.ppermute(f, "expert", ahead)
        g = lax.ppermute(g, "expert", back)
        blocks += [f, g]
    blocks.append(lax.ppermute(f[:half], "expert", ahead))
    blocks.append(lax.ppermute(g[half:], "expert", back))
    return blocks


def ring_scatter(parts, pairs):
    ahead, back = pairs
    count = len(ahead)
    half = parts[0].shape[0] // 2
    f = lax.ppermute(parts[-1][:half], "expert", ahead)
    g = lax.ppermute(parts[-1][half:], "expert", back)
    for step in range(count // 2 - 1, 0, -1):
        fwd, bwd = parts[2 * step], parts[2 * step - 1]
        if step == count // 2 - 1:
            fwd = jnp.concatenate([narrow(wide(fwd[:half]) + wide(f)), fwd[half:]])
            bwd = jnp.concatenate([bwd[:half], narrow(wide(bwd[half:]) + wide(g))])
        else:
            fwd, bwd = narrow(wide(fwd) + wide(f)), narrow(wide(bwd) + wide(g))
        f = lax.ppermute(fwd, "expert", ahead)
        g = lax.ppermute(bwd, "expert", back)
    return narrow(wide(parts[0]) + wide(f) + wide(g))


def dot(a, b, ca, cb):
    return lax.dot_general(a, b, (((ca,), (cb,)), ((), ())), preferred_element_type=F32)


def cost(flops, size):
    return pl.CostEstimate(flops=flops, bytes_accessed=size, transcendentals=0)


def forward(x, meta, held, w_in, slot, top):
    total, width = x.shape
    both = w_in.shape[2]
    hidden = both // 2
    tile = min(256, total)

    def kernel(held_ref, x_ref, meta_ref, w_ref, act_ref, lr_ref):
        m = wide(meta_ref[...])
        fixed = m[:, top : 2 * top] * 256.0 + m[:, 2 * top : 3 * top]
        gates = fixed / jnp.sum(fixed, axis=1, keepdims=True)
        hit = m[:, :top] == held_ref[slot].astype(F32)
        weight = jnp.sum(jnp.where(hit, gates, 0.0), axis=1, keepdims=True)
        pre = dot(x_ref[...], w_ref[0], 1, 0)
        gate, up = pre[:, :hidden], pre[:, hidden:]
        sig = jax.nn.sigmoid(gate)
        silu = gate * sig
        lean = weight * silu
        act_ref[...] = narrow(lean * up)
        lr_ref[:, :hidden] = narrow(weight * up * sig * (1.0 + gate * (1.0 - sig)))
        lr_ref[:, hidden:] = narrow(lean)

    row = lambda w: pl.BlockSpec((tile, w), lambda i: (i, 0))
    return pl.pallas_call(
        kernel,
        grid=(total // tile,),
        in_specs=[
            pl.BlockSpec(memory_space=pltpu.SMEM),
            row(width),
            row(meta.shape[1]),
            pl.BlockSpec((1, width, both), lambda i: (slot, 0, 0)),
        ],
        out_specs=[row(hidden), row(both)],
        out_shape=[
            jax.ShapeDtypeStruct((total, hidden), BF16),
            jax.ShapeDtypeStruct((total, both), BF16),
        ],
        compiler_params=pltpu.CompilerParams(vmem_limit_bytes=LIMIT),
        cost_estimate=cost(2 * total * width * both, 2 * width * (total + both)),
        name="forward",
    )(held, x, meta, w_in)


def mix(acts, w_out):
    slots, hidden, width = w_out.shape
    total = acts[0].shape[0]
    tile, cols = min(1024, total), min(512, width)

    def kernel(*refs):
        w_ref, out_ref = refs[slots], refs[slots + 1]
        acc = dot(refs[0][...], w_ref[0], 1, 0)
        for s in range(1, slots):
            acc = acc + dot(refs[s][...], w_ref[s], 1, 0)
        out_ref[...] = narrow(acc)

    return pl.pallas_call(
        kernel,
        grid=(total // tile, width // cols),
        in_specs=[pl.BlockSpec((tile, hidden), lambda r, j: (r, 0))] * slots
        + [pl.BlockSpec((slots, hidden, cols), lambda r, j: (0, 0, j))],
        out_specs=pl.BlockSpec((tile, cols), lambda r, j: (r, j)),
        out_shape=jax.ShapeDtypeStruct((total, width), BF16),
        compiler_params=pltpu.CompilerParams(vmem_limit_bytes=LIMIT),
        cost_estimate=cost(2 * total * width * slots * hidden, 2 * width * (total + slots * hidden)),
        name="mix",
    )(*acts, w_out)


def backward(d, lr, w_out, slot):
    total, width = d.shape
    both = lr.shape[1]
    hidden = both // 2
    tile = min(256, total)

    def kernel(d_ref, lr_ref, w_ref, out_ref):
        d_act = dot(d_ref[...], w_ref[0], 1, 1)
        out_ref[:, :hidden] = narrow(d_act * wide(lr_ref[:, :hidden]))
        out_ref[:, hidden:] = narrow(d_act * wide(lr_ref[:, hidden:]))

    row = lambda w: pl.BlockSpec((tile, w), lambda i: (i, 0))
    return pl.pallas_call(
        kernel,
        grid=(total // tile,),
        in_specs=[row(width), row(both), pl.BlockSpec((1, hidden, width), lambda i: (slot, 0, 0))],
        out_specs=row(both),
        out_shape=jax.ShapeDtypeStruct((total, both), BF16),
        compiler_params=pltpu.CompilerParams(vmem_limit_bytes=LIMIT),
        cost_estimate=cost(2 * total * width * hidden, 2 * width * (total + hidden)),
        name="backward",
    )(d, lr, w_out)


def gradients(x, d, act, d_pre, order, parts):
    total, width = x.shape
    hidden, both = act.shape[1], d_pre.shape[1]
    tile, part = min(1024, total), width // parts
    steps, half = total // tile, parts // 2

    def kernel(order_ref, x_ref, d_ref, act_ref, dp_ref, gi_a, go_a, gi_b, go_b, acc_in, acc_out):
        j, r = pl.program_id(0), pl.program_id(1)
        here_in = dot(x_ref[...], dp_ref[...], 0, 0)
        here_out = dot(act_ref[...], d_ref[...], 0, 0)

        def put(gi, go):
            if steps == 1:
                gi[0], go[0] = narrow(here_in), narrow(here_out)
                return

            @pl.when(r == steps - 1)
            def _():
                gi[0] = narrow(acc_in[...] + here_in)
                go[0] = narrow(acc_out[...] + here_out)

        if steps > 1:
            @pl.when(r == 0)
            def _():
                acc_in[...] = jnp.zeros_like(acc_in)
                acc_out[...] = jnp.zeros_like(acc_out)

        pl.when(j < half)(lambda: put(gi_a, go_a))
        pl.when(j >= half)(lambda: put(gi_b, go_b))
        if steps > 1:
            @pl.when(r < steps - 1)
            def _():
                acc_in[...] += here_in
                acc_out[...] += here_out

    first = lambda j, r, o: (jnp.minimum(j, half - 1), 0, 0)
    second = lambda j, r, o: (jnp.maximum(j - half, 0), 0, 0)
    cols = pl.BlockSpec((tile, part), lambda j, r, o: (r, o[j]))
    row = lambda w: pl.BlockSpec((tile, w), lambda j, r, o: (r, 0))
    spec_in = lambda m: pl.BlockSpec((1, part, both), m)
    spec_out = lambda m: pl.BlockSpec((1, hidden, part), m)
    shape_in = jax.ShapeDtypeStruct((half, part, both), BF16)
    shape_out = jax.ShapeDtypeStruct((half, hidden, part), BF16)
    return pl.pallas_call(
        kernel,
        grid_spec=pltpu.PrefetchScalarGridSpec(
            num_scalar_prefetch=1,
            grid=(parts, steps),
            in_specs=[cols, cols, row(hidden), row(both)],
            out_specs=[spec_in(first), spec_out(first), spec_in(second), spec_out(second)],
            scratch_shapes=[
                pltpu.VMEM((part, both) if steps > 1 else (8, 128), F32),
                pltpu.VMEM((hidden, part) if steps > 1 else (8, 128), F32),
            ],
        ),
        out_shape=[shape_in, shape_out, shape_in, shape_out],
        compiler_params=pltpu.CompilerParams(vmem_limit_bytes=LIMIT),
        cost_estimate=cost(2 * total * width * (both + hidden), 2 * width * (2 * total + both + hidden)),
        name="gradients",
    )(order, x, d, act, d_pre)


def rows_back(d_pres, w_in, start, count):
    slots, width, both = w_in.shape
    tile, cols = min(512, count), min(512, width)

    def kernel(*refs):
        w_ref, out_ref = refs[slots], refs[slots + 1]
        acc = dot(refs[0][...], w_ref[0], 1, 1)
        for s in range(1, slots):
            acc = acc + dot(refs[s][...], w_ref[s], 1, 1)
        out_ref[...] = narrow(acc)

    return pl.pallas_call(
        kernel,
        grid=(count // tile, width // cols),
        in_specs=[pl.BlockSpec((tile, both), lambda r, j: (start // tile + r, 0))] * slots
        + [pl.BlockSpec((slots, cols, both), lambda r, j: (0, j, 0))],
        out_specs=pl.BlockSpec((tile, cols), lambda r, j: (r, j)),
        out_shape=jax.ShapeDtypeStruct((count, width), BF16),
        compiler_params=pltpu.CompilerParams(vmem_limit_bytes=LIMIT),
        cost_estimate=cost(2 * count * width * slots * both, 2 * width * (count + slots * both)),
        name="rows_back",
    )(*d_pres, w_in)


def body(tokens, d_mixed, w_in, w_out, expert_ids, gate_fixed, placement):
    rows, width = tokens.shape
    slots = w_out.shape[0]
    ring, parts = lax.axis_size("expert"), lax.axis_size("dp")
    me_e, me_p = lax.axis_index("expert"), lax.axis_index("dp")
    pairs = ring_pairs(ring)
    top = expert_ids.shape[1]
    total = rows * ring

    meta = jnp.concatenate([expert_ids, gate_fixed // 256, gate_fixed % 256], axis=1)
    meta = jnp.pad(meta, ((0, 0), (0, 128 - 3 * top))).astype(BF16)
    x_blocks = ring_gather(jnp.concatenate([tokens, meta], axis=1), pairs)
    d_start, _ = lax.optimization_barrier((d_mixed, x_blocks[-3]))
    d_blocks = ring_gather(d_start, pairs)
    x = jnp.concatenate([b[:, :width] for b in x_blocks], axis=0)
    meta = jnp.concatenate([b[:, width:] for b in x_blocks], axis=0)
    d = jnp.concatenate(d_blocks, axis=0)

    local = me_e * slots + jnp.arange(slots, dtype=jnp.int32)
    names = jnp.arange(placement.shape[0], dtype=jnp.int32)
    held = jnp.sum(jnp.where(placement[None, :] == local[:, None], names[None, :], 0), axis=1)

    acts, lrs = zip(*[forward(x, meta, held, w_in, s, top) for s in range(slots)])
    mixed_part = mix(acts, w_out)

    core_pairs = [(i, i ^ 1) for i in range(parts)]
    chip_pairs = [(i, (i + parts // 2) % parts) for i in range(parts)]
    core, far, near = me_p % 2, (me_p // 2 + 1) % 2, me_p // 2
    order = jnp.stack([2 * far + 1 - core, 2 * near + 1 - core, 2 * far + core, 2 * near + core])

    d_pres, grads = [], []
    for s in range(slots):
        d_pre = backward(d, lrs[s], w_out, s)
        d_pres.append(d_pre)
        give_in, give_out, keep_in, keep_out = gradients(x, d, acts[s], d_pre, order, parts)
        pair = []
        for give, keep in ((give_in, keep_in), (give_out, keep_out)):
            got = lax.ppermute(give, "dp", core_pairs)
            away = lax.ppermute(narrow(wide(keep[0]) + wide(got[0])), "dp", chip_pairs)
            pair.append(narrow(wide(keep[1]) + wide(got[1]) + wide(away)))
        grads.append(pair)
    late = rows_back(d_pres, w_in, total // 2, total // 2)
    early = rows_back(d_pres, w_in, 0, total // 2)
    cut = lambda a: [a[i * rows : (i + 1) * rows] for i in range(a.shape[0] // rows)]
    mixed = ring_scatter(cut(mixed_part), pairs)
    d_tokens = ring_scatter(cut(early) + cut(late), pairs)
    return mixed, d_tokens, jnp.stack([g[0] for g in grads]), jnp.stack([g[1] for g in grads])


def solution(mesh):
    rows, slots = P(("dp", "expert"), None), P("expert", None, None)
    return jax.shard_map(
        body,
        mesh=mesh,
        in_specs=(rows, rows, slots, slots, rows, rows, P()),
        out_specs=(rows, rows, P("expert", "dp", None), P("expert", None, "dp")),
        check_vma=False,
    )
```

time: 640 us -> 392 us (0.61)
  waiting for transfers between devices: 414 us -> 188 us
  Pallas kernels: 0 us -> 120 us
  local copies, waits for them, and re-layouts: 92.4 us -> 11.5 us
  matrix products: 71.2 us -> 0 us
  starting transfers between devices: 22.3 us -> 47.5 us
  between operations: 14.5 us -> 1.35 us
    all_to_all x4 -> x0, waiting for transfers between devices: 414 us -> none  [the longest x1 111 us: body(): lax.all_to_all(x_send, 'expert', split_axis=0, concat_axis=0, tiled=True)]
    ppermute x0 -> x48, waiting for transfers between devices: none -> 188 us  [the longest x8 69.8 us: body(): away = lax.ppermute(narrow(wide(keep[0]) + wide(got[0])), 'dp', chip_pairs)]
    pallas_call x0 -> x15, Pallas kernels: none -> 120 us  [the longest x4 36.8 us: gradients(): pl.pallas_call(kernel, grid_spec=pltpu.PrefetchScalarGridSpec(num_scalar_...]
    gather x16 -> x0, local copies, waits for them, and re-layouts: 83.1 us -> none  [gather_routes(): picked = jnp.take(rows, position[:, k], axis=0).astype(jnp.float32)]
    dot_general x8 -> x0, matrix products: 71.2 us -> none  [the longest x1 14.5 us: body(): jnp.einsum('secf,edf->secd', d_pre, w_in, preferred_element_type=jnp.floa...]
    ppermute x0 -> x48, starting transfers between devices: none -> 47.5 us  [the longest x8 10.4 us: body(): away = lax.ppermute(narrow(wide(keep[0]) + wide(got[0])), 'dp', chip_pairs)]
    all_to_all x4 -> x0, starting transfers between devices: 21.5 us -> none  [the longest x1 7.41 us: body(): lax.all_to_all(x_send, 'expert', split_axis=0, concat_axis=0, tiled=True)]
    unnamed x8 -> x64, local copies, waits for them, and re-layouts: 0.02 us -> 8.82 us
  transfers between devices with their start and end apart: 6 -> 48, of which waited for: 4 -> 23; matrix products, arithmetic and copies ran while one was open for 24% -> 6% of each run, Pallas kernels for 0% -> 31%
where the time goes in v1:
time: 392 us; the launch traced here: 391 us
  waiting for transfers between devices  188 us (48%)
  Pallas kernels  120 us (31%)
  starting transfers between devices  47.5 us (12%)
  other arithmetic  22.2 us (6%)
  local copies, waits for them, and re-layouts  11.5 us (3%)
    ppermute x8, waiting for transfers between devices, body(): away = lax.ppermute(narrow(wide(keep[0]) + wide(got[0])), 'dp', chip_pairs)  69.8 us
    ppermute x6, waiting for transfers between devices, ring_gather(): g = lax.ppermute(g, 'expert', back)  50 us
    pallas_call x4, Pallas kernels, gradients(): pl.pallas_call(kernel, grid_spec=pltpu.PrefetchScalarGridSpec(num_scalar_...  36.8 us
    ppermute x6, waiting for transfers between devices, ring_scatter(): f = lax.ppermute(fwd, 'expert', ahead)  31.3 us
    pallas_call x4, Pallas kernels, forward(): pl.pallas_call(kernel, grid=(total // tile,), in_specs=[pl.BlockSpec(memo...  27.1 us
    pallas_call x4, Pallas kernels, backward(): pl.pallas_call(kernel, grid=(total // tile,), in_specs=[row(width), row(b...  22.7 us
    pallas_call x2, Pallas kernels, rows_back(): pl.pallas_call(kernel, grid=(count // tile, width // cols), in_specs=[pl....  21.7 us
    ppermute x2, waiting for transfers between devices, ring_gather(): blocks.append(lax.ppermute(f[:half], 'expert', ahead))  15.8 us
  transfers between devices with their start and end apart: 48, of which 23 were waited for; matrix products, arithmetic and copies ran while one was open for 6% of the time, Pallas kernels for 31%

profile of v1, /device:TPU:0, one launch (start us, length us, event | category | flops | bytes accessed | tf_op | source)
XLA Modules:
  0.0 391.2 jit_solution(2485481879785055650)
XLA Ops:
  8.4 10.6 %collective-permute-done.1 = bf16[128,2176]{1,0:T(8,128)(2,1)S(1)} collective-permute-done((bf16[128,2176]{1,0:T(8,128)(2,1)S(1)}, bf16[128,2176]{1,0:T(8,128)(2,1)S(1)}, u32[]{:S(2)}, u32[]{:S(2)}) %collective-permute-start.1) | collective-permute-done | bytes 557088 | tf_op jit(solution)/shard_map/ppermute | solution.py:33
  21.2 11.6 %collective-permute-done.3 = bf16[128,2176]{1,0:T(8,128)(2,1)S(1)} collective-permute-done((bf16[128,2176]{1,0:T(8,128)(2,1)S(1)}, bf16[128,2176]{1,0:T(8,128)(2,1)S(1)}, u32[]{:S(2)}, u32[]{:S(2)}) %collective-permute-start.3) | collective-permute-done | bytes 557088 | tf_op jit(solution)/shard_map/ppermute | solution.py:33
  35.0 10.8 %collective-permute-done.5 = bf16[128,2176]{1,0:T(8,128)(2,1)S(1)} collective-permute-done((bf16[128,2176]{1,0:T(8,128)(2,1)S(1)}, bf16[128,2176]{1,0:T(8,128)(2,1)S(1)}, u32[]{:S(2)}, u32[]{:S(2)}) %collective-permute-start.5) | collective-permute-done | bytes 557088 | tf_op jit(solution)/shard_map/ppermute | solution.py:33
  50.1 13.7 %collective-permute-done.6 = bf16[64,2176]{1,0:T(8,128)(2,1)S(1)} collective-permute-done((bf16[64,2176]{1,0:T(8,128)(2,1)S(1)}, bf16[64,2176]{1,0:T(8,128)(2,1)S(1)}, u32[]{:S(2)}, u32[]{:S(2)}) %collective-permute-start.6) | collective-permute-done | bytes 278560 | tf_op jit(solution)/shard_map/ppermute | solution.py:35
  65.8 6.7 %forward.7 = (bf16[1024,384]{1,0:T(8,128)(2,1)S(1)}, bf16[1024,768]{1,0:T(8,128)(2,1)S(1)}) custom-call(s32[4]{0:T(128)S(1)} %select_reduce_fusion.held_ref, bf16[1024,2048]{1,0:T(8,128)(2,1)} %copy-done.13, bf16[1024,128]{1,0:T(8,128)(2,1)S(1)} %constant_dynamic-update-slice_fusion.1.meta_ref, bf16[4,2048,768]{2,1,0:T(8,128)(2,1)} %refs_4_.5), custom_call_target="tpu_custom_call" | custom-call | flops 3221225472 | bytes 7340032 | tf_op jit(solution)/shard_map/forward/pallas_call | solution.py:88
  72.5 6.7 %forward.6 = (bf16[1024,384]{1,0:T(8,128)(2,1)S(1)}, bf16[1024,768]{1,0:T(8,128)(2,1)S(1)}) custom-call(s32[4]{0:T(128)S(1)} %select_reduce_fusion.held_ref, bf16[1024,2048]{1,0:T(8,128)(2,1)} %copy-done.13, bf16[1024,128]{1,0:T(8,128)(2,1)S(1)} %constant_dynamic-update-slice_fusion.1.meta_ref, bf16[4,2048,768]{2,1,0:T(8,128)(2,1)} %refs_4_.5), custom_call_target="tpu_custom_call" | custom-call | flops 3221225472 | bytes 7340032 | tf_op jit(solution)/shard_map/forward/pallas_call | solution.py:88
  79.3 6.7 %forward.5 = (bf16[1024,384]{1,0:T(8,128)(2,1)S(1)}, bf16[1024,768]{1,0:T(8,128)(2,1)S(1)}) custom-call(s32[4]{0:T(128)S(1)} %select_reduce_fusion.held_ref, bf16[1024,2048]{1,0:T(8,128)(2,1)} %copy-done.13, bf16[1024,128]{1,0:T(8,128)(2,1)S(1)} %constant_dynamic-update-slice_fusion.1.meta_ref, bf16[4,2048,768]{2,1,0:T(8,128)(2,1)} %refs_4_.5), custom_call_target="tpu_custom_call" | custom-call | flops 3221225472 | bytes 7340032 | tf_op jit(solution)/shard_map/forward/pallas_call | solution.py:88
  86.0 7.0 %forward.4 = (bf16[1024,384]{1,0:T(8,128)(2,1)S(1)}, bf16[1024,768]{1,0:T(8,128)(2,1)S(1)}) custom-call(s32[4]{0:T(128)S(1)} %select_reduce_fusion.held_ref, bf16[1024,2048]{1,0:T(8,128)(2,1)} %copy-done.13, bf16[1024,128]{1,0:T(8,128)(2,1)S(1)} %constant_dynamic-update-slice_fusion.1.meta_ref, bf16[4,2048,768]{2,1,0:T(8,128)(2,1)} %refs_4_.5), custom_call_target="tpu_custom_call" | custom-call | flops 3221225472 | bytes 7340032 | tf_op jit(solution)/shard_map/forward/pallas_call | solution.py:88
  93.0 12.1 %mix.1 = bf16[1024,2048]{1,0:T(8,128)(2,1)} custom-call(bf16[1024,384]{1,0:T(8,128)(2,1)S(1)} %get-tuple-element.29.refs_0_.act_ref, bf16[1024,384]{1,0:T(8,128)(2,1)S(1)} %get-tuple-element.30.refs_1_.act_ref, bf16[1024,384]{1,0:T(8,128)(2,1)S(1)} %get-tuple-element.31.refs_2_.act_ref, bf16[1024,384]{1,0:T(8,128)(2,1)S(1)} %get-tuple-element.32.refs_3_.act_ref, ...), custom_call_target="tpu_custom_call" | custom-call | flops 6442450944 | bytes 10485760 | tf_op jit(solution)/shard_map/mix/pallas_call | solution.py:120
  119.2 8.8 %collective-permute-done.19 = bf16[128,2048]{1,0:T(8,128)(2,1)S(1)} collective-permute-done((bf16[128,2048]{1,0:T(8,128)(2,1)S(1)}, bf16[128,2048]{1,0:T(8,128)(2,1)S(1)}, u32[]{:S(2)}, u32[]{:S(2)}) %collective-permute-start.19) | collective-permute-done | bytes 524320 | tf_op jit(solution)/shard_map/ppermute | solution.py:33
  130.1 8.1 %collective-permute-done.9 = bf16[128,2048]{1,0:T(8,128)(2,1)S(1)} collective-permute-done((bf16[128,2048]{1,0:T(8,128)(2,1)S(1)}, bf16[128,2048]{1,0:T(8,128)(2,1)S(1)}, u32[]{:S(2)}, u32[]{:S(2)}) %collective-permute-start.9) | collective-permute-done | bytes 524320 | tf_op jit(solution)/shard_map/ppermute | solution.py:53
  139.5 8.2 %collective-permute-done.21 = bf16[128,2048]{1,0:T(8,128)(2,1)S(1)} collective-permute-done((bf16[128,2048]{1,0:T(8,128)(2,1)S(1)}, bf16[128,2048]{1,0:T(8,128)(2,1)S(1)}, u32[]{:S(2)}, u32[]{:S(2)}) %collective-permute-start.21) | collective-permute-done | bytes 524320 | tf_op jit(solution)/shard_map/ppermute | solution.py:33
  150.7 10.0 %collective-permute-done.10 = bf16[128,2048]{1,0:T(8,128)(2,1)S(1)} collective-permute-done((bf16[128,2048]{1,0:T(8,128)(2,1)S(1)}, bf16[128,2048]{1,0:T(8,128)(2,1)S(1)}, u32[]{:S(2)}, u32[]{:S(2)}) %collective-permute-start.10) | collective-permute-done | bytes 524320 | tf_op jit(solution)/shard_map/ppermute | solution.py:53
  173.7 5.8 %backward.6.refs_2_.dp_ref = bf16[1024,768]{1,0:T(8,128)(2,1)S(1)} custom-call(bf16[1024,2048]{1,0:T(8,128)(2,1)} %copy-done.14, bf16[1024,768]{1,0:T(8,128)(2,1)S(1)} %get-tuple-element.36.lr_ref, bf16[4,384,2048]{2,1,0:T(8,128)(2,1)} %w_ref.15), custom_call_target="tpu_custom_call" | custom-call | flops 1610612736 | bytes 5767168 | tf_op jit(solution)/shard_map/backward/pallas_call | solution.py:145
  179.5 5.8 %backward.5.refs_1_.dp_ref = bf16[1024,768]{1,0:T(8,128)(2,1)S(1)} custom-call(bf16[1024,2048]{1,0:T(8,128)(2,1)} %copy-done.14, bf16[1024,768]{1,0:T(8,128)(2,1)S(1)} %get-tuple-element.35.lr_ref, bf16[4,384,2048]{2,1,0:T(8,128)(2,1)} %w_ref.15), custom_call_target="tpu_custom_call" | custom-call | flops 1610612736 | bytes 5767168 | tf_op jit(solution)/shard_map/backward/pallas_call | solution.py:145
  185.4 5.8 %backward.4.refs_0_.dp_ref = bf16[1024,768]{1,0:T(8,128)(2,1)S(1)} custom-call(bf16[1024,2048]{1,0:T(8,128)(2,1)} %copy-done.14, bf16[1024,768]{1,0:T(8,128)(2,1)S(1)} %get-tuple-element.34.lr_ref, bf16[4,384,2048]{2,1,0:T(8,128)(2,1)} %w_ref.15), custom_call_target="tpu_custom_call" | custom-call | flops 1610612736 | bytes 5767168 | tf_op jit(solution)/shard_map/backward/pallas_call | solution.py:145
  191.2 11.1 %rows_back.3 = bf16[512,2048]{1,0:T(8,128)(2,1)} custom-call(bf16[1024,768]{1,0:T(8,128)(2,1)S(1)} %backward.4.refs_0_.dp_ref, bf16[1024,768]{1,0:T(8,128)(2,1)S(1)} %backward.5.refs_1_.dp_ref, bf16[1024,768]{1,0:T(8,128)(2,1)S(1)} %backward.6.refs_2_.dp_ref, bf16[1024,768]{1,0:T(8,128)(2,1)} %copy-done.3, bf16[4,2048,768]{2,1,0:T(8,128)(2,1)} %refs_4_.5), custom_call_target="tpu_custom_call" | custom-call | flops 6442450944 | bytes 14680064 | tf_op jit(solution)/shard_map/rows_back/pallas_call | solution.py:230
  202.3 10.6 %rows_back.2 = bf16[512,2048]{1,0:T(8,128)(2,1)} custom-call(bf16[1024,768]{1,0:T(8,128)(2,1)S(1)} %backward.4.refs_0_.dp_ref, bf16[1024,768]{1,0:T(8,128)(2,1)S(1)} %backward.5.refs_1_.dp_ref, bf16[1024,768]{1,0:T(8,128)(2,1)S(1)} %backward.6.refs_2_.dp_ref, bf16[1024,768]{1,0:T(8,128)(2,1)} %copy-done.3, bf16[4,2048,768]{2,1,0:T(8,128)(2,1)} %refs_4_.5), custom_call_target="tpu_custom_call" | custom-call | flops 6442450944 | bytes 14680064 | tf_op jit(solution)/shard_map/rows_back/pallas_call | solution.py:230
  213.0 9.8 %gradients.7 = (bf16[2,512,768]{2,1,0:T(8,128)(2,1)S(1)}, bf16[2,384,512]{2,1,0:T(8,128)(2,1)}, bf16[2,512,768]{2,1,0:T(8,128)(2,1)S(1)}, bf16[2,384,512]{2,1,0:T(8,128)(2,1)S(1)}) custom-call(s32[4]{0:T(128)S(1)} %pad_add_fusion.order_ref, bf16[1024,2048]{1,0:T(8,128)(2,1)} %copy-done.13, bf16[1024,2048]{1,0:T(8,128)(2,1)} %copy-done.14, ...), custom_call_target="tpu_custom_call" | custom-call | flops 4831838208 | bytes 13107200 | tf_op jit(solution)/shard_map/gradients/pallas_call | solution.py:200
  223.9 9.0 %gradients.6 = (bf16[2,512,768]{2,1,0:T(8,128)(2,1)S(1)}, bf16[2,384,512]{2,1,0:T(8,128)(2,1)S(1)}, bf16[2,512,768]{2,1,0:T(8,128)(2,1)S(1)}, bf16[2,384,512]{2,1,0:T(8,128)(2,1)S(1)}) custom-call(s32[4]{0:T(128)S(1)} %pad_add_fusion.order_ref, bf16[1024,2048]{1,0:T(8,128)(2,1)} %copy-done.13, bf16[1024,2048]{1,0:T(8,128)(2,1)} %copy-done.14, ...), custom_call_target="tpu_custom_call" | custom-call | flops 4831838208 | bytes 13107200 | tf_op jit(solution)/shard_map/gradients/pallas_call | solution.py:200
  233.8 9.0 %gradients.5 = (bf16[2,512,768]{2,1,0:T(8,128)(2,1)S(1)}, bf16[2,384,512]{2,1,0:T(8,128)(2,1)S(1)}, bf16[2,512,768]{2,1,0:T(8,128)(2,1)S(1)}, bf16[2,384,512]{2,1,0:T(8,128)(2,1)S(1)}) custom-call(s32[4]{0:T(128)S(1)} %pad_add_fusion.order_ref, bf16[1024,2048]{1,0:T(8,128)(2,1)} %copy-done.13, bf16[1024,2048]{1,0:T(8,128)(2,1)} %copy-done.14, ...), custom_call_target="tpu_custom_call" | custom-call | flops 4831838208 | bytes 13107200 | tf_op jit(solution)/shard_map/gradients/pallas_call | solution.py:200
  246.8 9.0 %gradients.4 = (bf16[2,512,768]{2,1,0:T(8,128)(2,1)S(1)}, bf16[2,384,512]{2,1,0:T(8,128)(2,1)S(1)}, bf16[2,512,768]{2,1,0:T(8,128)(2,1)S(1)}, bf16[2,384,512]{2,1,0:T(8,128)(2,1)S(1)}) custom-call(s32[4]{0:T(128)S(1)} %pad_add_fusion.order_ref, bf16[1024,2048]{1,0:T(8,128)(2,1)} %copy-done.13, bf16[1024,2048]{1,0:T(8,128)(2,1)} %copy-done.14, ...), custom_call_target="tpu_custom_call" | custom-call | flops 4831838208 | bytes 13107200 | tf_op jit(solution)/shard_map/gradients/pallas_call | solution.py:200
  264.9 11.4 %collective-permute-done.25 = bf16[128,2048]{1,0:T(8,128)(2,1)S(1)} collective-permute-done((bf16[128,2048]{1,0:T(8,128)(2,1)S(1)}, bf16[128,2048]{1,0:T(8,128)(2,1)S(1)}, u32[]{:S(2)}, u32[]{:S(2)}) %collective-permute-start.25) | collective-permute-done | bytes 524320 | tf_op jit(solution)/shard_map/ppermute | solution.py:53
  283.4 7.7 %collective-permute-done.47 = bf16[384,512]{1,0:T(8,128)(2,1)S(1)} collective-permute-done((bf16[384,512]{1,0:T(8,128)(2,1)S(1)}, bf16[384,512]{1,0:T(8,128)(2,1)S(1)}, u32[]{:S(2)}, u32[]{:S(2)}) %collective-permute-start.47) | collective-permute-done | bytes 393248 | tf_op jit(solution)/shard_map/ppermute | solution.py:281
  293.8 5.8 %collective-permute-done.45 = bf16[384,512]{1,0:T(8,128)(2,1)S(1)} collective-permute-done((bf16[384,512]{1,0:T(8,128)(2,1)S(1)}, bf16[384,512]{1,0:T(8,128)(2,1)S(1)}, u32[]{:S(2)}, u32[]{:S(2)}) %collective-permute-start.45) | collective-permute-done | bytes 393248 | tf_op jit(solution)/shard_map/ppermute | solution.py:281
  301.3 6.8 %collective-permute-done.43 = bf16[384,512]{1,0:T(8,128)(2,1)S(1)} collective-permute-done((bf16[384,512]{1,0:T(8,128)(2,1)S(1)}, bf16[384,512]{1,0:T(8,128)(2,1)S(1)}, u32[]{:S(2)}, u32[]{:S(2)}) %collective-permute-start.43) | collective-permute-done | bytes 393248 | tf_op jit(solution)/shard_map/ppermute | solution.py:281
  308.6 6.1 %collective-permute-done.41 = bf16[384,512]{1,0:T(8,128)(2,1)S(1)} collective-permute-done((bf16[384,512]{1,0:T(8,128)(2,1)S(1)}, bf16[384,512]{1,0:T(8,128)(2,1)S(1)}, u32[]{:S(2)}, u32[]{:S(2)}) %collective-permute-start.41) | collective-permute-done | bytes 393248 | tf_op jit(solution)/shard_map/ppermute | solution.py:281
  323.1 8.1 %collective-permute-done.30 = bf16[128,2048]{1,0:T(8,128)(2,1)S(1)} collective-permute-done((bf16[128,2048]{1,0:T(8,128)(2,1)S(1)}, bf16[128,2048]{1,0:T(8,128)(2,1)S(1)}, u32[]{:S(2)}, u32[]{:S(2)}) %collective-permute-start.30) | collective-permute-done | bytes 524320 | tf_op jit(solution)/shard_map/ppermute | solution.py:54
  337.1 6.4 %collective-permute-done.31 = bf16[128,2048]{1,0:T(8,128)(2,1)S(1)} collective-permute-done((bf16[128,2048]{1,0:T(8,128)(2,1)S(1)}, bf16[128,2048]{1,0:T(8,128)(2,1)S(1)}, u32[]{:S(2)}, u32[]{:S(2)}) %collective-permute-start.31) | collective-permute-done | bytes 524320 | tf_op jit(solution)/shard_map/ppermute | solution.py:54
  344.9 13.7 %collective-permute-done.37 = bf16[512,768]{1,0:T(8,128)(2,1)S(1)} collective-permute-done((bf16[512,768]{1,0:T(8,128)(2,1)S(1)}, bf16[512,768]{1,0:T(8,128)(2,1)S(1)}, u32[]{:S(2)}, u32[]{:S(2)}) %collective-permute-start.37) | collective-permute-done | bytes 786464 | tf_op jit(solution)/shard_map/ppermute | solution.py:281
  358.9 16.5 %collective-permute-done.35 = bf16[512,768]{1,0:T(8,128)(2,1)S(1)} collective-permute-done((bf16[512,768]{1,0:T(8,128)(2,1)S(1)}, bf16[512,768]{1,0:T(8,128)(2,1)S(1)}, u32[]{:S(2)}, u32[]{:S(2)}) %collective-permute-start.35) | collective-permute-done | bytes 786464 | tf_op jit(solution)/shard_map/ppermute | solution.py:281
  375.8 13.2 %collective-permute-done.33 = bf16[512,768]{1,0:T(8,128)(2,1)S(1)} collective-permute-done((bf16[512,768]{1,0:T(8,128)(2,1)S(1)}, bf16[512,768]{1,0:T(8,128)(2,1)S(1)}, u32[]{:S(2)}, u32[]{:S(2)}) %collective-permute-start.33) | collective-permute-done | bytes 786464 | tf_op jit(solution)/shard_map/ppermute | solution.py:281
  (192 shorter events, 97.2 us)
Async XLA Ops:
  3.3 15.7 %collective-permute-start.1 = (bf16[128,2176]{1,0:T(8,128)(2,1)S(1)}, bf16[128,2176]{1,0:T(8,128)(2,1)S(1)}, u32[]{:S(2)}, u32[]{:S(2)}) collective-permute-start(bf16[128,2176]{1,0:T(8,128)(2,1)S(1)} %pad_maximum_fusion.2), channel_id=1, source_target_pairs={{2,0},{4,2},{6,4},{7,6},{5,7},{3,5},{1,3},{0,1},{10,8},{12,10},{14... | collective-permute-start | bytes 1671176 | tf_op jit(solution)/shard_map/ppermute | solution.py:33
  6.3 14.4 %collective-permute-start = (bf16[128,2176]{1,0:T(8,128)(2,1)S(1)}, bf16[128,2176]{1,0:T(8,128)(2,1)S(1)}, u32[]{:S(2)}, u32[]{:S(2)}) collective-permute-start(bf16[128,2176]{1,0:T(8,128)(2,1)S(1)} %pad_maximum_fusion.2), channel_id=1, source_target_pairs={{0,2},{2,4},{4,6},{6,7},{7,5},{5,3},{3,1},{1,0},{8,10},{10,12},{12... | collective-permute-start | bytes 1671176 | tf_op jit(solution)/shard_map/ppermute | solution.py:32
  34.2 14.9 %collective-permute-start.4 = (bf16[128,2176]{1,0:T(8,128)(2,1)S(1)}, bf16[128,2176]{1,0:T(8,128)(2,1)S(1)}, u32[]{:S(2)}, u32[]{:S(2)}) collective-permute-start(bf16[128,2176]{1,0:T(8,128)(2,1)S(1)} %collective-permute-done.2), channel_id=1, source_target_pairs={{0,2},{2,4},{4,6},{6,7},{7,5},{5,3},{3,1},{1,0},{8,10},{10,12},{12... | collective-permute-start | bytes 1671176 | tf_op jit(solution)/shard_map/ppermute | solution.py:32
  45.7 62.9 %collective-permute-start.17 = (bf16[128,2048]{1,0:T(8,128)(2,1)S(1)}, bf16[128,2048]{1,0:T(8,128)(2,1)S(1)}, u32[]{:S(2)}, u32[]{:S(2)}) collective-permute-start(bf16[128,2048]{1,0:T(8,128)(2,1)S(1)} %copy-done.19), channel_id=1, source_target_pairs={{2,0},{4,2},{6,4},{7,6},{5,7},{3,5},{1,3},{0,1},{10,8},{12,10},{14... | collective-permute-start | bytes 1572872 | tf_op jit(solution)/shard_map/ppermute | solution.py:33
  47.0 63.3 %collective-permute-start.16 = (bf16[128,2048]{1,0:T(8,128)(2,1)S(1)}, bf16[128,2048]{1,0:T(8,128)(2,1)S(1)}, u32[]{:S(2)}, u32[]{:S(2)}) collective-permute-start(bf16[128,2048]{1,0:T(8,128)(2,1)S(1)} %copy-done.19), channel_id=1, source_target_pairs={{0,2},{2,4},{4,6},{6,7},{7,5},{5,3},{3,1},{1,0},{8,10},{10,12},{12... | collective-permute-start | bytes 1572872 | tf_op jit(solution)/shard_map/ppermute | solution.py:32
  47.8 16.0 %collective-permute-start.7 = (bf16[64,2176]{1,0:T(8,128)(2,1)S(1)}, bf16[64,2176]{1,0:T(8,128)(2,1)S(1)}, u32[]{:S(2)}, u32[]{:S(2)}) collective-permute-start(bf16[64,2176]{1,0:T(8,128)(2,1)S(1)} %slice.322), channel_id=1, source_target_pairs={{2,0},{4,2},{6,4},{7,6},{5,7},{3,5},{1,3},{0,1},{10,8},{12,10},{14... | collective-permute-start | bytes 835592 | tf_op jit(solution)/shard_map/ppermute | solution.py:36
  49.1 14.7 %collective-permute-start.6 = (bf16[64,2176]{1,0:T(8,128)(2,1)S(1)}, bf16[64,2176]{1,0:T(8,128)(2,1)S(1)}, u32[]{:S(2)}, u32[]{:S(2)}) collective-permute-start(bf16[64,2176]{1,0:T(8,128)(2,1)S(1)} %slice.320), channel_id=1, source_target_pairs={{0,2},{2,4},{4,6},{6,7},{7,5},{5,3},{3,1},{1,0},{8,10},{10,12},{12... | collective-permute-start | bytes 835592 | tf_op jit(solution)/shard_map/ppermute | solution.py:35
  108.6 19.4 %collective-permute-start.19 = (bf16[128,2048]{1,0:T(8,128)(2,1)S(1)}, bf16[128,2048]{1,0:T(8,128)(2,1)S(1)}, u32[]{:S(2)}, u32[]{:S(2)}) collective-permute-start(bf16[128,2048]{1,0:T(8,128)(2,1)S(1)} %collective-permute-done.17), channel_id=1, source_target_pairs={{2,0},{4,2},{6,4},{7,6},{5,7},{3,5},{1,3},{0,1},{10,8},{12,10},{14... | collective-permute-start | bytes 1572872 | tf_op jit(solution)/shard_map/ppermute | solution.py:33
  110.2 18.7 %collective-permute-start.18 = (bf16[128,2048]{1,0:T(8,128)(2,1)S(1)}, bf16[128,2048]{1,0:T(8,128)(2,1)S(1)}, u32[]{:S(2)}, u32[]{:S(2)}) collective-permute-start(bf16[128,2048]{1,0:T(8,128)(2,1)S(1)} %collective-permute-done.16), channel_id=1, source_target_pairs={{0,2},{2,4},{4,6},{6,7},{7,5},{5,3},{3,1},{1,0},{8,10},{10,12},{12... | collective-permute-start | bytes 1572872 | tf_op jit(solution)/shard_map/ppermute | solution.py:32
  117.0 21.2 %collective-permute-start.9 = (bf16[128,2048]{1,0:T(8,128)(2,1)S(1)}, bf16[128,2048]{1,0:T(8,128)(2,1)S(1)}, u32[]{:S(2)}, u32[]{:S(2)}) collective-permute-start(bf16[128,2048]{1,0:T(8,128)(2,1)S(1)} %pad_maximum_fusion.3), channel_id=1, source_target_pairs={{0,2},{2,4},{4,6},{6,7},{7,5},{5,3},{3,1},{1,0},{8,10},{10,12},{12... | collective-permute-start | bytes 1572872 | tf_op jit(solution)/shard_map/ppermute | solution.py:53
  118.1 32.5 %collective-permute-start.13 = (bf16[128,2048]{1,0:T(8,128)(2,1)S(1)}, bf16[128,2048]{1,0:T(8,128)(2,1)S(1)}, u32[]{:S(2)}, u32[]{:S(2)}) collective-permute-start(bf16[128,2048]{1,0:T(8,128)(2,1)S(1)} %pad_maximum_fusion.4), channel_id=1, source_target_pairs={{2,0},{4,2},{6,4},{7,6},{5,7},{3,5},{1,3},{0,1},{10,8},{12,10},{14... | collective-permute-start | bytes 1572872 | tf_op jit(solution)/shard_map/ppermute | solution.py:54
  128.0 19.7 %collective-permute-start.21 = (bf16[128,2048]{1,0:T(8,128)(2,1)S(1)}, bf16[128,2048]{1,0:T(8,128)(2,1)S(1)}, u32[]{:S(2)}, u32[]{:S(2)}) collective-permute-start(bf16[128,2048]{1,0:T(8,128)(2,1)S(1)} %collective-permute-done.19), channel_id=1, source_target_pairs={{2,0},{4,2},{6,4},{7,6},{5,7},{3,5},{1,3},{0,1},{10,8},{12,10},{14... | collective-permute-start | bytes 1572872 | tf_op jit(solution)/shard_map/ppermute | solution.py:33
  129.0 20.4 %collective-permute-start.20 = (bf16[128,2048]{1,0:T(8,128)(2,1)S(1)}, bf16[128,2048]{1,0:T(8,128)(2,1)S(1)}, u32[]{:S(2)}, u32[]{:S(2)}) collective-permute-start(bf16[128,2048]{1,0:T(8,128)(2,1)S(1)} %collective-permute-done.18), channel_id=1, source_target_pairs={{0,2},{2,4},{4,6},{6,7},{7,5},{5,3},{3,1},{1,0},{8,10},{10,12},{12... | collective-permute-start | bytes 1572872 | tf_op jit(solution)/shard_map/ppermute | solution.py:32
  138.3 22.3 %collective-permute-start.10 = (bf16[128,2048]{1,0:T(8,128)(2,1)S(1)}, bf16[128,2048]{1,0:T(8,128)(2,1)S(1)}, u32[]{:S(2)}, u32[]{:S(2)}) collective-permute-start(bf16[128,2048]{1,0:T(8,128)(2,1)S(1)} %add_convert_fusion.13), channel_id=1, source_target_pairs={{0,2},{2,4},{4,6},{6,7},{7,5},{5,3},{3,1},{1,0},{8,10},{10,12},{12... | collective-permute-start | bytes 1572872 | tf_op jit(solution)/shard_map/ppermute | solution.py:53
  147.7 18.6 %collective-permute-start.23 = (bf16[64,2048]{1,0:T(8,128)(2,1)S(1)}, bf16[64,2048]{1,0:T(8,128)(2,1)S(1)}, u32[]{:S(2)}, u32[]{:S(2)}) collective-permute-start(bf16[64,2048]{1,0:T(8,128)(2,1)S(1)} %slice.344), channel_id=1, source_target_pairs={{2,0},{4,2},{6,4},{7,6},{5,7},{3,5},{1,3},{0,1},{10,8},{12,10},{14... | collective-permute-start | bytes 786440 | tf_op jit(solution)/shard_map/ppermute | solution.py:36
  149.4 16.8 %collective-permute-start.22 = (bf16[64,2048]{1,0:T(8,128)(2,1)S(1)}, bf16[64,2048]{1,0:T(8,128)(2,1)S(1)}, u32[]{:S(2)}, u32[]{:S(2)}) collective-permute-start(bf16[64,2048]{1,0:T(8,128)(2,1)S(1)} %slice.343), channel_id=1, source_target_pairs={{0,2},{2,4},{4,6},{6,7},{7,5},{5,3},{3,1},{1,0},{8,10},{10,12},{12... | collective-permute-start | bytes 786440 | tf_op jit(solution)/shard_map/ppermute | solution.py:35
  162.1 117.0 %collective-permute-start.11 = (bf16[128,2048]{1,0:T(8,128)(2,1)}, bf16[128,2048]{1,0:T(8,128)(2,1)}, u32[]{:S(2)}, u32[]{:S(2)}) collective-permute-start(bf16[128,2048]{1,0:T(8,128)(2,1)} %get-tuple-element.54), channel_id=1, source_target_pairs={{0,2},{2,4},{4,6},{6,7},{7,5},{5,3},{3,1},{1,0},{8,10},{10,12},{12... | collective-permute-start | bytes 1572872 | tf_op jit(solution)/shard_map/ppermute | solution.py:53
  163.2 95.8 %collective-permute-start.14 = (bf16[128,2048]{1,0:T(8,128)(2,1)}, bf16[128,2048]{1,0:T(8,128)(2,1)}, u32[]{:S(2)}, u32[]{:S(2)}) collective-permute-start(bf16[128,2048]{1,0:T(8,128)(2,1)} %get-tuple-element.55), channel_id=1, source_target_pairs={{2,0},{4,2},{6,4},{7,6},{5,7},{3,5},{1,3},{0,1},{10,8},{12,10},{14... | collective-permute-start | bytes 1572872 | tf_op jit(solution)/shard_map/ppermute | solution.py:54
  260.8 58.7 %collective-permute-start.38 = (bf16[2,512,768]{2,1,0:T(8,128)(2,1)S(1)}, bf16[2,512,768]{2,1,0:T(8,128)(2,1)S(1)}, u32[]{:S(2)}, u32[]{:S(2)}) collective-permute-start(bf16[2,512,768]{2,1,0:T(8,128)(2,1)S(1)} %copy-done.5), channel_id=1, source_target_pairs={{0,8},{8,0},{16,24},{24,16},{1,9},{9,1},{17,25},{25,17},{2,10},{10... | collective-permute-start | bytes 4718600 | tf_op jit(solution)/shard_map/ppermute | solution.py:280
  263.3 58.0 %collective-permute-start.36 = (bf16[2,512,768]{2,1,0:T(8,128)(2,1)S(1)}, bf16[2,512,768]{2,1,0:T(8,128)(2,1)S(1)}, u32[]{:S(2)}, u32[]{:S(2)}) collective-permute-start(bf16[2,512,768]{2,1,0:T(8,128)(2,1)S(1)} %get-tuple-element.43), channel_id=1, source_target_pairs={{0,8},{8,0},{16,24},{24,16},{1,9},{9,1},{17,25},{25,17},{2,10},{10... | collective-permute-start | bytes 4718600 | tf_op jit(solution)/shard_map/ppermute | solution.py:280
  263.6 17.1 %collective-permute-start.15 = (bf16[128,2048]{1,0:T(8,128)(2,1)S(1)}, bf16[128,2048]{1,0:T(8,128)(2,1)S(1)}, u32[]{:S(2)}, u32[]{:S(2)}) collective-permute-start(bf16[128,2048]{1,0:T(8,128)(2,1)S(1)} %add_convert_fusion.10), channel_id=1, source_target_pairs={{2,0},{4,2},{6,4},{7,6},{5,7},{3,5},{1,3},{0,1},{10,8},{12,10},{14... | collective-permute-start | bytes 1572872 | tf_op jit(solution)/shard_map/ppermute | solution.py:54
  276.3 39.9 %collective-permute-start.29 = (bf16[128,2048]{1,0:T(8,128)(2,1)S(1)}, bf16[128,2048]{1,0:T(8,128)(2,1)S(1)}, u32[]{:S(2)}, u32[]{:S(2)}) collective-permute-start(bf16[128,2048]{1,0:T(8,128)(2,1)S(1)} %pad_maximum_fusion.6), channel_id=1, source_target_pairs={{2,0},{4,2},{6,4},{7,6},{5,7},{3,5},{1,3},{0,1},{10,8},{12,10},{14... | collective-permute-start | bytes 1572872 | tf_op jit(solution)/shard_map/ppermute | solution.py:54
  280.7 18.9 %collective-permute-start.45 = (bf16[384,512]{1,0:T(8,128)(2,1)S(1)}, bf16[384,512]{1,0:T(8,128)(2,1)S(1)}, u32[]{:S(2)}, u32[]{:S(2)}) collective-permute-start(bf16[384,512]{1,0:T(8,128)(2,1)S(1)} %fusion.18), channel_id=1, source_target_pairs={{0,16},{8,24},{16,0},{24,8},{1,17},{9,25},{17,1},{25,9},{2,18},{10... | collective-permute-start | bytes 1179656 | tf_op jit(solution)/shard_map/ppermute | solution.py:281
  291.2 16.9 %collective-permute-start.43 = (bf16[384,512]{1,0:T(8,128)(2,1)S(1)}, bf16[384,512]{1,0:T(8,128)(2,1)S(1)}, u32[]{:S(2)}, u32[]{:S(2)}) collective-permute-start(bf16[384,512]{1,0:T(8,128)(2,1)S(1)} %fusion.17), channel_id=1, source_target_pairs={{0,16},{8,24},{16,0},{24,8},{1,17},{9,25},{17,1},{25,9},{2,18},{10... | collective-permute-start | bytes 1179656 | tf_op jit(solution)/shard_map/ppermute | solution.py:281
  299.6 15.2 %collective-permute-start.41 = (bf16[384,512]{1,0:T(8,128)(2,1)S(1)}, bf16[384,512]{1,0:T(8,128)(2,1)S(1)}, u32[]{:S(2)}, u32[]{:S(2)}) collective-permute-start(bf16[384,512]{1,0:T(8,128)(2,1)S(1)} %fusion.16), channel_id=1, source_target_pairs={{0,16},{8,24},{16,0},{24,8},{1,17},{9,25},{17,1},{25,9},{2,18},{10... | collective-permute-start | bytes 1179656 | tf_op jit(solution)/shard_map/ppermute | solution.py:281
  314.8 18.1 %collective-permute-start.34 = (bf16[2,512,768]{2,1,0:T(8,128)(2,1)S(1)}, bf16[2,512,768]{2,1,0:T(8,128)(2,1)S(1)}, u32[]{:S(2)}, u32[]{:S(2)}) collective-permute-start(bf16[2,512,768]{2,1,0:T(8,128)(2,1)S(1)} %get-tuple-element.41), channel_id=1, source_target_pairs={{0,8},{8,0},{16,24},{24,16},{1,9},{9,1},{17,25},{25,17},{2,10},{10... | collective-permute-start | bytes 4718600 | tf_op jit(solution)/shard_map/ppermute | solution.py:280
  316.3 18.5 %collective-permute-start.32 = (bf16[2,512,768]{2,1,0:T(8,128)(2,1)S(1)}, bf16[2,512,768]{2,1,0:T(8,128)(2,1)S(1)}, u32[]{:S(2)}, u32[]{:S(2)}) collective-permute-start(bf16[2,512,768]{2,1,0:T(8,128)(2,1)S(1)} %get-tuple-element.39), channel_id=1, source_target_pairs={{0,8},{8,0},{16,24},{24,16},{1,9},{9,1},{17,25},{25,17},{2,10},{10... | collective-permute-start | bytes 4718600 | tf_op jit(solution)/shard_map/ppermute | solution.py:280
  319.0 16.6 %collective-permute-start.27 = (bf16[128,2048]{1,0:T(8,128)(2,1)S(1)}, bf16[128,2048]{1,0:T(8,128)(2,1)S(1)}, u32[]{:S(2)}, u32[]{:S(2)}) collective-permute-start(bf16[128,2048]{1,0:T(8,128)(2,1)S(1)} %get-tuple-element.62), channel_id=1, source_target_pairs={{0,2},{2,4},{4,6},{6,7},{7,5},{5,3},{3,1},{1,0},{8,10},{10,12},{12... | collective-permute-start | bytes 1572872 | tf_op jit(solution)/shard_map/ppermute | solution.py:53
  321.3 23.3 %collective-permute-start.39 = (bf16[512,768]{1,0:T(8,128)(2,1)S(1)}, bf16[512,768]{1,0:T(8,128)(2,1)S(1)}, u32[]{:S(2)}, u32[]{:S(2)}) collective-permute-start(bf16[512,768]{1,0:T(8,128)(2,1)S(1)} %fusion.7), channel_id=1, source_target_pairs={{0,16},{8,24},{16,0},{24,8},{1,17},{9,25},{17,1},{25,9},{2,18},{10... | collective-permute-start | bytes 2359304 | tf_op jit(solution)/shard_map/ppermute | solution.py:281
  331.2 27.4 %collective-permute-start.37 = (bf16[512,768]{1,0:T(8,128)(2,1)S(1)}, bf16[512,768]{1,0:T(8,128)(2,1)S(1)}, u32[]{:S(2)}, u32[]{:S(2)}) collective-permute-start(bf16[512,768]{1,0:T(8,128)(2,1)S(1)} %fusion.6), channel_id=1, source_target_pairs={{0,16},{8,24},{16,0},{24,8},{1,17},{9,25},{17,1},{25,9},{2,18},{10... | collective-permute-start | bytes 2359304 | tf_op jit(solution)/shard_map/ppermute | solution.py:281
  334.7 40.7 %collective-permute-start.35 = (bf16[512,768]{1,0:T(8,128)(2,1)S(1)}, bf16[512,768]{1,0:T(8,128)(2,1)S(1)}, u32[]{:S(2)}, u32[]{:S(2)}) collective-permute-start(bf16[512,768]{1,0:T(8,128)(2,1)S(1)} %fusion.5), channel_id=1, source_target_pairs={{0,16},{8,24},{16,0},{24,8},{1,17},{9,25},{17,1},{25,9},{2,18},{10... | collective-permute-start | bytes 2359304 | tf_op jit(solution)/shard_map/ppermute | solution.py:281
  335.5 53.5 %collective-permute-start.33 = (bf16[512,768]{1,0:T(8,128)(2,1)S(1)}, bf16[512,768]{1,0:T(8,128)(2,1)S(1)}, u32[]{:S(2)}, u32[]{:S(2)}) collective-permute-start(bf16[512,768]{1,0:T(8,128)(2,1)S(1)} %fusion.4), channel_id=1, source_target_pairs={{0,16},{8,24},{16,0},{24,8},{1,17},{9,25},{17,1},{25,9},{2,18},{10... | collective-permute-start | bytes 2359304 | tf_op jit(solution)/shard_map/ppermute | solution.py:281
  (36 other events, 333.1 us)

commit v2 on v0

v2 whole, which is shorter than its diff:
```python
import jax
import jax.numpy as jnp
from jax import lax
from jax.experimental import pallas as pl
from jax.experimental.pallas import tpu as pltpu
from jax.sharding import PartitionSpec as P


F32, BF16 = jnp.float32, jnp.bfloat16
LIMIT = 48 << 20
LANES = 128


def ring_pairs(count):
    order = list(range(0, count, 2)) + list(range(count - 1 - count % 2, 0, -2))
    ahead = [(order[i], order[(i + 1) % count]) for i in range(count)]
    return ahead, [(b, a) for a, b in ahead]


def narrow(a):
    return a.astype(BF16)


def wide(a):
    return a.astype(F32)


def dot(a, b, ca, cb):
    return lax.dot_general(a, b, (((ca,), (cb,)), ((), ())), preferred_element_type=F32)


def cost(flops, size):
    return pl.CostEstimate(flops=int(flops), bytes_accessed=int(size), transcendentals=0)


def call(kernel, flops, size, **kwargs):
    return pl.pallas_call(
        kernel, compiler_params=pltpu.CompilerParams(vmem_limit_bytes=LIMIT), cost_estimate=cost(flops, size), **kwargs
    )


def full(a):
    return pl.BlockSpec(a.shape, lambda *_: (0,) * a.ndim)


def route_rows(blocks, held, order, slots, room, lean, top, width, parts):
    flat = [part for block in blocks for part in block]
    sizes = [len(block) for block in blocks]
    count, rows = len(blocks), sum(part.shape[0] for part in blocks[0])
    part = width // parts

    def kernel(*refs):
        held_ref, order_ref, ins = refs[0], refs[1], list(refs[2 : 2 + len(flat)])
        outs, packed = refs[2 + len(flat) : -1], refs[-1]
        before = (
            lax.broadcasted_iota(jnp.int32, (rows, rows), 0)
            < lax.broadcasted_iota(jnp.int32, (rows, rows), 1)
        ).astype(BF16)
        place = lax.broadcasted_iota(jnp.int32, (room, rows), 0).astype(F32)
        kept = [[] for _ in range(slots)]
        for i, size in enumerate(sizes):
            pieces = [ins.pop(0)[...] for _ in range(size)]
            block = pieces[0] if size == 1 else jnp.concatenate(pieces, axis=0)
            meta = wide(block[:, width:]).T
            ids = meta[:top]
            fixed = meta[top : 2 * top] * 256.0 + meta[2 * top : 3 * top]
            gates = fixed / jnp.sum(fixed, axis=0, keepdims=True)
            rows_out, pick_out, gate_out = outs[3 * i : 3 * i + 3]
            picks = []
            for s in range(slots):
                same = ids == held_ref[s].astype(F32)
                hit = jnp.sum(jnp.where(same, 1.0, 0.0), axis=0, keepdims=True)
                gate = jnp.sum(jnp.where(same, gates, 0.0), axis=0, keepdims=True)
                rank = dot(narrow(jnp.broadcast_to(hit, (8, rows))), before, 1, 0)[:1]
                pick = jnp.where(place == rank, hit, 0.0)
                picks.append(pick)
                weight = jnp.sum(pick * gate, axis=1, keepdims=True)
                gate_out[s] = jnp.broadcast_to(weight, (room, LANES))
            pick = narrow(jnp.concatenate(picks, axis=0))
            pick_out[...] = pick
            sorted_rows = dot(pick, block[:, :width], 1, 0).reshape(slots, room, width)
            rows_out[...] = narrow(sorted_rows)
            for s in range(slots):
                kept[s].append(sorted_rows[s, :lean])
            if (i + 1) * lean % 16 == 0:
                n = len(kept[0]) * lean
                for s in range(slots):
                    packed[s, (i + 1) * lean - n : (i + 1) * lean, :] = narrow(jnp.concatenate(kept[s], axis=0))
                kept = [[] for _ in range(slots)]
        for j in range(parts):
            cols = pl.ds(pl.multiple_of(order_ref[j] * part, part), part)
            outs[3 * count + j][...] = packed[:, :, cols]

    shapes = [
        jax.ShapeDtypeStruct((slots, room, width), BF16),
        jax.ShapeDtypeStruct((slots * room, rows), BF16),
        jax.ShapeDtypeStruct((slots, room, LANES), F32),
    ] * count + [jax.ShapeDtypeStruct((slots, count * lean, part), BF16)] * parts
    outs = call(
        kernel,
        2 * count * slots * room * rows * width,
        2 * count * width * (rows + 2 * slots * room),
        in_specs=[pl.BlockSpec(memory_space=pltpu.SMEM)] * 2 + [full(a) for a in flat],
        out_specs=[full(a) for a in shapes],
        out_shape=shapes,
        scratch_shapes=[pltpu.VMEM((slots, count * lean, width), BF16)],
    )(held, order, *flat)
    return [outs[3 * i : 3 * i + 3] for i in range(count)], outs[3 * count :]


def pick_rows(blocks, picks, slots):
    flat = [part for block in blocks for part in block]
    sizes = [len(block) for block in blocks]
    count, width = len(blocks), flat[0].shape[1]
    total, rows = picks[0].shape

    def kernel(*refs):
        ins, sel, outs = list(refs[: len(flat)]), refs[len(flat) : len(flat) + count], refs[len(flat) + count :]
        for i, size in enumerate(sizes):
            parts = [ins.pop(0)[...] for _ in range(size)]
            block = parts[0] if size == 1 else jnp.concatenate(parts, axis=0)
            outs[i][...] = narrow(dot(sel[i][...], block, 1, 0)).reshape(slots, total // slots, width)

    shapes = [jax.ShapeDtypeStruct((slots, total // slots, width), BF16)] * count
    return call(
        kernel,
        2 * count * total * rows * width,
        2 * count * width * (rows + total),
        in_specs=[full(a) for a in flat + list(picks)],
        out_specs=[full(a) for a in shapes],
        out_shape=shapes,
    )(*flat, *picks)


def rows_of(refs):
    return jnp.concatenate([r[0] for r in refs], axis=0)


def forward(xs, gates, w_in, w_out, first, last):
    _, width, both = w_in.shape
    hidden, count, room = both // 2, len(xs), xs[0].shape[1]
    total, here = count * room, last - first

    def kernel(*refs):
        x_refs, g_refs = refs[:count], refs[count : 2 * count]
        wi_ref, wo_ref, out_ref, act_ref, lr_ref = refs[2 * count :]
        weight = rows_of(g_refs)[:, :1]
        pre = dot(rows_of(x_refs), wi_ref[0], 1, 0)
        gate, up = pre[:, :hidden], pre[:, hidden:]
        sig = jax.nn.sigmoid(gate)
        lean = weight * (gate * sig)
        act = narrow(lean * up)
        act_ref[0] = act
        lr_ref[0, :, :hidden] = weight * up * sig * (1.0 + gate * (1.0 - sig))
        lr_ref[0, :, hidden:] = lean
        out_ref[0] = narrow(dot(act, wo_ref[0], 1, 0)).reshape(count, room, width)

    at = lambda s: (s + first, 0, 0)
    shapes = [
        jax.ShapeDtypeStruct((here, count, room, width), BF16),
        jax.ShapeDtypeStruct((here, total, hidden), BF16),
        jax.ShapeDtypeStruct((here, total, both), F32),
    ]
    return call(
        kernel,
        2 * here * total * width * (both + hidden),
        2 * here * width * (2 * total + both + hidden),
        grid=(here,),
        in_specs=[pl.BlockSpec((1, room, width), at)] * count
        + [pl.BlockSpec((1, room, LANES), at)] * count
        + [pl.BlockSpec((1, width, both), at), pl.BlockSpec((1, hidden, width), at)],
        out_specs=[
            pl.BlockSpec((1, count, room, width), lambda s: (s, 0, 0, 0)),
            pl.BlockSpec((1, total, hidden), lambda s: (s, 0, 0)),
            pl.BlockSpec((1, total, both), lambda s: (s, 0, 0)),
        ],
        out_shape=shapes,
    )(*xs, *gates, w_in, w_out)


def backward(ds, lr, w_out, first, last, lean):
    count, (slots, room, width) = len(ds), ds[0].shape
    hidden, both = w_out.shape[1], lr.shape[2]
    total, here = count * room, last - first

    def kernel(*refs):
        d_refs = refs[:count]
        lr_ref, w_ref, all_ref, lean_ref = refs[count:]
        d_act = dot(rows_of(d_refs), w_ref[0], 1, 1)
        d_pre = jnp.concatenate([d_act * lr_ref[0, :, :hidden], d_act * lr_ref[0, :, hidden:]], axis=1)
        all_ref[0] = narrow(d_pre)
        rows = d_pre.reshape(count, room, both)[:, :lean].reshape(count * lean, both)
        lean_ref[0] = narrow(rows)

    at = lambda s: (s + first, 0, 0)
    return call(
        kernel,
        2 * here * total * width * hidden,
        2 * here * width * (total + hidden),
        grid=(here,),
        in_specs=[pl.BlockSpec((1, room, width), at)] * count
        + [pl.BlockSpec((1, total, both), lambda s: (s, 0, 0)), pl.BlockSpec((1, hidden, width), at)],
        out_specs=[
            pl.BlockSpec((1, total, both), lambda s: (s, 0, 0)),
            pl.BlockSpec((1, count * lean, both), lambda s: (s, 0, 0)),
        ],
        out_shape=[
            jax.ShapeDtypeStruct((here, total, both), BF16),
            jax.ShapeDtypeStruct((here, count * lean, both), BF16),
        ],
    )(*ds, lr, w_out)


def out_gradients(ds, acts, order, parts, first):
    count, (_, room, width) = len(ds), ds[0].shape
    here, total, hidden = acts.shape
    part, half = width // parts, parts // 2

    def kernel(*refs):
        order_ref, d_refs = refs[0], refs[1 : 1 + count]
        act_ref, first_ref, second_ref, whole = refs[1 + count :]
        whole[...] = narrow(dot(act_ref[0], rows_of(d_refs), 0, 0))
        for j in range(parts):
            cols = pl.ds(pl.multiple_of(order_ref[j] * part, part), part)
            (first_ref if j < half else second_ref)[j % half, 0] = whole[:, cols]

    shape = jax.ShapeDtypeStruct((half, here, hidden, part), BF16)
    spec = pl.BlockSpec((half, 1, hidden, part), lambda s, o: (0, s, 0, 0))
    return call(
        kernel,
        2 * here * total * width * hidden,
        2 * here * width * (total + hidden),
        grid_spec=pltpu.PrefetchScalarGridSpec(
            num_scalar_prefetch=1,
            grid=(here,),
            in_specs=[pl.BlockSpec((1, room, width), lambda s, o: (s + first, 0, 0))] * count
            + [pl.BlockSpec((1, total, hidden), lambda s, o: (s, 0, 0))],
            out_specs=[spec, spec],
            scratch_shapes=[pltpu.VMEM((hidden, width), BF16)],
        ),
        out_shape=[shape, shape],
    )(order, *ds, acts)


def in_gradients(xs, d_pres, first, last, into):
    slots, half_rows, part = xs[0].shape
    both, groups = d_pres[0].shape[2], len(d_pres)
    here = last - first

    def kernel(*refs):
        x = jnp.concatenate([r[0] for r in refs[: 2 * groups]], axis=0)
        d = jnp.concatenate([r[0] for r in refs[2 * groups : 3 * groups]], axis=0)
        refs[-1][0] = narrow(dot(x, d, 0, 0))

    at = lambda s: (s + first, 0, 0)
    return call(
        kernel,
        4 * here * groups * half_rows * part * both,
        4 * here * groups * half_rows * (part + both),
        grid=(here,),
        in_specs=[pl.BlockSpec((1, half_rows, part), at)] * (2 * groups)
        + [pl.BlockSpec((1, 2 * half_rows, both), lambda s: (s, 0, 0))] * groups
        + ([] if into is None else [pl.BlockSpec(memory_space=pl.ANY)]),
        out_specs=pl.BlockSpec((1, part, both), at),
        out_shape=jax.ShapeDtypeStruct((slots, part, both), BF16),
        input_output_aliases={} if into is None else {3 * groups: 0},
    )(*xs, *d_pres, *([] if into is None else [into]))


def rows_back(d_pres, w_in, count):
    slots, width, both = w_in.shape
    here, total = d_pres[0].shape[0], d_pres[0].shape[1]

    def kernel(*refs):
        w_ref, out_ref = refs[-2], refs[-1]
        for i in range(len(d_pres)):
            @pl.when(pl.program_id(0) // here == i)
            def _():
                out_ref[0] = narrow(dot(refs[i][0], w_ref[0], 1, 1)).reshape(out_ref.shape[1:])

    def at(i):
        return lambda s: (jnp.clip(s - i * here, 0, here - 1), 0, 0)

    return call(
        kernel,
        2 * total * width * slots * both,
        2 * width * slots * (total + both),
        grid=(slots,),
        in_specs=[pl.BlockSpec((1, total, both), at(i)) for i in range(len(d_pres))]
        + [pl.BlockSpec((1, width, both), lambda s: (s, 0, 0))],
        out_specs=pl.BlockSpec((1, count, total // count, width), lambda s: (s, 0, 0, 0)),
        out_shape=jax.ShapeDtypeStruct((slots, count, total // count, width), BF16),
    )(*d_pres, w_in)


def combine(outs, jobs, shapes):
    width = outs[0].shape[3]
    arrays, specs, plan = [], [], []
    for block, pick, addends in jobs:
        arrays += [o for o in outs] + [pick] + [a for _, a in addends]
        specs += [
            pl.BlockSpec((o.shape[0], 1, o.shape[2], width), lambda *_, b=block: (0, b, 0, 0)) for o in outs
        ]
        specs += [full(pick)] + [full(a) for _, a in addends]
        plan.append([at for at, _ in addends])
    out_shapes = [jax.ShapeDtypeStruct((n, width), BF16) for pieces in shapes for n in pieces]

    def kernel(*refs):
        ins, res = list(refs[: len(arrays)]), list(refs[len(arrays) :])
        for addends, pieces in zip(plan, shapes):
            rows = jnp.concatenate(
                [ins.pop(0)[...].reshape(-1, width) for _ in outs], axis=0
            )
            acc = dot(ins.pop(0)[...], rows, 0, 0)
            for at in addends:
                more = wide(ins.pop(0)[...])
                if more.shape[0] == acc.shape[0]:
                    acc = acc + more
                else:
                    cut = [acc[:at], acc[at : at + more.shape[0]] + more, acc[at + more.shape[0] :]]
                    acc = jnp.concatenate([c for c in cut if c.shape[0]], axis=0)
            at = 0
            for n in pieces:
                res.pop(0)[...] = narrow(acc[at : at + n])
                at += n

    size = sum(2 * a.size for a in out_shapes)
    return call(
        kernel,
        2 * len(jobs) * jobs[0][1].size * width,
        2 * len(jobs) * jobs[0][1].shape[0] * width + 3 * size,
        grid=(1,),
        in_specs=specs,
        out_specs=[full(a) for a in out_shapes],
        out_shape=out_shapes,
    )(*arrays)


def ring_scatter(outs, picks, pairs):
    ahead, back = pairs
    count, rows = len(ahead), picks[0].shape[1]
    half = rows // 2
    f, g = combine(outs, [(count - 1, picks[-1], [])], [[half, half]])
    offsets = (0, half)
    for step in range(count // 2 - 1, 0, -1):
        f = lax.ppermute(f, "expert", ahead)
        g = lax.ppermute(g, "expert", back)
        jobs = [(2 * step, picks[2 * step], [(offsets[0], f)]), (2 * step - 1, picks[2 * step - 1], [(offsets[1], g)])]
        f, g = combine(outs, jobs, [[rows], [rows]])
        offsets = (0, 0)
    f = lax.ppermute(f, "expert", ahead)
    g = lax.ppermute(g, "expert", back)
    return combine(outs, [(0, picks[0], [(0, f), (0, g)])], [[rows]])[0]


def ring_gather(block, pairs):
    ahead, back = pairs
    half = block.shape[0] // 2
    f = g = block
    blocks = [[block]]
    for _ in range(1, len(ahead) // 2):
        f = lax.ppermute(f, "expert", ahead)
        g = lax.ppermute(g, "expert", back)
        blocks += [[f], [g]]
    low = lax.ppermute(f[:half], "expert", ahead)
    high = lax.ppermute(g[half:], "expert", back)
    return blocks + [[low, high]], f


def body(tokens, d_mixed, w_in, w_out, expert_ids, gate_fixed, placement):
    rows, width = tokens.shape
    slots, experts, top = w_out.shape[0], placement.shape[0], expert_ids.shape[1]
    ring, parts = lax.axis_size("expert"), lax.axis_size("dp")
    me_e, me_p = lax.axis_index("expert"), lax.axis_index("dp")
    pairs = ring_pairs(ring)
    most = max(2, 5 * rows * top // (4 * experts))
    room, lean = -(-most // 16) * 16, -(-most // 8) * 8

    core_pairs = [(i, i ^ 1) for i in range(parts)]
    chip_pairs = [(i, (i + parts // 2) % parts) for i in range(parts)]
    far_pairs = [(i, (i ^ 1) + parts // 2 if i < parts // 2 else (i ^ 1) - parts // 2) for i in range(parts)]
    core, far, near = me_p % 2, (me_p // 2 + 1) % 2, me_p // 2
    order = jnp.stack([2 * far + 1 - core, 2 * near + 1 - core, 2 * far + core, 2 * near + core])
    routes = (far_pairs, core_pairs, chip_pairs)

    local = me_e * slots + jnp.arange(slots, dtype=jnp.int32)
    names = jnp.arange(experts, dtype=jnp.int32)
    held = jnp.sum(jnp.where(placement[None, :] == local[:, None], names[None, :], 0), axis=1)

    meta = jnp.concatenate([expert_ids, gate_fixed // 256, gate_fixed % 256], axis=1)
    meta = jnp.pad(meta, ((0, 0), (0, LANES - 3 * top))).astype(BF16)
    x_blocks, last = ring_gather(jnp.concatenate([tokens, meta], axis=1), pairs)
    start, _ = lax.optimization_barrier((d_mixed, last))
    d_blocks, _ = ring_gather(start, pairs)

    half = ring // 2
    routed, columns = [], []
    for i in range(2):
        got, cols = route_rows(x_blocks[i * half : (i + 1) * half], held, order, slots, room, lean, top, width, parts)
        routed += got
        columns.append([lax.ppermute(cols[j], "dp", routes[j]) for j in range(parts - 1)] + [cols[-1]])
    xs, picks, gates = (list(a) for a in zip(*routed))

    pair = slots // 2
    lows = range(0, slots, pair)
    outs, acts, lrs = zip(*[forward(xs, gates, w_in, w_out, low, low + pair) for low in lows])
    ds = []
    for low, high in ((0, half), (half, ring - 1), (ring - 1, ring)):
        ds += pick_rows(d_blocks[low:high], picks[low:high], slots)

    d_pres, leans, grads = [], [], []
    for low, act, lr in zip(lows, acts, lrs):
        d_pre, mine = backward(ds, lr, w_out, low, low + pair, lean)
        d_pres.append(d_pre)
        across = lax.ppermute(mine, "dp", chip_pairs)
        beside = lax.ppermute(mine, "dp", core_pairs)
        both = lax.ppermute(across, "dp", core_pairs)
        leans.append([both, beside, across, mine])
        give, keep = out_gradients(ds, act, order, parts, low)
        got = lax.ppermute(give, "dp", core_pairs)
        away = lax.ppermute(narrow(wide(keep[0]) + wide(got[0])), "dp", chip_pairs)
        grads.append(narrow(wide(keep[1]) + wide(got[1]) + wide(away)))
    grad_out = jnp.concatenate(grads, axis=0)
    rows_by_group = [columns[i][j] for j in range(parts) for i in range(2)]
    grad_in = None
    for low, d_lean in zip(lows, leans):
        grad_in = in_gradients(rows_by_group, d_lean, low, low + pair, grad_in)

    mixed = ring_scatter(outs, picks, pairs)
    backs = rows_back(d_pres, w_in, ring)
    d_tokens = ring_scatter([backs], picks, pairs)
    return mixed, d_tokens, grad_in, grad_out


def solution(mesh):
    rows, slots = P(("dp", "expert"), None), P("expert", None, None)
    return jax.shard_map(
        body,
        mesh=mesh,
        in_specs=(rows, rows, slots, slots, rows, rows, P()),
        out_specs=(rows, rows, P("expert", "dp", None), P("expert", None, "dp")),
        check_vma=False,
    )
```

time: 640 us -> 292 us (0.46)
  waiting for transfers between devices: 414 us -> 123 us
  Pallas kernels: 0 us -> 93.9 us
  local copies, waits for them, and re-layouts: 92.4 us -> 17 us
  matrix products: 71.2 us -> 0 us
  starting transfers between devices: 22.3 us -> 44 us
  between operations: 14.5 us -> 1.03 us
  other arithmetic: 19.4 us -> 11.4 us
    all_to_all x4 -> x0, waiting for transfers between devices: 414 us -> none  [the longest x1 111 us: body(): lax.all_to_all(x_send, 'expert', split_axis=0, concat_axis=0, tiled=True)]
    ppermute x0 -> x48, waiting for transfers between devices: none -> 123 us  [the longest x6 42.5 us: ring_gather(): f = lax.ppermute(f, 'expert', ahead)]
    pallas_call x0 -> x24, Pallas kernels: none -> 93.9 us  [the longest x10 20.5 us: combine(): call(kernel, 2 * len(jobs) * jobs[0][1].size * width, 2 * len(jobs) * job...]
    gather x16 -> x0, local copies, waits for them, and re-layouts: 83.1 us -> none  [gather_routes(): picked = jnp.take(rows, position[:, k], axis=0).astype(jnp.float32)]
    dot_general x8 -> x0, matrix products: 71.2 us -> none  [the longest x1 14.5 us: body(): jnp.einsum('secf,edf->secd', d_pre, w_in, preferred_element_type=jnp.floa...]
    ppermute x0 -> x48, starting transfers between devices: none -> 44 us  [the longest x8 13 us: ring_scatter(): f = lax.ppermute(f, 'expert', ahead)]
    all_to_all x4 -> x0, starting transfers between devices: 21.5 us -> none  [the longest x1 7.41 us: body(): lax.all_to_all(x_send, 'expert', split_axis=0, concat_axis=0, tiled=True)]
    unnamed x8 -> x100, local copies, waits for them, and re-layouts: 0.02 us -> 13.9 us
  transfers between devices with their start and end apart: 6 -> 48, of which waited for: 4 -> 22; matrix products, arithmetic and copies ran while one was open for 24% -> 3% of each run, Pallas kernels for 0% -> 32%
where the time goes in v2:
time: 292 us; the launch traced here: 290 us
  waiting for transfers between devices  123 us (42%)
  Pallas kernels  93.9 us (32%)
  starting transfers between devices  44 us (15%)
  local copies, waits for them, and re-layouts  17 us (6%)
  other arithmetic  11.4 us (4%)
    ppermute x6, waiting for transfers between devices, ring_gather(): f = lax.ppermute(f, 'expert', ahead)  42.5 us
    ppermute x8, waiting for transfers between devices, ring_scatter(): f = lax.ppermute(f, 'expert', ahead)  26.4 us
    pallas_call x10, Pallas kernels, combine(): call(kernel, 2 * len(jobs) * jobs[0][1].size * width, 2 * len(jobs) * job...  20.5 us
    pallas_call x2, Pallas kernels, forward(): call(kernel, 2 * here * total * width * (both + hidden), 2 * here * width...  20.2 us
    ppermute x8, waiting for transfers between devices, ring_scatter(): g = lax.ppermute(g, 'expert', back)  16.4 us
    ppermute x2, waiting for transfers between devices, body(): away = lax.ppermute(narrow(wide(keep[0]) + wide(got[0])), 'dp', chip_pairs)  15.1 us
    unnamed x100, local copies, waits for them, and re-layouts  13.9 us
    ppermute x8, starting transfers between devices, ring_scatter(): f = lax.ppermute(f, 'expert', ahead)  13 us
  transfers between devices with their start and end apart: 48, of which 22 were waited for; matrix products, arithmetic and copies ran while one was open for 3% of the time, Pallas kernels for 32%

profile of v2, /device:TPU:0, one launch (start us, length us, event | category | flops | bytes accessed | tf_op | source)
XLA Modules:
  0.0 290.4 jit_solution(17165332340753839889)
XLA Ops:
  3.3 3.1 %collective-permute-start = (bf16[128,2176]{1,0:T(8,128)(2,1)S(1)}, bf16[128,2176]{1,0:T(8,128)(2,1)S(1)}, u32[]{:S(2)}, u32[]{:S(2)}) collective-permute-start(bf16[128,2176]{1,0:T(8,128)(2,1)S(1)} %fusion.5.refs_2_), channel_id=1, source_target_pairs={{0,2},{2,4},{4,6},{6,7},{7,5},{5,3},{3,1},{1,0},{8,10},{10,12},{12... | collective-permute-start | bytes 1671176 | tf_op jit(solution)/shard_map/ppermute | solution.py:362
  6.4 12.5 %collective-permute-done.refs_3_ = bf16[128,2176]{1,0:T(8,128)(2,1)S(1)} collective-permute-done((bf16[128,2176]{1,0:T(8,128)(2,1)S(1)}, bf16[128,2176]{1,0:T(8,128)(2,1)S(1)}, u32[]{:S(2)}, u32[]{:S(2)}) %collective-permute-start) | collective-permute-done | bytes 557088 | tf_op jit(solution)/shard_map/ppermute | solution.py:362
  20.9 11.8 %collective-permute-done.2.refs_5_ = bf16[128,2176]{1,0:T(8,128)(2,1)S(1)} collective-permute-done((bf16[128,2176]{1,0:T(8,128)(2,1)S(1)}, bf16[128,2176]{1,0:T(8,128)(2,1)S(1)}, u32[]{:S(2)}, u32[]{:S(2)}) %collective-permute-start.2) | collective-permute-done | bytes 557088 | tf_op jit(solution)/shard_map/ppermute | solution.py:362
  36.3 9.3 %collective-permute-done.4.refs_3_ = bf16[128,2176]{1,0:T(8,128)(2,1)S(1)} collective-permute-done((bf16[128,2176]{1,0:T(8,128)(2,1)S(1)}, bf16[128,2176]{1,0:T(8,128)(2,1)S(1)}, u32[]{:S(2)}, u32[]{:S(2)}) %collective-permute-start.4) | collective-permute-done | bytes 557088 | tf_op jit(solution)/shard_map/ppermute | solution.py:362
  48.8 8.9 %collective-permute-done.16.refs_1_ = bf16[128,2048]{1,0:T(8,128)(2,1)} collective-permute-done((bf16[128,2048]{1,0:T(8,128)(2,1)}, bf16[128,2048]{1,0:T(8,128)(2,1)}, u32[]{:S(2)}, u32[]{:S(2)}) %collective-permute-start.16) | collective-permute-done | bytes 524320 | tf_op jit(solution)/shard_map/ppermute | solution.py:362
  59.0 3.0 %collective-permute-done.17.refs_2_ = bf16[128,2048]{1,0:T(8,128)(2,1)} collective-permute-done((bf16[128,2048]{1,0:T(8,128)(2,1)}, bf16[128,2048]{1,0:T(8,128)(2,1)}, u32[]{:S(2)}, u32[]{:S(2)}) %collective-permute-start.17) | collective-permute-done | bytes 524320 | tf_op jit(solution)/shard_map/ppermute | solution.py:363
  64.8 9.1 %collective-permute-done.5.refs_4_ = bf16[128,2176]{1,0:T(8,128)(2,1)S(1)} collective-permute-done((bf16[128,2176]{1,0:T(8,128)(2,1)S(1)}, bf16[128,2176]{1,0:T(8,128)(2,1)S(1)}, u32[]{:S(2)}, u32[]{:S(2)}) %collective-permute-start.5) | collective-permute-done | bytes 557088 | tf_op jit(solution)/shard_map/ppermute | solution.py:363
  77.8 3.9 %shard_map.102 = (bf16[4,48,2048]{2,1,0:T(8,128)(2,1)}, bf16[192,128]{1,0:T(8,128)(2,1)S(1)}, f32[4,48,128]{2,1,0:T(8,128)S(1)}, bf16[4,48,2048]{2,1,0:T(8,128)(...) custom-call(s32[4]{0:T(128)S(1)} %select_reduce_fusion.refs_0_, ...), custom_call_target="tpu_custom_call" | custom-call | flops 402653184 | bytes 8388608 | tf_op jit(solution)/shard_map/pallas_call | solution.py:99
  82.5 5.4 %collective-permute-done.7.refs_6_ = bf16[64,2176]{1,0:T(8,128)(2,1)} collective-permute-done((bf16[64,2176]{1,0:T(8,128)(2,1)}, bf16[64,2176]{1,0:T(8,128)(2,1)}, u32[]{:S(2)}, u32[]{:S(2)}) %collective-permute-start.7) | collective-permute-done | bytes 278560 | tf_op jit(solution)/shard_map/ppermute | solution.py:366
  88.9 4.3 %shard_map.103 = (bf16[4,48,2048]{2,1,0:T(8,128)(2,1)}, bf16[192,128]{1,0:T(8,128)(2,1)S(1)}, f32[4,48,128]{2,1,0:T(8,128)S(1)}, bf16[4,48,2048]{2,1,0:T(8,128)(...) custom-call(s32[4]{0:T(128)S(1)} %select_reduce_fusion.refs_0_, ...), custom_call_target="tpu_custom_call" | custom-call | flops 402653184 | bytes 8388608 | tf_op jit(solution)/shard_map/pallas_call | solution.py:99
  99.8 10.0 %shard_map.104 = (bf16[2,8,48,2048]{3,2,1,0:T(8,128)(2,1)}, bf16[2,384,384]{2,1,0:T(8,128)(2,1)S(1)}, f32[2,384,768]{2,1,0:T(8,128)}) custom-call(bf16[4,48,2048]{2,1,0:T(8,128)(2,1)S(1)} %copy-done.2, bf16[4,48,2048]{2,1,0:T(8,128)(2,1)S(1)} %copy-done.3, bf16[4,48,2048]{2,1,0:T(8,128)(2,1)S(1)} %copy-done.4, bf16[4,48,2048]{2,1,0:T(8,128)(2,1)S(1)} %copy-done.5, ...), custom_call_target="tpu_custom_call" | custom-call | flops 3623878656 | bytes 15728640 | tf_op jit(solution)/shard_map/pallas_call | solution.py:164
  109.8 10.2 %shard_map.105 = (bf16[2,8,48,2048]{3,2,1,0:T(8,128)(2,1)}, bf16[2,384,384]{2,1,0:T(8,128)(2,1)S(1)}, f32[2,384,768]{2,1,0:T(8,128)}) custom-call(bf16[4,48,2048]{2,1,0:T(8,128)(2,1)S(1)} %copy-done.2, bf16[4,48,2048]{2,1,0:T(8,128)(2,1)S(1)} %copy-done.3, bf16[4,48,2048]{2,1,0:T(8,128)(2,1)S(1)} %copy-done.4, bf16[4,48,2048]{2,1,0:T(8,128)(2,1)S(1)} %copy-done.5, ...), custom_call_target="tpu_custom_call" | custom-call | flops 3623878656 | bytes 15728640 | tf_op jit(solution)/shard_map/pallas_call | solution.py:164
  132.2 2.3 shard_map.107
  134.6 2.4 shard_map.111
  142.9 4.9 %shard_map.114 = (bf16[2,384,768]{2,1,0:T(8,128)(2,1)}, bf16[2,320,768]{2,1,0:T(8,128)(2,1)}) custom-call(bf16[4,48,2048]{2,1,0:T(8,128)(2,1)S(1)} %get-tuple-element.109.refs_0_.refs_1_, bf16[4,48,2048]{2,1,0:T(8,128)(2,1)S(1)} %get-tuple-element.110.refs_1_.refs_2_, bf16[4,48,2048]{2,1,0:T(8,128)(2,1)S(1)} %get-tuple-element.111.refs_2_.refs_3_, ...), custom_call_target="tpu_custom_call" | custom-call | flops 1207959552 | bytes 6291456 | tf_op jit(solution)/shard_map/pallas_call | solution.py:196
  147.7 5.0 %shard_map.115 = (bf16[2,384,768]{2,1,0:T(8,128)(2,1)}, bf16[2,320,768]{2,1,0:T(8,128)(2,1)}) custom-call(bf16[4,48,2048]{2,1,0:T(8,128)(2,1)S(1)} %get-tuple-element.109.refs_0_.refs_1_, bf16[4,48,2048]{2,1,0:T(8,128)(2,1)S(1)} %get-tuple-element.110.refs_1_.refs_2_, bf16[4,48,2048]{2,1,0:T(8,128)(2,1)S(1)} %get-tuple-element.111.refs_2_.refs_3_, ...), custom_call_target="tpu_custom_call" | custom-call | flops 1207959552 | bytes 6291456 | tf_op jit(solution)/shard_map/pallas_call | solution.py:196
  154.5 10.1 %shard_map.116.refs_0_.refs_3_ = bf16[4,8,48,2048]{3,2,1,0:T(8,128)(2,1)} custom-call(bf16[2,384,768]{2,1,0:T(8,128)(2,1)S(1)} %copy-done.18, bf16[2,384,768]{2,1,0:T(8,128)(2,1)S(1)} %copy-done.19, bf16[4,2048,768]{2,1,0:T(8,128)(2,1)} %refs_2_.1), custom_call_target="tpu_custom_call" | custom-call | flops 4831838208 | bytes 18874368 | tf_op jit(solution)/shard_map/pallas_call | solution.py:284
  171.8 3.4 %collective-permute-done.24.refs_2_ = bf16[64,2048]{1,0:T(8,128)(2,1)S(1)} collective-permute-done((bf16[64,2048]{1,0:T(8,128)(2,1)S(1)}, bf16[64,2048]{1,0:T(8,128)(2,1)S(1)}, u32[]{:S(2)}, u32[]{:S(2)}) %collective-permute-start.24) | collective-permute-done | bytes 262176 | tf_op jit(solution)/shard_map/ppermute | solution.py:346
  177.3 2.7 shard_map.118
  181.6 4.9 %collective-permute-done.12.refs_3_ = bf16[128,2048]{1,0:T(8,128)(2,1)S(1)} collective-permute-done((bf16[128,2048]{1,0:T(8,128)(2,1)S(1)}, bf16[128,2048]{1,0:T(8,128)(2,1)S(1)}, u32[]{:S(2)}, u32[]{:S(2)}) %collective-permute-start.12) | collective-permute-done | bytes 524320 | tf_op jit(solution)/shard_map/ppermute | solution.py:346
  188.3 2.3 shard_map.109
  192.1 2.7 collective-permute-done.37.refs_5_
  195.2 4.9 %shard_map.125 = (bf16[2,2,384,512]{3,2,1,0:T(8,128)(2,1)}, bf16[2,2,384,512]{3,2,1,0:T(8,128)(2,1)}) custom-call(s32[4]{0:T(128)S(1)} %pad_add_fusion.refs_1_.refs_0_, bf16[4,48,2048]{2,1,0:T(8,128)(2,1)S(1)} %get-tuple-element.109.refs_0_.refs_1_, bf16[4,48,2048]{2,1,0:T(8,128)(2,1)S(1)} %get-tuple-element.110.refs_1_.refs_2_, ...), custom_call_target="tpu_custom_call" | custom-call | flops 1207959552 | bytes 6291456 | tf_op jit(solution)/shard_map/pallas_call | solution.py:229
  200.2 4.9 %shard_map.124 = (bf16[2,2,384,512]{3,2,1,0:T(8,128)(2,1)}, bf16[2,2,384,512]{3,2,1,0:T(8,128)(2,1)}) custom-call(s32[4]{0:T(128)S(1)} %pad_add_fusion.refs_1_.refs_0_, bf16[4,48,2048]{2,1,0:T(8,128)(2,1)S(1)} %get-tuple-element.109.refs_0_.refs_1_, bf16[4,48,2048]{2,1,0:T(8,128)(2,1)S(1)} %get-tuple-element.110.refs_1_.refs_2_, ...), custom_call_target="tpu_custom_call" | custom-call | flops 1207959552 | bytes 6291456 | tf_op jit(solution)/shard_map/pallas_call | solution.py:229
  210.0 2.5 collective-permute-start.38
  214.4 7.4 %collective-permute-done.28.refs_2_ = bf16[128,2048]{1,0:T(8,128)(2,1)S(1)} collective-permute-done((bf16[128,2048]{1,0:T(8,128)(2,1)S(1)}, bf16[128,2048]{1,0:T(8,128)(2,1)S(1)}, u32[]{:S(2)}, u32[]{:S(2)}) %collective-permute-start.28) | collective-permute-done | bytes 524320 | tf_op jit(solution)/shard_map/ppermute | solution.py:346
  222.3 12.6 %collective-permute-done.29.refs_5_ = bf16[128,2048]{1,0:T(8,128)(2,1)S(1)} collective-permute-done((bf16[128,2048]{1,0:T(8,128)(2,1)S(1)}, bf16[128,2048]{1,0:T(8,128)(2,1)S(1)}, u32[]{:S(2)}, u32[]{:S(2)}) %collective-permute-start.29) | collective-permute-done | bytes 524320 | tf_op jit(solution)/shard_map/ppermute | solution.py:347
  242.5 8.8 %collective-permute-done.30.refs_2_ = bf16[128,2048]{1,0:T(8,128)(2,1)S(1)} collective-permute-done((bf16[128,2048]{1,0:T(8,128)(2,1)S(1)}, bf16[128,2048]{1,0:T(8,128)(2,1)S(1)}, u32[]{:S(2)}, u32[]{:S(2)}) %collective-permute-start.30) | collective-permute-done | bytes 524320 | tf_op jit(solution)/shard_map/ppermute | solution.py:351
  258.1 2.4 shard_map.121
  260.4 4.9 %shard_map.122.refs_12_ = bf16[4,512,768]{2,1,0:T(8,128)(2,1)} custom-call(bf16[4,160,512]{2,1,0:T(8,128)(2,1)S(1)} %collective-permute-done.32.refs_0_, bf16[4,160,512]{2,1,0:T(8,128)(2,1)} %collective-permute-done.33.refs_1_, bf16[4,160,512]{2,1,0:T(8,128)(2,1)S(1)} %collective-permute-done.34.refs_2_, bf16[4,160,512]{2,1,0:T(8,128)(2,1)S(1)} %copy-done.11, ...), custom_call_target="tpu_custom_call" | custom-call | flops 2013265920 | bytes 6553600 | tf_op jit(solution)/shard_map/pallas_call | solution.py:256
  266.3 4.9 %shard_map.123 = bf16[4,512,768]{2,1,0:T(8,128)(2,1)} custom-call(bf16[4,160,512]{2,1,0:T(8,128)(2,1)S(1)} %collective-permute-done.32.refs_0_, bf16[4,160,512]{2,1,0:T(8,128)(2,1)} %collective-permute-done.33.refs_1_, bf16[4,160,512]{2,1,0:T(8,128)(2,1)S(1)} %collective-permute-done.34.refs_2_, ...), custom_call_target="tpu_custom_call", output_to_operand_aliasing={{}: (12, {})} | custom-call | flops 2013265920 | bytes 6553600 | tf_op jit(solution)/shard_map/pallas_call | solution.py:256
  273.4 14.3 %collective-permute-done.45 = bf16[2,384,512]{2,1,0:T(8,128)(2,1)S(1)} collective-permute-done((bf16[2,384,512]{2,1,0:T(8,128)(2,1)}, bf16[2,384,512]{2,1,0:T(8,128)(2,1)S(1)}, u32[]{:S(2)}, u32[]{:S(2)}) %collective-permute-start.45) | collective-permute-done | bytes 786464 | tf_op jit(solution)/shard_map/ppermute | solution.py:421
  (205 shorter events, 89.7 us)
Async XLA Ops:
  3.3 15.6 %collective-permute-start = (bf16[128,2176]{1,0:T(8,128)(2,1)S(1)}, bf16[128,2176]{1,0:T(8,128)(2,1)S(1)}, u32[]{:S(2)}, u32[]{:S(2)}) collective-permute-start(bf16[128,2176]{1,0:T(8,128)(2,1)S(1)} %fusion.5.refs_2_), channel_id=1, source_target_pairs={{0,2},{2,4},{4,6},{6,7},{7,5},{5,3},{3,1},{1,0},{8,10},{10,12},{12... | collective-permute-start | bytes 1671176 | tf_op jit(solution)/shard_map/ppermute | solution.py:362
  46.9 15.1 %collective-permute-start.17 = (bf16[128,2048]{1,0:T(8,128)(2,1)}, bf16[128,2048]{1,0:T(8,128)(2,1)}, u32[]{:S(2)}, u32[]{:S(2)}) collective-permute-start(bf16[128,2048]{1,0:T(8,128)(2,1)} %refs_0_), channel_id=1, source_target_pairs={{2,0},{4,2},{6,4},{7,6},{5,7},{3,5},{1,3},{0,1},{10,8},{12,10},{14... | collective-permute-start | bytes 1572872 | tf_op jit(solution)/shard_map/ppermute | solution.py:363
  48.2 25.7 %collective-permute-start.5 = (bf16[128,2176]{1,0:T(8,128)(2,1)S(1)}, bf16[128,2176]{1,0:T(8,128)(2,1)S(1)}, u32[]{:S(2)}, u32[]{:S(2)}) collective-permute-start(bf16[128,2176]{1,0:T(8,128)(2,1)S(1)} %collective-permute-done.3.refs_2_), channel_id=1, source_target_pairs={{2,0},{4,2},{6,4},{7,6},{5,7},{3,5},{1,3},{0,1},{10,8},{12,10},{14... | collective-permute-start | bytes 1671176 | tf_op jit(solution)/shard_map/ppermute | solution.py:363
  57.7 35.5 %collective-permute-start.18 = (bf16[128,2048]{1,0:T(8,128)(2,1)}, bf16[128,2048]{1,0:T(8,128)(2,1)}, u32[]{:S(2)}, u32[]{:S(2)}) collective-permute-start(bf16[128,2048]{1,0:T(8,128)(2,1)} %collective-permute-done.16.refs_1_), channel_id=1, source_target_pairs={{0,2},{2,4},{4,6},{6,7},{7,5},{5,3},{3,1},{1,0},{8,10},{10,12},{12... | collective-permute-start | bytes 1572872 | tf_op jit(solution)/shard_map/ppermute | solution.py:362
  62.0 32.8 %collective-permute-start.19 = (bf16[128,2048]{1,0:T(8,128)(2,1)}, bf16[128,2048]{1,0:T(8,128)(2,1)}, u32[]{:S(2)}, u32[]{:S(2)}) collective-permute-start(bf16[128,2048]{1,0:T(8,128)(2,1)} %collective-permute-done.17.refs_2_), channel_id=1, source_target_pairs={{2,0},{4,2},{6,4},{7,6},{5,7},{3,5},{1,3},{0,1},{10,8},{12,10},{14... | collective-permute-start | bytes 1572872 | tf_op jit(solution)/shard_map/ppermute | solution.py:363
  63.5 18.3 %collective-permute-start.6 = (bf16[64,2176]{1,0:T(8,128)(2,1)}, bf16[64,2176]{1,0:T(8,128)(2,1)S(1)}, u32[]{:S(2)}, u32[]{:S(2)}) collective-permute-start(bf16[64,2176]{1,0:T(8,128)(2,1)} %slice.48), channel_id=1, source_target_pairs={{0,2},{2,4},{4,6},{6,7},{7,5},{5,3},{3,1},{1,0},{8,10},{10,12},{12... | collective-permute-start | bytes 835592 | tf_op jit(solution)/shard_map/ppermute | solution.py:365
  81.7 71.0 %collective-permute-start.32 = (bf16[4,160,512]{2,1,0:T(8,128)(2,1)}, bf16[4,160,512]{2,1,0:T(8,128)(2,1)S(1)}, u32[]{:S(2)}, u32[]{:S(2)}) collective-permute-start(bf16[4,160,512]{2,1,0:T(8,128)(2,1)} %get-tuple-element.128), channel_id=1, source_target_pairs={{0,24},{8,16},{16,8},{24,0},{1,25},{9,17},{17,9},{25,1},{2,26},{10... | collective-permute-start | bytes 1966088 | tf_op jit(solution)/shard_map/ppermute | solution.py:401
  93.2 30.5 %collective-permute-start.20 = (bf16[128,2048]{1,0:T(8,128)(2,1)}, bf16[128,2048]{1,0:T(8,128)(2,1)S(1)}, u32[]{:S(2)}, u32[]{:S(2)}) collective-permute-start(bf16[128,2048]{1,0:T(8,128)(2,1)} %collective-permute-done.18.refs_3_), channel_id=1, source_target_pairs={{0,2},{2,4},{4,6},{6,7},{7,5},{5,3},{3,1},{1,0},{8,10},{10,12},{12... | collective-permute-start | bytes 1572872 | tf_op jit(solution)/shard_map/ppermute | solution.py:362
  94.8 31.2 %collective-permute-start.21 = (bf16[128,2048]{1,0:T(8,128)(2,1)}, bf16[128,2048]{1,0:T(8,128)(2,1)S(1)}, u32[]{:S(2)}, u32[]{:S(2)}) collective-permute-start(bf16[128,2048]{1,0:T(8,128)(2,1)} %collective-permute-done.19.refs_0_), channel_id=1, source_target_pairs={{2,0},{4,2},{6,4},{7,6},{5,7},{3,5},{1,3},{0,1},{10,8},{12,10},{14... | collective-permute-start | bytes 1572872 | tf_op jit(solution)/shard_map/ppermute | solution.py:363
  129.0 40.7 %collective-permute-start.34 = (bf16[4,160,512]{2,1,0:T(8,128)(2,1)}, bf16[4,160,512]{2,1,0:T(8,128)(2,1)S(1)}, u32[]{:S(2)}, u32[]{:S(2)}) collective-permute-start(bf16[4,160,512]{2,1,0:T(8,128)(2,1)} %get-tuple-element.130), channel_id=1, source_target_pairs={{0,8},{8,0},{16,24},{24,16},{1,9},{9,1},{17,25},{25,17},{2,10},{10... | collective-permute-start | bytes 1966088 | tf_op jit(solution)/shard_map/ppermute | solution.py:401
  130.7 40.6 %collective-permute-start.36 = (bf16[4,160,512]{2,1,0:T(8,128)(2,1)}, bf16[4,160,512]{2,1,0:T(8,128)(2,1)S(1)}, u32[]{:S(2)}, u32[]{:S(2)}) collective-permute-start(bf16[4,160,512]{2,1,0:T(8,128)(2,1)} %get-tuple-element.132), channel_id=1, source_target_pairs={{0,16},{8,24},{16,0},{24,8},{1,17},{9,25},{17,1},{25,9},{2,18},{10... | collective-permute-start | bytes 1966088 | tf_op jit(solution)/shard_map/ppermute | solution.py:401
  138.9 41.2 %collective-permute-start.33 = (bf16[4,160,512]{2,1,0:T(8,128)(2,1)}, bf16[4,160,512]{2,1,0:T(8,128)(2,1)}, u32[]{:S(2)}, u32[]{:S(2)}) collective-permute-start(bf16[4,160,512]{2,1,0:T(8,128)(2,1)} %get-tuple-element.129), channel_id=1, source_target_pairs={{0,24},{8,16},{16,8},{24,0},{1,25},{9,17},{17,9},{25,1},{2,26},{10... | collective-permute-start | bytes 1966088 | tf_op jit(solution)/shard_map/ppermute | solution.py:401
  138.9 27.0 %collective-permute-start.10 = (bf16[128,2048]{1,0:T(8,128)(2,1)}, bf16[128,2048]{1,0:T(8,128)(2,1)S(1)}, u32[]{:S(2)}, u32[]{:S(2)}) collective-permute-start(bf16[128,2048]{1,0:T(8,128)(2,1)} %get-tuple-element.100), channel_id=1, source_target_pairs={{0,2},{2,4},{4,6},{6,7},{7,5},{5,3},{3,1},{1,0},{8,10},{10,12},{12... | collective-permute-start | bytes 1572872 | tf_op jit(solution)/shard_map/ppermute | solution.py:346
  169.7 16.8 %collective-permute-start.12 = (bf16[128,2048]{1,0:T(8,128)(2,1)S(1)}, bf16[128,2048]{1,0:T(8,128)(2,1)S(1)}, u32[]{:S(2)}, u32[]{:S(2)}) collective-permute-start(bf16[128,2048]{1,0:T(8,128)(2,1)S(1)} %get-tuple-element.103), channel_id=1, source_target_pairs={{0,2},{2,4},{4,6},{6,7},{7,5},{5,3},{3,1},{1,0},{8,10},{10,12},{12... | collective-permute-start | bytes 1572872 | tf_op jit(solution)/shard_map/ppermute | solution.py:346
  171.4 15.6 %collective-permute-start.13 = (bf16[128,2048]{1,0:T(8,128)(2,1)S(1)}, bf16[128,2048]{1,0:T(8,128)(2,1)S(1)}, u32[]{:S(2)}, u32[]{:S(2)}) collective-permute-start(bf16[128,2048]{1,0:T(8,128)(2,1)S(1)} %get-tuple-element.105), channel_id=1, source_target_pairs={{2,0},{4,2},{6,4},{7,6},{5,7},{3,5},{1,3},{0,1},{10,8},{12,10},{14... | collective-permute-start | bytes 1572872 | tf_op jit(solution)/shard_map/ppermute | solution.py:347
  175.2 15.4 %collective-permute-start.35 = (bf16[4,160,512]{2,1,0:T(8,128)(2,1)}, bf16[4,160,512]{2,1,0:T(8,128)(2,1)S(1)}, u32[]{:S(2)}, u32[]{:S(2)}) collective-permute-start(bf16[4,160,512]{2,1,0:T(8,128)(2,1)} %get-tuple-element.131), channel_id=1, source_target_pairs={{0,8},{8,0},{16,24},{24,16},{1,9},{9,1},{17,25},{25,17},{2,10},{10... | collective-permute-start | bytes 1966088 | tf_op jit(solution)/shard_map/ppermute | solution.py:401
  176.8 17.9 %collective-permute-start.37 = (bf16[4,160,512]{2,1,0:T(8,128)(2,1)}, bf16[4,160,512]{2,1,0:T(8,128)(2,1)}, u32[]{:S(2)}, u32[]{:S(2)}) collective-permute-start(bf16[4,160,512]{2,1,0:T(8,128)(2,1)} %get-tuple-element.133), channel_id=1, source_target_pairs={{0,16},{8,24},{16,0},{24,8},{1,17},{9,25},{17,1},{25,9},{2,18},{10... | collective-permute-start | bytes 1966088 | tf_op jit(solution)/shard_map/ppermute | solution.py:401
  180.1 20.0 %collective-permute-start.26 = (bf16[128,2048]{1,0:T(8,128)(2,1)}, bf16[128,2048]{1,0:T(8,128)(2,1)}, u32[]{:S(2)}, u32[]{:S(2)}) collective-permute-start(bf16[128,2048]{1,0:T(8,128)(2,1)} %get-tuple-element.122), channel_id=1, source_target_pairs={{0,2},{2,4},{4,6},{6,7},{7,5},{5,3},{3,1},{1,0},{8,10},{10,12},{12... | collective-permute-start | bytes 1572872 | tf_op jit(solution)/shard_map/ppermute | solution.py:346
  186.5 18.7 %collective-permute-start.27 = (bf16[128,2048]{1,0:T(8,128)(2,1)}, bf16[128,2048]{1,0:T(8,128)(2,1)}, u32[]{:S(2)}, u32[]{:S(2)}) collective-permute-start(bf16[128,2048]{1,0:T(8,128)(2,1)} %get-tuple-element.123), channel_id=1, source_target_pairs={{2,0},{4,2},{6,4},{7,6},{5,7},{3,5},{1,3},{0,1},{10,8},{12,10},{14... | collective-permute-start | bytes 1572872 | tf_op jit(solution)/shard_map/ppermute | solution.py:347
  186.9 27.4 %collective-permute-start.41 = (bf16[2,320,768]{2,1,0:T(8,128)(2,1)}, bf16[2,320,768]{2,1,0:T(8,128)(2,1)}, u32[]{:S(2)}, u32[]{:S(2)}) collective-permute-start(bf16[2,320,768]{2,1,0:T(8,128)(2,1)} %get-tuple-element.137.refs_11_), channel_id=1, source_target_pairs={{0,16},{8,24},{16,0},{24,8},{1,17},{9,25},{17,1},{25,9},{2,18},{10... | collective-permute-start | bytes 2949128 | tf_op jit(solution)/shard_map/ppermute | solution.py:415
  190.6 17.4 %collective-permute-start.14 = (bf16[128,2048]{1,0:T(8,128)(2,1)}, bf16[128,2048]{1,0:T(8,128)(2,1)S(1)}, u32[]{:S(2)}, u32[]{:S(2)}) collective-permute-start(bf16[128,2048]{1,0:T(8,128)(2,1)} %get-tuple-element.106), channel_id=1, source_target_pairs={{0,2},{2,4},{4,6},{6,7},{7,5},{5,3},{3,1},{1,0},{8,10},{10,12},{12... | collective-permute-start | bytes 1572872 | tf_op jit(solution)/shard_map/ppermute | solution.py:351
  194.7 15.3 %collective-permute-start.15 = (bf16[128,2048]{1,0:T(8,128)(2,1)S(1)}, bf16[128,2048]{1,0:T(8,128)(2,1)S(1)}, u32[]{:S(2)}, u32[]{:S(2)}) collective-permute-start(bf16[128,2048]{1,0:T(8,128)(2,1)S(1)} %get-tuple-element.107), channel_id=1, source_target_pairs={{2,0},{4,2},{6,4},{7,6},{5,7},{3,5},{1,3},{0,1},{10,8},{12,10},{14... | collective-permute-start | bytes 1572872 | tf_op jit(solution)/shard_map/ppermute | solution.py:352
  200.1 39.5 %collective-permute-start.46 = (bf16[2,2,384,512]{3,2,1,0:T(8,128)(2,1)}, bf16[2,2,384,512]{3,2,1,0:T(8,128)(2,1)}, u32[]{:S(2)}, u32[]{:S(2)}) collective-permute-start(bf16[2,2,384,512]{3,2,1,0:T(8,128)(2,1)} %get-tuple-element.143), channel_id=1, source_target_pairs={{0,8},{8,0},{16,24},{24,16},{1,9},{9,1},{17,25},{25,17},{2,10},{10... | collective-permute-start | bytes 4718600 | tf_op jit(solution)/shard_map/ppermute | solution.py:420
  205.1 34.8 %collective-permute-start.44 = (bf16[2,2,384,512]{3,2,1,0:T(8,128)(2,1)}, bf16[2,2,384,512]{3,2,1,0:T(8,128)(2,1)}, u32[]{:S(2)}, u32[]{:S(2)}) collective-permute-start(bf16[2,2,384,512]{3,2,1,0:T(8,128)(2,1)} %get-tuple-element.140), channel_id=1, source_target_pairs={{0,8},{8,0},{16,24},{24,16},{1,9},{9,1},{17,25},{25,17},{2,10},{10... | collective-permute-start | bytes 4718600 | tf_op jit(solution)/shard_map/ppermute | solution.py:420
  210.0 26.7 %collective-permute-start.38 = (bf16[2,320,768]{2,1,0:T(8,128)(2,1)}, bf16[2,320,768]{2,1,0:T(8,128)(2,1)}, u32[]{:S(2)}, u32[]{:S(2)}) collective-permute-start(bf16[2,320,768]{2,1,0:T(8,128)(2,1)} %get-tuple-element.136.refs_11_), channel_id=1, source_target_pairs={{0,16},{8,24},{16,0},{24,8},{1,17},{9,25},{17,1},{25,9},{2,18},{10... | collective-permute-start | bytes 2949128 | tf_op jit(solution)/shard_map/ppermute | solution.py:415
  214.4 24.3 %collective-permute-start.43 = (bf16[2,320,768]{2,1,0:T(8,128)(2,1)S(1)}, bf16[2,320,768]{2,1,0:T(8,128)(2,1)S(1)}, u32[]{:S(2)}, u32[]{:S(2)}) collective-permute-start(bf16[2,320,768]{2,1,0:T(8,128)(2,1)S(1)} %copy-done.46), channel_id=1, source_target_pairs={{0,8},{8,0},{16,24},{24,16},{1,9},{9,1},{17,25},{25,17},{2,10},{10... | collective-permute-start | bytes 2949128 | tf_op jit(solution)/shard_map/ppermute | solution.py:416
  234.9 25.6 %collective-permute-start.42 = (bf16[2,320,768]{2,1,0:T(8,128)(2,1)}, bf16[2,320,768]{2,1,0:T(8,128)(2,1)S(1)}, u32[]{:S(2)}, u32[]{:S(2)}) collective-permute-start(bf16[2,320,768]{2,1,0:T(8,128)(2,1)} %collective-permute-done.41.refs_10_), channel_id=1, source_target_pairs={{0,8},{8,0},{16,24},{24,16},{1,9},{9,1},{17,25},{25,17},{2,10},{10... | collective-permute-start | bytes 2949128 | tf_op jit(solution)/shard_map/ppermute | solution.py:417
  238.6 26.7 %collective-permute-start.40 = (bf16[2,320,768]{2,1,0:T(8,128)(2,1)}, bf16[2,320,768]{2,1,0:T(8,128)(2,1)S(1)}, u32[]{:S(2)}, u32[]{:S(2)}) collective-permute-start(bf16[2,320,768]{2,1,0:T(8,128)(2,1)} %get-tuple-element.136.refs_11_), channel_id=1, source_target_pairs={{0,8},{8,0},{16,24},{24,16},{1,9},{9,1},{17,25},{25,17},{2,10},{10... | collective-permute-start | bytes 2949128 | tf_op jit(solution)/shard_map/ppermute | solution.py:416
  239.6 25.7 %collective-permute-start.39 = (bf16[2,320,768]{2,1,0:T(8,128)(2,1)}, bf16[2,320,768]{2,1,0:T(8,128)(2,1)S(1)}, u32[]{:S(2)}, u32[]{:S(2)}) collective-permute-start(bf16[2,320,768]{2,1,0:T(8,128)(2,1)} %collective-permute-done.38.refs_10_), channel_id=1, source_target_pairs={{0,8},{8,0},{16,24},{24,16},{1,9},{9,1},{17,25},{25,17},{2,10},{10... | collective-permute-start | bytes 2949128 | tf_op jit(solution)/shard_map/ppermute | solution.py:417
  239.9 15.6 %collective-permute-start.31 = (bf16[128,2048]{1,0:T(8,128)(2,1)S(1)}, bf16[128,2048]{1,0:T(8,128)(2,1)S(1)}, u32[]{:S(2)}, u32[]{:S(2)}) collective-permute-start(bf16[128,2048]{1,0:T(8,128)(2,1)S(1)} %get-tuple-element.127), channel_id=1, source_target_pairs={{2,0},{4,2},{6,4},{7,6},{5,7},{3,5},{1,3},{0,1},{10,8},{12,10},{14... | collective-permute-start | bytes 1572872 | tf_op jit(solution)/shard_map/ppermute | solution.py:352
  251.3 20.6 %collective-permute-start.47 = (bf16[2,384,512]{2,1,0:T(8,128)(2,1)}, bf16[2,384,512]{2,1,0:T(8,128)(2,1)S(1)}, u32[]{:S(2)}, u32[]{:S(2)}) collective-permute-start(bf16[2,384,512]{2,1,0:T(8,128)(2,1)} %fusion.4), channel_id=1, source_target_pairs={{0,16},{8,24},{16,0},{24,8},{1,17},{9,25},{17,1},{25,9},{2,18},{10... | collective-permute-start | bytes 2359304 | tf_op jit(solution)/shard_map/ppermute | solution.py:421
  255.5 32.2 %collective-permute-start.45 = (bf16[2,384,512]{2,1,0:T(8,128)(2,1)}, bf16[2,384,512]{2,1,0:T(8,128)(2,1)S(1)}, u32[]{:S(2)}, u32[]{:S(2)}) collective-permute-start(bf16[2,384,512]{2,1,0:T(8,128)(2,1)} %fusion.3), channel_id=1, source_target_pairs={{0,16},{8,24},{16,0},{24,8},{1,17},{9,25},{17,1},{25,9},{2,18},{10... | collective-permute-start | bytes 2359304 | tf_op jit(solution)/shard_map/ppermute | solution.py:421
  (66 other events, 779.8 us)

commit v3 on v2

--- a/solution.py
+++ b/solution.py
@@ -7,7 +7,7 @@
 
 
 F32, BF16 = jnp.float32, jnp.bfloat16
-LIMIT = 48 << 20
+LIMIT = 20 << 20
 LANES = 128
 
 
@@ -17,6 +17,10 @@
     return ahead, [(b, a) for a, b in ahead]
 
 
+def in_hbm(a):
+    return pltpu.with_memory_space_constraint(a, pltpu.HBM)
+
+
 def narrow(a):
     return a.astype(BF16)
 
@@ -43,14 +47,42 @@
     return pl.BlockSpec(a.shape, lambda *_: (0,) * a.ndim)
 
 
-def route_rows(blocks, held, order, slots, room, lean, top, width, parts):
+def pack_rows(tokens, expert_ids, gate_fixed):
+    rows, width = tokens.shape
+    top, half = expert_ids.shape[1], rows // 2
+    expert_ids, gate_fixed = expert_ids.T, gate_fixed.T
+
+    def kernel(x_ref, ids_ref, gate_ref, low_ref, high_ref):
+        lane = lax.broadcasted_iota(jnp.int32, (top, LANES), 1)
+        here = lax.broadcasted_iota(jnp.int32, (top, LANES), 0)
+        gate = gate_ref[...]
+        meta = jnp.zeros((rows, LANES), F32)
+        for i, a in enumerate((ids_ref[...], lax.shift_right_logical(gate, 8), gate & 255)):
+            spread = jnp.where(lane == here + i * top, 1.0, 0.0)
+            meta = meta + dot(narrow(wide(a)), narrow(spread), 0, 0)
+        for i, ref in enumerate((low_ref, high_ref)):
+            ref[:, :width] = x_ref[i * half : (i + 1) * half, :]
+            ref[:, width:] = narrow(meta[i * half : (i + 1) * half])
+
+    shape = jax.ShapeDtypeStruct((half, width + LANES), BF16)
+    return call(
+        kernel,
+        2 * rows * LANES * top,
+        4 * rows * width,
+        in_specs=[full(tokens), full(expert_ids), full(gate_fixed)],
+        out_specs=[full(shape)] * 2,
+        out_shape=[shape] * 2,
+    )(tokens, expert_ids, gate_fixed)
+
+
+def route_rows(blocks, placement, info, slots, room, lean, top, width, parts):
     flat = [part for block in blocks for part in block]
     sizes = [len(block) for block in blocks]
     count, rows = len(blocks), sum(part.shape[0] for part in blocks[0])
     part = width // parts
 
     def kernel(*refs):
-        held_ref, order_ref, ins = refs[0], refs[1], list(refs[2 : 2 + len(flat)])
+        place_ref, info_ref, ins = refs[0], refs[1], list(refs[2 : 2 + len(flat)])
         outs, packed = refs[2 + len(flat) : -1], refs[-1]
         before = (
             lax.broadcasted_iota(jnp.int32, (rows, rows), 0)
@@ -58,6 +90,10 @@
         ).astype(BF16)
         place = lax.broadcasted_iota(jnp.int32, (room, rows), 0).astype(F32)
         kept = [[] for _ in range(slots)]
+        held = [jnp.int32(0)] * slots
+        for e in range(placement.shape[0]):
+            for s in range(slots):
+                held[s] = jnp.where(place_ref[e] == info_ref[parts] + s, e, held[s])
         for i, size in enumerate(sizes):
             pieces = [ins.pop(0)[...] for _ in range(size)]
             block = pieces[0] if size == 1 else jnp.concatenate(pieces, axis=0)
@@ -68,7 +104,7 @@
             rows_out, pick_out, gate_out = outs[3 * i : 3 * i + 3]
             picks = []
             for s in range(slots):
-                same = ids == held_ref[s].astype(F32)
+                same = ids == held[s].astype(F32)
                 hit = jnp.sum(jnp.where(same, 1.0, 0.0), axis=0, keepdims=True)
                 gate = jnp.sum(jnp.where(same, gates, 0.0), axis=0, keepdims=True)
                 rank = dot(narrow(jnp.broadcast_to(hit, (8, rows))), before, 1, 0)[:1]
@@ -88,7 +124,7 @@
                     packed[s, (i + 1) * lean - n : (i + 1) * lean, :] = narrow(jnp.concatenate(kept[s], axis=0))
                 kept = [[] for _ in range(slots)]
         for j in range(parts):
-            cols = pl.ds(pl.multiple_of(order_ref[j] * part, part), part)
+            cols = pl.ds(pl.multiple_of(info_ref[j] * part, part), part)
             outs[3 * count + j][...] = packed[:, :, cols]
 
     shapes = [
@@ -104,7 +140,7 @@
         out_specs=[full(a) for a in shapes],
         out_shape=shapes,
         scratch_shapes=[pltpu.VMEM((slots, count * lean, width), BF16)],
-    )(held, order, *flat)
+    )(placement, info, *flat)
     return [outs[3 * i : 3 * i + 3] for i in range(count)], outs[3 * count :]
 
 
@@ -136,10 +172,10 @@
     return jnp.concatenate([r[0] for r in refs], axis=0)
 
 
-def forward(xs, gates, w_in, w_out, first, last):
-    _, width, both = w_in.shape
+def forward(xs, gates, w_in, w_out):
+    slots, width, both = w_in.shape
     hidden, count, room = both // 2, len(xs), xs[0].shape[1]
-    total, here = count * room, last - first
+    total = count * room
 
     def kernel(*refs):
         x_refs, g_refs = refs[:count], refs[count : 2 * count]
@@ -155,39 +191,40 @@
         lr_ref[0, :, hidden:] = lean
         out_ref[0] = narrow(dot(act, wo_ref[0], 1, 0)).reshape(count, room, width)
 
-    at = lambda s: (s + first, 0, 0)
+    at = lambda s: (s, 0, 0)
     shapes = [
-        jax.ShapeDtypeStruct((here, count, room, width), BF16),
-        jax.ShapeDtypeStruct((here, total, hidden), BF16),
-        jax.ShapeDtypeStruct((here, total, both), F32),
+        jax.ShapeDtypeStruct((slots, count, room, width), BF16),
+        jax.ShapeDtypeStruct((slots, total, hidden), BF16),
+        jax.ShapeDtypeStruct((slots, total, both), F32),
     ]
     return call(
         kernel,
-        2 * here * total * width * (both + hidden),
-        2 * here * width * (2 * total + both + hidden),
-        grid=(here,),
+        2 * slots * total * width * (both + hidden),
+        2 * slots * width * (2 * total + both + hidden),
+        grid=(slots,),
         in_specs=[pl.BlockSpec((1, room, width), at)] * count
         + [pl.BlockSpec((1, room, LANES), at)] * count
         + [pl.BlockSpec((1, width, both), at), pl.BlockSpec((1, hidden, width), at)],
         out_specs=[
             pl.BlockSpec((1, count, room, width), lambda s: (s, 0, 0, 0)),
-            pl.BlockSpec((1, total, hidden), lambda s: (s, 0, 0)),
-            pl.BlockSpec((1, total, both), lambda s: (s, 0, 0)),
+            pl.BlockSpec((1, total, hidden), at),
+            pl.BlockSpec((1, total, both), at),
         ],
         out_shape=shapes,
     )(*xs, *gates, w_in, w_out)
 
 
-def backward(ds, lr, w_out, first, last, lean):
+def backward(ds, lrs, w_out, first, last, lean):
     count, (slots, room, width) = len(ds), ds[0].shape
-    hidden, both = w_out.shape[1], lr.shape[2]
+    hidden, both = w_out.shape[1], lrs[0].shape[2]
     total, here = count * room, last - first
 
     def kernel(*refs):
         d_refs = refs[:count]
-        lr_ref, w_ref, all_ref, lean_ref = refs[count:]
+        w_ref, all_ref, lean_ref = refs[count + len(lrs) :]
         d_act = dot(rows_of(d_refs), w_ref[0], 1, 1)
-        d_pre = jnp.concatenate([d_act * lr_ref[0, :, :hidden], d_act * lr_ref[0, :, hidden:]], axis=1)
+        lr = rows_of(refs[count : count + len(lrs)])
+        d_pre = jnp.concatenate([d_act * lr[:, :hidden], d_act * lr[:, hidden:]], axis=1)
         all_ref[0] = narrow(d_pre)
         rows = d_pre.reshape(count, room, both)[:, :lean].reshape(count * lean, both)
         lean_ref[0] = narrow(rows)
@@ -199,7 +236,8 @@
         2 * here * width * (total + hidden),
         grid=(here,),
         in_specs=[pl.BlockSpec((1, room, width), at)] * count
-        + [pl.BlockSpec((1, total, both), lambda s: (s, 0, 0)), pl.BlockSpec((1, hidden, width), at)],
+        + [pl.BlockSpec((1, total // len(lrs), both), at)] * len(lrs)
+        + [pl.BlockSpec((1, hidden, width), at)],
         out_specs=[
             pl.BlockSpec((1, total, both), lambda s: (s, 0, 0)),
             pl.BlockSpec((1, count * lean, both), lambda s: (s, 0, 0)),
@@ -208,18 +246,18 @@
             jax.ShapeDtypeStruct((here, total, both), BF16),
             jax.ShapeDtypeStruct((here, count * lean, both), BF16),
         ],
-    )(*ds, lr, w_out)
-
-
-def out_gradients(ds, acts, order, parts, first):
+    )(*ds, *lrs, w_out)
+
+
+def out_gradients(ds, acts, order, parts, first, here):
     count, (_, room, width) = len(ds), ds[0].shape
-    here, total, hidden = acts.shape
+    total, hidden = count * room, acts[0].shape[2]
     part, half = width // parts, parts // 2
 
     def kernel(*refs):
         order_ref, d_refs = refs[0], refs[1 : 1 + count]
-        act_ref, first_ref, second_ref, whole = refs[1 + count :]
-        whole[...] = narrow(dot(act_ref[0], rows_of(d_refs), 0, 0))
+        act_refs, (first_ref, second_ref, whole) = refs[1 + count : -3], refs[-3:]
+        whole[...] = narrow(dot(rows_of(act_refs), rows_of(d_refs), 0, 0))
         for j in range(parts):
             cols = pl.ds(pl.multiple_of(order_ref[j] * part, part), part)
             (first_ref if j < half else second_ref)[j % half, 0] = whole[:, cols]
@@ -234,12 +272,34 @@
             num_scalar_prefetch=1,
             grid=(here,),
             in_specs=[pl.BlockSpec((1, room, width), lambda s, o: (s + first, 0, 0))] * count
-            + [pl.BlockSpec((1, total, hidden), lambda s, o: (s, 0, 0))],
+            + [pl.BlockSpec((1, total // len(acts), hidden), lambda s, o: (s + first, 0, 0))] * len(acts),
             out_specs=[spec, spec],
             scratch_shapes=[pltpu.VMEM((hidden, width), BF16)],
         ),
         out_shape=[shape, shape],
-    )(order, *ds, acts)
+    )(order, *ds, *acts)
+
+
+def finish(pieces):
+    arrays = [a for piece in pieces for a in piece]
+    here, hidden, part = pieces[0][2].shape
+    shape = jax.ShapeDtypeStruct((here * len(pieces), hidden, part), BF16)
+
+    def kernel(*refs):
+        for i in range(len(pieces)):
+            keep, got, away = refs[3 * i : 3 * i + 3]
+            refs[-1][i * here : (i + 1) * here] = narrow(wide(keep[0]) + wide(got[0]) + wide(away[...]))
+
+    own = pl.BlockSpec((1, here, hidden, part), lambda *_: (1, 0, 0, 0))
+    return call(
+        kernel,
+        3 * here * hidden * part,
+        8 * here * hidden * part,
+        grid=(1,),
+        in_specs=[own, own, full(pieces[0][2])] * len(pieces),
+        out_specs=full(shape),
+        out_shape=shape,
+    )(*arrays)
 
 
 def in_gradients(xs, d_pres, first, last, into):
@@ -267,49 +327,46 @@
     )(*xs, *d_pres, *([] if into is None else [into]))
 
 
-def rows_back(d_pres, w_in, count):
-    slots, width, both = w_in.shape
-    here, total = d_pres[0].shape[0], d_pres[0].shape[1]
-
-    def kernel(*refs):
-        w_ref, out_ref = refs[-2], refs[-1]
-        for i in range(len(d_pres)):
-            @pl.when(pl.program_id(0) // here == i)
-            def _():
-                out_ref[0] = narrow(dot(refs[i][0], w_ref[0], 1, 1)).reshape(out_ref.shape[1:])
-
-    def at(i):
-        return lambda s: (jnp.clip(s - i * here, 0, here - 1), 0, 0)
-
-    return call(
-        kernel,
-        2 * total * width * slots * both,
-        2 * width * slots * (total + both),
-        grid=(slots,),
-        in_specs=[pl.BlockSpec((1, total, both), at(i)) for i in range(len(d_pres))]
-        + [pl.BlockSpec((1, width, both), lambda s: (s, 0, 0))],
+def rows_back(d_pre, w_in, count, first):
+    here, total, both = d_pre.shape
+    width = w_in.shape[1]
+
+    def kernel(d_ref, w_ref, out_ref):
+        out_ref[0] = narrow(dot(d_ref[0], w_ref[0], 1, 1)).reshape(out_ref.shape[1:])
+
+    return call(
+        kernel,
+        2 * total * width * here * both,
+        2 * width * here * (total + both),
+        grid=(here,),
+        in_specs=[
+            pl.BlockSpec((1, total, both), lambda s: (s, 0, 0)),
+            pl.BlockSpec((1, width, both), lambda s: (s + first, 0, 0)),
+        ],
         out_specs=pl.BlockSpec((1, count, total // count, width), lambda s: (s, 0, 0, 0)),
-        out_shape=jax.ShapeDtypeStruct((slots, count, total // count, width), BF16),
-    )(*d_pres, w_in)
+        out_shape=jax.ShapeDtypeStruct((here, count, total // count, width), BF16),
+    )(d_pre, w_in)
 
 
 def combine(outs, jobs, shapes):
-    width = outs[0].shape[3]
+    width = outs[0][0].shape[3]
     arrays, specs, plan = [], [], []
     for block, pick, addends in jobs:
-        arrays += [o for o in outs] + [pick] + [a for _, a in addends]
+        count = outs[0][0].shape[1]
+        here, block = outs[block // count], block % count
+        arrays += [o for o in here] + [pick] + [a for _, a in addends]
         specs += [
-            pl.BlockSpec((o.shape[0], 1, o.shape[2], width), lambda *_, b=block: (0, b, 0, 0)) for o in outs
+            pl.BlockSpec((o.shape[0], 1, o.shape[2], width), lambda *_, b=block: (0, b, 0, 0)) for o in here
         ]
         specs += [full(pick)] + [full(a) for _, a in addends]
         plan.append([at for at, _ in addends])
-    out_shapes = [jax.ShapeDtypeStruct((n, width), BF16) for pieces in shapes for n in pieces]
+    out_shapes = [jax.ShapeDtypeStruct((n, width), BF16) for pieces in shapes for _, n in pieces]
 
     def kernel(*refs):
         ins, res = list(refs[: len(arrays)]), list(refs[len(arrays) :])
         for addends, pieces in zip(plan, shapes):
             rows = jnp.concatenate(
-                [ins.pop(0)[...].reshape(-1, width) for _ in outs], axis=0
+                [ins.pop(0)[...].reshape(-1, width) for _ in outs[0]], axis=0
             )
             acc = dot(ins.pop(0)[...], rows, 0, 0)
             for at in addends:
@@ -319,10 +376,8 @@
                 else:
                     cut = [acc[:at], acc[at : at + more.shape[0]] + more, acc[at + more.shape[0] :]]
                     acc = jnp.concatenate([c for c in cut if c.shape[0]], axis=0)
-            at = 0
-            for n in pieces:
+            for at, n in pieces:
                 res.pop(0)[...] = narrow(acc[at : at + n])
-                at += n
 
     size = sum(2 * a.size for a in out_shapes)
     return call(
@@ -340,17 +395,41 @@
     ahead, back = pairs
     count, rows = len(ahead), picks[0].shape[1]
     half = rows // 2
-    f, g = combine(outs, [(count - 1, picks[-1], [])], [[half, half]])
+    f, g = combine(outs, [(count - 1, picks[-1], [])], [[(0, half), (half, half)]])
     offsets = (0, half)
     for step in range(count // 2 - 1, 0, -1):
         f = lax.ppermute(f, "expert", ahead)
         g = lax.ppermute(g, "expert", back)
         jobs = [(2 * step, picks[2 * step], [(offsets[0], f)]), (2 * step - 1, picks[2 * step - 1], [(offsets[1], g)])]
-        f, g = combine(outs, jobs, [[rows], [rows]])
+        f, g = combine(outs, jobs, [[(0, rows)], [(0, rows)]])
         offsets = (0, 0)
     f = lax.ppermute(f, "expert", ahead)
     g = lax.ppermute(g, "expert", back)
-    return combine(outs, [(0, picks[0], [(0, f), (0, g)])], [[rows]])[0]
+    return combine(outs, [(0, picks[0], [(0, f), (0, g)])], [[(0, rows)]])[0]
+
+
+def ring_scatter_halves(outs, picks, pairs):
+    ahead, back = pairs
+    count, rows = len(ahead), picks[0].shape[1]
+    half, last = rows // 2, len(ahead) // 2
+    lows, highs = (0, half), (half, half)
+    lf, hg = combine(outs, [(count - 1, picks[-1], [])], [[lows, highs]])
+    lg = hf = None
+    for stage in range(1, last + 1):
+        lf = lax.ppermute(lf, "expert", ahead)
+        lg = None if lg is None else lax.ppermute(lg, "expert", back)
+        hf = None if hf is None else lax.ppermute(hf, "expert", ahead)
+        hg = lax.ppermute(hg, "expert", back)
+        if stage == last:
+            break
+        fwd, bwd = 2 * (last - stage), 2 * (last - stage) - 1
+        jobs = lambda at, f, g: [
+            (b, picks[b], [] if a is None else [(at, a)]) for b, a in ((fwd, f), (bwd, g))
+        ]
+        lf, lg = combine(outs, jobs(0, lf, lg), [[lows], [lows]])
+        hf, hg = combine(outs, jobs(half, hf, hg), [[highs], [highs]])
+    addends = [(0, lf), (0, lg), (half, hf), (half, hg)]
+    return combine(outs, [(0, picks[0], addends)], [[(0, rows)]])[0]
 
 
 def ring_gather(block, pairs):
@@ -364,7 +443,23 @@
         blocks += [[f], [g]]
     low = lax.ppermute(f[:half], "expert", ahead)
     high = lax.ppermute(g[half:], "expert", back)
-    return blocks + [[low, high]], f
+    return blocks + [[low, high]]
+
+
+def ring_gather_halves(low, high, pairs):
+    ahead, back = pairs
+    lf = lg = low
+    hf = hg = high
+    blocks = [[low, high]]
+    for _ in range(1, len(ahead) // 2):
+        lf = lax.ppermute(lf, "expert", ahead)
+        lg = lax.ppermute(lg, "expert", back)
+        hf = lax.ppermute(hf, "expert", ahead)
+        hg = lax.ppermute(hg, "expert", back)
+        blocks += [[lf, hf], [lg, hg]]
+    low = lax.ppermute(lf, "expert", ahead)
+    high = lax.ppermute(hg, "expert", back)
+    return blocks + [[low, high]]
 
 
 def body(tokens, d_mixed, w_in, w_out, expert_ids, gate_fixed, placement):
@@ -383,52 +478,52 @@
     order = jnp.stack([2 * far + 1 - core, 2 * near + 1 - core, 2 * far + core, 2 * near + core])
     routes = (far_pairs, core_pairs, chip_pairs)
 
-    local = me_e * slots + jnp.arange(slots, dtype=jnp.int32)
-    names = jnp.arange(experts, dtype=jnp.int32)
-    held = jnp.sum(jnp.where(placement[None, :] == local[:, None], names[None, :], 0), axis=1)
-
-    meta = jnp.concatenate([expert_ids, gate_fixed // 256, gate_fixed % 256], axis=1)
-    meta = jnp.pad(meta, ((0, 0), (0, LANES - 3 * top))).astype(BF16)
-    x_blocks, last = ring_gather(jnp.concatenate([tokens, meta], axis=1), pairs)
-    start, _ = lax.optimization_barrier((d_mixed, last))
-    d_blocks, _ = ring_gather(start, pairs)
-
+    info = jnp.concatenate([order, (me_e * slots)[None]])
+    w_in, w_out = in_hbm(w_in), in_hbm(w_out)
+    x_blocks = ring_gather_halves(*pack_rows(tokens, expert_ids, gate_fixed), pairs)
+    d_blocks = ring_gather(d_mixed, pairs)
+
+    x_blocks = [[in_hbm(a) for a in block] for block in x_blocks]
     half = ring // 2
     routed, columns = [], []
     for i in range(2):
-        got, cols = route_rows(x_blocks[i * half : (i + 1) * half], held, order, slots, room, lean, top, width, parts)
+        got, cols = route_rows(
+            x_blocks[i * half : (i + 1) * half], placement, info, slots, room, lean, top, width, parts
+        )
         routed += got
         columns.append([lax.ppermute(cols[j], "dp", routes[j]) for j in range(parts - 1)] + [cols[-1]])
     xs, picks, gates = (list(a) for a in zip(*routed))
 
     pair = slots // 2
     lows = range(0, slots, pair)
-    outs, acts, lrs = zip(*[forward(xs, gates, w_in, w_out, low, low + pair) for low in lows])
+    outs, acts, lrs = zip(
+        *[forward(xs[i * half : (i + 1) * half], gates[i * half : (i + 1) * half], w_in, w_out) for i in range(2)]
+    )
     ds = []
     for low, high in ((0, half), (half, ring - 1), (ring - 1, ring)):
         ds += pick_rows(d_blocks[low:high], picks[low:high], slots)
 
     d_pres, leans, grads = [], [], []
-    for low, act, lr in zip(lows, acts, lrs):
-        d_pre, mine = backward(ds, lr, w_out, low, low + pair, lean)
+    for low in lows:
+        d_pre, mine = backward(ds, lrs, w_out, low, low + pair, lean)
         d_pres.append(d_pre)
         across = lax.ppermute(mine, "dp", chip_pairs)
         beside = lax.ppermute(mine, "dp", core_pairs)
         both = lax.ppermute(across, "dp", core_pairs)
         leans.append([both, beside, across, mine])
-        give, keep = out_gradients(ds, act, order, parts, low)
+        give, keep = out_gradients(ds, acts, order, parts, low, pair)
         got = lax.ppermute(give, "dp", core_pairs)
         away = lax.ppermute(narrow(wide(keep[0]) + wide(got[0])), "dp", chip_pairs)
-        grads.append(narrow(wide(keep[1]) + wide(got[1]) + wide(away)))
-    grad_out = jnp.concatenate(grads, axis=0)
+        grads.append((keep, got, away))
+    grad_out = finish(grads)
     rows_by_group = [columns[i][j] for j in range(parts) for i in range(2)]
     grad_in = None
     for low, d_lean in zip(lows, leans):
         grad_in = in_gradients(rows_by_group, d_lean, low, low + pair, grad_in)
 
-    mixed = ring_scatter(outs, picks, pairs)
-    backs = rows_back(d_pres, w_in, ring)
-    d_tokens = ring_scatter([backs], picks, pairs)
+    mixed = ring_scatter([[o] for o in outs], picks, pairs)
+    backs = [rows_back(d_pre, w_in, ring, low) for low, d_pre in zip(lows, d_pres)]
+    d_tokens = ring_scatter_halves([backs], picks, pairs)
     return mixed, d_tokens, grad_in, grad_out
 
 

time: 292 us -> 293 us (level)
  waiting for transfers between devices: 123 us -> 159 us
  Pallas kernels: 93.9 us -> 67.1 us
  starting transfers between devices: 44 us -> 60.9 us
  local copies, waits for them, and re-layouts: 17 us -> 3.23 us
  other arithmetic: 11.4 us -> 0.53 us
    ppermute x0 -> x28, waiting for transfers between devices: none -> 79.3 us  [the longest x3 22.6 us: ring_gather_halves(): hf = lax.ppermute(hf, 'expert', ahead)]
    ppermute x2, waiting for transfers between devices: 1.86 us -> 36.3 us  [body(): across = lax.ppermute(mine, 'dp', chip_pairs)]
    ppermute x6 -> x3, waiting for transfers between devices: 42.5 us -> 8.71 us  [ring_gather(): f = lax.ppermute(f, 'expert', ahead)]
    ppermute x0 -> x28, starting transfers between devices: none -> 33.3 us  [the longest x3 6.75 us: ring_gather_halves(): lf = lax.ppermute(lf, 'expert', ahead)]
    ppermute x8 -> x4, waiting for transfers between devices: 26.4 us -> 9.15 us  [ring_scatter(): f = lax.ppermute(f, 'expert', ahead)]
    ppermute x8 -> x4, waiting for transfers between devices: 16.4 us -> 0.01 us  [ring_scatter(): g = lax.ppermute(g, 'expert', back)]
    pallas_call x10 -> x13, Pallas kernels: 20.5 us -> 7.07 us  [combine(): call(kernel, 2 * len(jobs) * jobs[0][1].size * width, 2 * len(jobs) * job...]
    ppermute x6 -> x3, waiting for transfers between devices: 12.6 us -> 0.01 us  [ring_gather(): g = lax.ppermute(g, 'expert', back)]
  transfers between devices with their start and end apart: 48 -> 60, of which waited for: 22 -> 23; matrix products, arithmetic and copies ran while one was open for 3% -> 0% of each run, Pallas kernels for 32% -> 22%
where the time goes in v3:
time: 293 us; the launch traced here: 292 us
  waiting for transfers between devices  159 us (54%)
  Pallas kernels  67.1 us (23%)
  starting transfers between devices  60.9 us (21%)
  local copies, waits for them, and re-layouts  3.23 us (1%)
    ppermute x2, waiting for transfers between devices, body(): across = lax.ppermute(mine, 'dp', chip_pairs)  36.3 us
    ppermute x3, waiting for transfers between devices, ring_gather_halves(): hf = lax.ppermute(hf, 'expert', ahead)  22.6 us
    ppermute x2, waiting for transfers between devices, body(): away = lax.ppermute(narrow(wide(keep[0]) + wide(got[0])), 'dp', chip_pairs)  22.2 us
    pallas_call x2, Pallas kernels, forward(): call(kernel, 2 * slots * total * width * (both + hidden), 2 * slots * wid...  20.1 us
    ppermute x3, waiting for transfers between devices, ring_scatter_halves(): hf = None if hf is None else lax.ppermute(hf, 'expert', ahead)  16.5 us
    ppermute x3, waiting for transfers between devices, ring_gather_halves(): lf = lax.ppermute(lf, 'expert', ahead)  10.8 us
    pallas_call x2, Pallas kernels, rows_back(): call(kernel, 2 * total * width * here * both, 2 * width * here * (total +...  9.52 us
    ppermute x4, waiting for transfers between devices, ring_scatter(): f = lax.ppermute(f, 'expert', ahead)  9.15 us
  transfers between devices with their start and end apart: 60, of which 23 were waited for; matrix products, arithmetic and copies ran while one was open for 0% of the time, Pallas kernels for 22%

profile of v3, /device:TPU:0, one launch (start us, length us, event | category | flops | bytes accessed | tf_op | source)
XLA Modules:
  0.0 292.3 jit_solution(5750101444987148147)
XLA Ops:
  3.3 3.1 %collective-permute-start = (bf16[64,2176]{1,0:T(8,128)(2,1)S(1)}, bf16[64,2176]{1,0:T(8,128)(2,1)S(1)}, u32[]{:S(2)}, u32[]{:S(2)}) collective-permute-start(bf16[64,2176]{1,0:T(8,128)(2,1)S(1)} %get-tuple-element.81.refs_2_), channel_id=1, source_target_pairs={{0,2},{2,4},{4,6},{6,7},{7,5},{5,3},{3,1},{1,0},{8,10},{10,12},{12... | collective-permute-start | bytes 835592 | tf_op jit(solution)/shard_map/ppermute | solution.py:455
  10.5 3.4 %collective-permute-done.refs_4_ = bf16[64,2176]{1,0:T(8,128)(2,1)S(1)} collective-permute-done((bf16[64,2176]{1,0:T(8,128)(2,1)S(1)}, bf16[64,2176]{1,0:T(8,128)(2,1)S(1)}, u32[]{:S(2)}, u32[]{:S(2)}) %collective-permute-start) | collective-permute-done | bytes 278560 | tf_op jit(solution)/shard_map/ppermute | solution.py:455
  15.8 14.3 %collective-permute-done.1.refs_5_ = bf16[64,2176]{1,0:T(8,128)(2,1)S(1)} collective-permute-done((bf16[64,2176]{1,0:T(8,128)(2,1)S(1)}, bf16[64,2176]{1,0:T(8,128)(2,1)S(1)}, u32[]{:S(2)}, u32[]{:S(2)}) %collective-permute-start.1) | collective-permute-done | bytes 278560 | tf_op jit(solution)/shard_map/ppermute | solution.py:457
  34.2 5.5 %collective-permute-done.4.refs_8_ = bf16[64,2176]{1,0:T(8,128)(2,1)S(1)} collective-permute-done((bf16[64,2176]{1,0:T(8,128)(2,1)S(1)}, bf16[64,2176]{1,0:T(8,128)(2,1)S(1)}, u32[]{:S(2)}, u32[]{:S(2)}) %collective-permute-start.4) | collective-permute-done | bytes 278560 | tf_op jit(solution)/shard_map/ppermute | solution.py:455
  41.5 4.1 %collective-permute-done.5.refs_9_ = bf16[64,2176]{1,0:T(8,128)(2,1)S(1)} collective-permute-done((bf16[64,2176]{1,0:T(8,128)(2,1)S(1)}, bf16[64,2176]{1,0:T(8,128)(2,1)S(1)}, u32[]{:S(2)}, u32[]{:S(2)}) %collective-permute-start.5) | collective-permute-done | bytes 278560 | tf_op jit(solution)/shard_map/ppermute | solution.py:457
  53.5 4.1 %collective-permute-done.9.refs_5_ = bf16[64,2176]{1,0:T(8,128)(2,1)S(1)} collective-permute-done((bf16[64,2176]{1,0:T(8,128)(2,1)S(1)}, bf16[64,2176]{1,0:T(8,128)(2,1)S(1)}, u32[]{:S(2)}, u32[]{:S(2)}) %collective-permute-start.9) | collective-permute-done | bytes 278560 | tf_op jit(solution)/shard_map/ppermute | solution.py:457
  60.1 8.7 %collective-permute-done.24.refs_3_ = bf16[128,2048]{1,0:T(8,128)(2,1)S(1)} collective-permute-done((bf16[128,2048]{1,0:T(8,128)(2,1)S(1)}, bf16[128,2048]{1,0:T(8,128)(2,1)S(1)}, u32[]{:S(2)}, u32[]{:S(2)}) %collective-permute-start.24) | collective-permute-done | bytes 524320 | tf_op jit(solution)/shard_map/ppermute | solution.py:441
  70.9 3.5 %collective-permute-done.10.refs_6_ = bf16[64,2176]{1,0:T(8,128)(2,1)} collective-permute-done((bf16[64,2176]{1,0:T(8,128)(2,1)}, bf16[64,2176]{1,0:T(8,128)(2,1)}, u32[]{:S(2)}, u32[]{:S(2)}) %collective-permute-start.10) | collective-permute-done | bytes 278560 | tf_op jit(solution)/shard_map/ppermute | solution.py:456
  74.9 5.4 %collective-permute-done.13.refs_9_ = bf16[64,2176]{1,0:T(8,128)(2,1)} collective-permute-done((bf16[64,2176]{1,0:T(8,128)(2,1)}, bf16[64,2176]{1,0:T(8,128)(2,1)}, u32[]{:S(2)}, u32[]{:S(2)}) %collective-permute-start.13) | collective-permute-done | bytes 278560 | tf_op jit(solution)/shard_map/ppermute | solution.py:461
  81.0 3.3 %shard_map.105 = (bf16[4,48,2048]{2,1,0:T(8,128)(2,1)S(1)}, bf16[192,128]{1,0:T(8,128)(2,1)S(1)}, f32[4,48,128]{2,1,0:T(8,128)S(1)}, bf16[4,48,2048]{2,1,0:T(8,1...) custom-call(s32[32]{0:T(128)S(1)} %copy-done.6, ...), custom_call_target="tpu_custom_call" | custom-call | flops 402653184 | bytes 8388608 | tf_op jit(solution)/shard_map/pallas_call | solution.py:135
  84.3 10.0 %shard_map.106 = (bf16[4,4,48,2048]{3,2,1,0:T(8,128)(2,1)S(1)}, bf16[4,192,384]{2,1,0:T(8,128)(2,1)S(1)}, f32[4,192,768]{2,1,0:T(8,128)S(1)}) custom-call(bf16[4,48,2048]{2,1,0:T(8,128)(2,1)S(1)} %get-tuple-element.94.refs_0_, bf16[4,48,2048]{2,1,0:T(8,128)(2,1)S(1)} %get-tuple-element.95.refs_1_, bf16[4,48,2048]{2,1,0:T(8,128)(2,1)S(1)} %get-tuple-element.96.refs_2_, ...), custom_call_target="tpu_custom_call" | custom-call | flops 3623878656 | bytes 25165824 | tf_op jit(solution)/shard_map/pallas_call | solution.py:200
  96.3 3.3 %shard_map.103 = (bf16[4,48,2048]{2,1,0:T(8,128)(2,1)S(1)}, bf16[192,128]{1,0:T(8,128)(2,1)S(1)}, f32[4,48,128]{2,1,0:T(8,128)S(1)}, bf16[4,48,2048]{2,1,0:T(8,1...) custom-call(s32[32]{0:T(128)S(1)} %copy-done.6, ...), custom_call_target="tpu_custom_call" | custom-call | flops 402653184 | bytes 8388608 | tf_op jit(solution)/shard_map/pallas_call | solution.py:135
  104.2 10.1 %shard_map.104 = (bf16[4,4,48,2048]{3,2,1,0:T(8,128)(2,1)S(1)}, bf16[4,192,384]{2,1,0:T(8,128)(2,1)S(1)}, f32[4,192,768]{2,1,0:T(8,128)S(1)}) custom-call(bf16[4,48,2048]{2,1,0:T(8,128)(2,1)S(1)} %get-tuple-element.83.refs_0_, bf16[4,48,2048]{2,1,0:T(8,128)(2,1)S(1)} %get-tuple-element.84.refs_1_, bf16[4,48,2048]{2,1,0:T(8,128)(2,1)S(1)} %get-tuple-element.85.refs_2_, ...), custom_call_target="tpu_custom_call" | custom-call | flops 3623878656 | bytes 25165824 | tf_op jit(solution)/shard_map/pallas_call | solution.py:200
  119.2 3.5 %shard_map.115 = (bf16[2,384,768]{2,1,0:T(8,128)(2,1)S(1)}, bf16[2,320,768]{2,1,0:T(8,128)(2,1)S(1)}) custom-call(bf16[4,48,2048]{2,1,0:T(8,128)(2,1)S(1)} %get-tuple-element.117.refs_0_.refs_1_, bf16[4,48,2048]{2,1,0:T(8,128)(2,1)S(1)} %get-tuple-element.118.refs_1_.refs_2_, bf16[4,48,2048]{2,1,0:T(8,128)(2,1)S(1)} %get-tuple-element.119.refs_2_.refs_3_, ...), custom_call_target="tpu_custom_call" | custom-call | flops 1207959552 | bytes 6291456 | tf_op jit(solution)/shard_map/pallas_call | solution.py:233
  122.7 3.5 %shard_map.117 = (bf16[2,384,768]{2,1,0:T(8,128)(2,1)S(1)}, bf16[2,320,768]{2,1,0:T(8,128)(2,1)S(1)}) custom-call(bf16[4,48,2048]{2,1,0:T(8,128)(2,1)S(1)} %get-tuple-element.117.refs_0_.refs_1_, bf16[4,48,2048]{2,1,0:T(8,128)(2,1)S(1)} %get-tuple-element.118.refs_1_.refs_2_, bf16[4,48,2048]{2,1,0:T(8,128)(2,1)S(1)} %get-tuple-element.119.refs_2_.refs_3_, ...), custom_call_target="tpu_custom_call" | custom-call | flops 1207959552 | bytes 6291456 | tf_op jit(solution)/shard_map/pallas_call | solution.py:233
  126.2 4.8 %shard_map.116.refs_0_.refs_4_.refs_3_ = bf16[2,8,48,2048]{3,2,1,0:T(8,128)(2,1)S(1)} custom-call(bf16[2,384,768]{2,1,0:T(8,128)(2,1)S(1)} %get-tuple-element.126.d_ref, bf16[4,2048,768]{2,1,0:T(8,128)(2,1)} %w_ref.3), custom_call_target="tpu_custom_call" | custom-call | flops 2415919104 | bytes 9437184 | tf_op jit(solution)/shard_map/pallas_call | solution.py:337
  133.0 4.8 %shard_map.118.refs_1_.refs_5_.refs_4_ = bf16[2,8,48,2048]{3,2,1,0:T(8,128)(2,1)S(1)} custom-call(bf16[2,384,768]{2,1,0:T(8,128)(2,1)S(1)} %get-tuple-element.127.d_ref, bf16[4,2048,768]{2,1,0:T(8,128)(2,1)} %w_ref.3), custom_call_target="tpu_custom_call" | custom-call | flops 2415919104 | bytes 9437184 | tf_op jit(solution)/shard_map/pallas_call | solution.py:337
  139.7 3.7 %collective-permute-done.45.refs_1_ = bf16[4,160,512]{2,1,0:T(8,128)(2,1)S(1)} collective-permute-done((bf16[4,160,512]{2,1,0:T(8,128)(2,1)S(1)}, bf16[4,160,512]{2,1,0:T(8,128)(2,1)S(1)}, u32[]{:S(2)}, u32[]{:S(2)}) %collective-permute-start.45) | collective-permute-done | bytes 655392 | tf_op jit(solution)/shard_map/ppermute | solution.py:494
  144.7 5.7 %collective-permute-done.30.refs_3_ = bf16[64,2048]{1,0:T(8,128)(2,1)S(1)} collective-permute-done((bf16[64,2048]{1,0:T(8,128)(2,1)S(1)}, bf16[64,2048]{1,0:T(8,128)(2,1)S(1)}, u32[]{:S(2)}, u32[]{:S(2)}) %collective-permute-start.30) | collective-permute-done | bytes 262176 | tf_op jit(solution)/shard_map/ppermute | solution.py:419
  153.9 5.7 %collective-permute-done.37.refs_6_ = bf16[64,2048]{1,0:T(8,128)(2,1)S(1)} collective-permute-done((bf16[64,2048]{1,0:T(8,128)(2,1)S(1)}, bf16[64,2048]{1,0:T(8,128)(2,1)S(1)}, u32[]{:S(2)}, u32[]{:S(2)}) %collective-permute-start.37) | collective-permute-done | bytes 262176 | tf_op jit(solution)/shard_map/ppermute | solution.py:422
  167.6 10.7 %collective-permute-done.38.refs_3_ = bf16[64,2048]{1,0:T(8,128)(2,1)S(1)} collective-permute-done((bf16[64,2048]{1,0:T(8,128)(2,1)S(1)}, bf16[64,2048]{1,0:T(8,128)(2,1)S(1)}, u32[]{:S(2)}, u32[]{:S(2)}) %collective-permute-start.38) | collective-permute-done | bytes 262176 | tf_op jit(solution)/shard_map/ppermute | solution.py:421
  179.6 3.1 %shard_map.129 = (bf16[2,2,384,512]{3,2,1,0:T(8,128)(2,1)S(1)}, bf16[2,2,384,512]{3,2,1,0:T(8,128)(2,1)S(1)}) custom-call(s32[4]{0:T(128)S(1)} %pad_add_fusion.refs_0_, bf16[4,48,2048]{2,1,0:T(8,128)(2,1)S(1)} %get-tuple-element.117.refs_0_.refs_1_, bf16[4,48,2048]{2,1,0:T(8,128)(2,1)S(1)} %get-tuple-element.118.refs_1_.refs_2_, ...), custom_call_target="tpu_custom_call" | custom-call | flops 1207959552 | bytes 6291456 | tf_op jit(solution)/shard_map/pallas_call | solution.py:267
  182.7 3.1 %shard_map.130 = (bf16[2,2,384,512]{3,2,1,0:T(8,128)(2,1)S(1)}, bf16[2,2,384,512]{3,2,1,0:T(8,128)(2,1)S(1)}) custom-call(s32[4]{0:T(128)S(1)} %pad_add_fusion.refs_0_, bf16[4,48,2048]{2,1,0:T(8,128)(2,1)S(1)} %get-tuple-element.117.refs_0_.refs_1_, bf16[4,48,2048]{2,1,0:T(8,128)(2,1)S(1)} %get-tuple-element.118.refs_1_.refs_2_, ...), custom_call_target="tpu_custom_call" | custom-call | flops 1207959552 | bytes 6291456 | tf_op jit(solution)/shard_map/pallas_call | solution.py:267
  189.4 5.8 %collective-permute-done.40.refs_3_ = bf16[64,2048]{1,0:T(8,128)(2,1)S(1)} collective-permute-done((bf16[64,2048]{1,0:T(8,128)(2,1)S(1)}, bf16[64,2048]{1,0:T(8,128)(2,1)S(1)}, u32[]{:S(2)}, u32[]{:S(2)}) %collective-permute-start.40) | collective-permute-done | bytes 262176 | tf_op jit(solution)/shard_map/ppermute | solution.py:421
  196.1 17.4 %collective-permute-done.50.refs_10_ = bf16[2,320,768]{2,1,0:T(8,128)(2,1)S(1)} collective-permute-done((bf16[2,320,768]{2,1,0:T(8,128)(2,1)S(1)}, bf16[2,320,768]{2,1,0:T(8,128)(2,1)S(1)}, u32[]{:S(2)}, u32[]{:S(2)}) %collective-permute-start.50) | collective-permute-done | bytes 983072 | tf_op jit(solution)/shard_map/ppermute | solution.py:510
  214.3 18.9 %collective-permute-done.53.refs_10_ = bf16[2,320,768]{2,1,0:T(8,128)(2,1)S(1)} collective-permute-done((bf16[2,320,768]{2,1,0:T(8,128)(2,1)S(1)}, bf16[2,320,768]{2,1,0:T(8,128)(2,1)S(1)}, u32[]{:S(2)}, u32[]{:S(2)}) %collective-permute-start.53) | collective-permute-done | bytes 983072 | tf_op jit(solution)/shard_map/ppermute | solution.py:510
  237.3 5.0 %collective-permute-done.36.refs_4_ = bf16[64,2048]{1,0:T(8,128)(2,1)S(1)} collective-permute-done((bf16[64,2048]{1,0:T(8,128)(2,1)S(1)}, bf16[64,2048]{1,0:T(8,128)(2,1)S(1)}, u32[]{:S(2)}, u32[]{:S(2)}) %collective-permute-start.36) | collective-permute-done | bytes 262176 | tf_op jit(solution)/shard_map/ppermute | solution.py:420
  248.2 9.1 %collective-permute-done.20.refs_2_ = bf16[128,2048]{1,0:T(8,128)(2,1)S(1)} collective-permute-done((bf16[128,2048]{1,0:T(8,128)(2,1)S(1)}, bf16[128,2048]{1,0:T(8,128)(2,1)S(1)}, u32[]{:S(2)}, u32[]{:S(2)}) %collective-permute-start.20) | collective-permute-done | bytes 524320 | tf_op jit(solution)/shard_map/ppermute | solution.py:406
  261.7 3.4 %shard_map.127.refs_12_ = bf16[4,512,768]{2,1,0:T(8,128)(2,1)} custom-call(bf16[4,160,512]{2,1,0:T(8,128)(2,1)S(1)} %collective-permute-done.44.refs_0_, bf16[4,160,512]{2,1,0:T(8,128)(2,1)S(1)} %collective-permute-done.45.refs_1_, bf16[4,160,512]{2,1,0:T(8,128)(2,1)S(1)} %collective-permute-done.46.refs_2_, ...), custom_call_target="tpu_custom_call" | custom-call | flops 2013265920 | bytes 6553600 | tf_op jit(solution)/shard_map/pallas_call | solution.py:316
  265.0 3.4 %shard_map.128 = bf16[4,512,768]{2,1,0:T(8,128)(2,1)} custom-call(bf16[4,160,512]{2,1,0:T(8,128)(2,1)S(1)} %collective-permute-done.44.refs_0_, bf16[4,160,512]{2,1,0:T(8,128)(2,1)S(1)} %collective-permute-done.45.refs_1_, bf16[4,160,512]{2,1,0:T(8,128)(2,1)S(1)} %collective-permute-done.46.refs_2_, ...), custom_call_target="tpu_custom_call", output_to_operand_aliasing={{}: (12, {})} | custom-call | flops 2013265920 | bytes 6553600 | tf_op jit(solution)/shard_map/pallas_call | solution.py:316
  268.4 9.3 %collective-permute-done.57.refs_2_ = bf16[2,384,512]{2,1,0:T(8,128)(2,1)S(1)} collective-permute-done((bf16[2,384,512]{2,1,0:T(8,128)(2,1)S(1)}, bf16[2,384,512]{2,1,0:T(8,128)(2,1)S(1)}, u32[]{:S(2)}, u32[]{:S(2)}) %collective-permute-start.57) | collective-permute-done | bytes 786464 | tf_op jit(solution)/shard_map/ppermute | solution.py:516
  277.8 12.9 %collective-permute-done.59.refs_5_ = bf16[2,384,512]{2,1,0:T(8,128)(2,1)S(1)} collective-permute-done((bf16[2,384,512]{2,1,0:T(8,128)(2,1)S(1)}, bf16[2,384,512]{2,1,0:T(8,128)(2,1)S(1)}, u32[]{:S(2)}, u32[]{:S(2)}) %collective-permute-start.59) | collective-permute-done | bytes 786464 | tf_op jit(solution)/shard_map/ppermute | solution.py:516
  (154 shorter events, 78.8 us)
Async XLA Ops:
  6.4 27.6 %collective-permute-start.22 = (bf16[128,2048]{1,0:T(8,128)(2,1)}, bf16[128,2048]{1,0:T(8,128)(2,1)S(1)}, u32[]{:S(2)}, u32[]{:S(2)}) collective-permute-start(bf16[128,2048]{1,0:T(8,128)(2,1)} %refs_0_.5), channel_id=1, source_target_pairs={{0,2},{2,4},{4,6},{6,7},{7,5},{5,3},{3,1},{1,0},{8,10},{10,12},{12... | collective-permute-start | bytes 1572872 | tf_op jit(solution)/shard_map/ppermute | solution.py:441
  8.0 22.2 %collective-permute-start.1 = (bf16[64,2176]{1,0:T(8,128)(2,1)S(1)}, bf16[64,2176]{1,0:T(8,128)(2,1)S(1)}, u32[]{:S(2)}, u32[]{:S(2)}) collective-permute-start(bf16[64,2176]{1,0:T(8,128)(2,1)S(1)} %get-tuple-element.82.refs_3_), channel_id=1, source_target_pairs={{0,2},{2,4},{4,6},{6,7},{7,5},{5,3},{3,1},{1,0},{8,10},{10,12},{12... | collective-permute-start | bytes 835592 | tf_op jit(solution)/shard_map/ppermute | solution.py:457
  9.6 22.5 %collective-permute-start.2 = (bf16[64,2176]{1,0:T(8,128)(2,1)S(1)}, bf16[64,2176]{1,0:T(8,128)(2,1)S(1)}, u32[]{:S(2)}, u32[]{:S(2)}) collective-permute-start(bf16[64,2176]{1,0:T(8,128)(2,1)S(1)} %get-tuple-element.81.refs_2_), channel_id=1, source_target_pairs={{2,0},{4,2},{6,4},{7,6},{5,7},{3,5},{1,3},{0,1},{10,8},{12,10},{14... | collective-permute-start | bytes 835592 | tf_op jit(solution)/shard_map/ppermute | solution.py:456
  10.0 23.6 %collective-permute-start.3 = (bf16[64,2176]{1,0:T(8,128)(2,1)S(1)}, bf16[64,2176]{1,0:T(8,128)(2,1)S(1)}, u32[]{:S(2)}, u32[]{:S(2)}) collective-permute-start(bf16[64,2176]{1,0:T(8,128)(2,1)S(1)} %get-tuple-element.82.refs_3_), channel_id=1, source_target_pairs={{2,0},{4,2},{6,4},{7,6},{5,7},{3,5},{1,3},{0,1},{10,8},{12,10},{14... | collective-permute-start | bytes 835592 | tf_op jit(solution)/shard_map/ppermute | solution.py:458
  13.8 33.9 %collective-permute-start.23 = (bf16[128,2048]{1,0:T(8,128)(2,1)}, bf16[128,2048]{1,0:T(8,128)(2,1)S(1)}, u32[]{:S(2)}, u32[]{:S(2)}) collective-permute-start(bf16[128,2048]{1,0:T(8,128)(2,1)} %refs_0_.5), channel_id=1, source_target_pairs={{2,0},{4,2},{6,4},{7,6},{5,7},{3,5},{1,3},{0,1},{10,8},{12,10},{14... | collective-permute-start | bytes 1572872 | tf_op jit(solution)/shard_map/ppermute | solution.py:442
  47.7 21.1 %collective-permute-start.24 = (bf16[128,2048]{1,0:T(8,128)(2,1)S(1)}, bf16[128,2048]{1,0:T(8,128)(2,1)S(1)}, u32[]{:S(2)}, u32[]{:S(2)}) collective-permute-start(bf16[128,2048]{1,0:T(8,128)(2,1)S(1)} %collective-permute-done.22.refs_1_), channel_id=1, source_target_pairs={{0,2},{2,4},{4,6},{6,7},{7,5},{5,3},{3,1},{1,0},{8,10},{10,12},{12... | collective-permute-start | bytes 1572872 | tf_op jit(solution)/shard_map/ppermute | solution.py:441
  49.5 21.1 %collective-permute-start.25 = (bf16[128,2048]{1,0:T(8,128)(2,1)S(1)}, bf16[128,2048]{1,0:T(8,128)(2,1)S(1)}, u32[]{:S(2)}, u32[]{:S(2)}) collective-permute-start(bf16[128,2048]{1,0:T(8,128)(2,1)S(1)} %collective-permute-done.23.refs_2_), channel_id=1, source_target_pairs={{2,0},{4,2},{6,4},{7,6},{5,7},{3,5},{1,3},{0,1},{10,8},{12,10},{14... | collective-permute-start | bytes 1572872 | tf_op jit(solution)/shard_map/ppermute | solution.py:442
  51.8 22.6 %collective-permute-start.10 = (bf16[64,2176]{1,0:T(8,128)(2,1)}, bf16[64,2176]{1,0:T(8,128)(2,1)}, u32[]{:S(2)}, u32[]{:S(2)}) collective-permute-start(bf16[64,2176]{1,0:T(8,128)(2,1)} %collective-permute-done.6.refs_2_), channel_id=1, source_target_pairs={{2,0},{4,2},{6,4},{7,6},{5,7},{3,5},{1,3},{0,1},{10,8},{12,10},{14... | collective-permute-start | bytes 835592 | tf_op jit(solution)/shard_map/ppermute | solution.py:456
  59.5 20.9 %collective-permute-start.13 = (bf16[64,2176]{1,0:T(8,128)(2,1)}, bf16[64,2176]{1,0:T(8,128)(2,1)}, u32[]{:S(2)}, u32[]{:S(2)}) collective-permute-start(bf16[64,2176]{1,0:T(8,128)(2,1)} %collective-permute-done.11.refs_7_), channel_id=1, source_target_pairs={{2,0},{4,2},{6,4},{7,6},{5,7},{3,5},{1,3},{0,1},{10,8},{12,10},{14... | collective-permute-start | bytes 835592 | tf_op jit(solution)/shard_map/ppermute | solution.py:461
  68.8 32.5 %collective-permute-start.26 = (bf16[128,2048]{1,0:T(8,128)(2,1)S(1)}, bf16[128,2048]{1,0:T(8,128)(2,1)S(1)}, u32[]{:S(2)}, u32[]{:S(2)}) collective-permute-start(bf16[128,2048]{1,0:T(8,128)(2,1)S(1)} %collective-permute-done.24.refs_3_), channel_id=1, source_target_pairs={{0,2},{2,4},{4,6},{6,7},{7,5},{5,3},{3,1},{1,0},{8,10},{10,12},{12... | collective-permute-start | bytes 1572872 | tf_op jit(solution)/shard_map/ppermute | solution.py:441
  70.7 31.2 %collective-permute-start.27 = (bf16[128,2048]{1,0:T(8,128)(2,1)S(1)}, bf16[128,2048]{1,0:T(8,128)(2,1)S(1)}, u32[]{:S(2)}, u32[]{:S(2)}) collective-permute-start(bf16[128,2048]{1,0:T(8,128)(2,1)S(1)} %collective-permute-done.25.refs_0_), channel_id=1, source_target_pairs={{2,0},{4,2},{6,4},{7,6},{5,7},{3,5},{1,3},{0,1},{10,8},{12,10},{14... | collective-permute-start | bytes 1572872 | tf_op jit(solution)/shard_map/ppermute | solution.py:442
  99.7 31.3 %collective-permute-start.44 = (bf16[4,160,512]{2,1,0:T(8,128)(2,1)S(1)}, bf16[4,160,512]{2,1,0:T(8,128)(2,1)S(1)}, u32[]{:S(2)}, u32[]{:S(2)}) collective-permute-start(bf16[4,160,512]{2,1,0:T(8,128)(2,1)S(1)} %get-tuple-element.142), channel_id=1, source_target_pairs={{0,24},{8,16},{16,8},{24,0},{1,25},{9,17},{17,9},{25,1},{2,26},{10... | collective-permute-start | bytes 1966088 | tf_op jit(solution)/shard_map/ppermute | solution.py:494
  99.7 32.8 %collective-permute-start.46 = (bf16[4,160,512]{2,1,0:T(8,128)(2,1)S(1)}, bf16[4,160,512]{2,1,0:T(8,128)(2,1)S(1)}, u32[]{:S(2)}, u32[]{:S(2)}) collective-permute-start(bf16[4,160,512]{2,1,0:T(8,128)(2,1)S(1)} %get-tuple-element.144), channel_id=1, source_target_pairs={{0,8},{8,0},{16,24},{24,16},{1,9},{9,1},{17,25},{25,17},{2,10},{10... | collective-permute-start | bytes 1966088 | tf_op jit(solution)/shard_map/ppermute | solution.py:494
  115.3 22.8 %collective-permute-start.48 = (bf16[4,160,512]{2,1,0:T(8,128)(2,1)S(1)}, bf16[4,160,512]{2,1,0:T(8,128)(2,1)S(1)}, u32[]{:S(2)}, u32[]{:S(2)}) collective-permute-start(bf16[4,160,512]{2,1,0:T(8,128)(2,1)S(1)} %get-tuple-element.146), channel_id=1, source_target_pairs={{0,16},{8,24},{16,0},{24,8},{1,17},{9,25},{17,1},{25,9},{2,18},{10... | collective-permute-start | bytes 1966088 | tf_op jit(solution)/shard_map/ppermute | solution.py:494
  117.1 26.3 %collective-permute-start.45 = (bf16[4,160,512]{2,1,0:T(8,128)(2,1)S(1)}, bf16[4,160,512]{2,1,0:T(8,128)(2,1)S(1)}, u32[]{:S(2)}, u32[]{:S(2)}) collective-permute-start(bf16[4,160,512]{2,1,0:T(8,128)(2,1)S(1)} %get-tuple-element.143), channel_id=1, source_target_pairs={{0,24},{8,16},{16,8},{24,0},{1,25},{9,17},{17,9},{25,1},{2,26},{10... | collective-permute-start | bytes 1966088 | tf_op jit(solution)/shard_map/ppermute | solution.py:494
  117.2 44.5 %collective-permute-start.47 = (bf16[4,160,512]{2,1,0:T(8,128)(2,1)S(1)}, bf16[4,160,512]{2,1,0:T(8,128)(2,1)S(1)}, u32[]{:S(2)}, u32[]{:S(2)}) collective-permute-start(bf16[4,160,512]{2,1,0:T(8,128)(2,1)S(1)} %get-tuple-element.145), channel_id=1, source_target_pairs={{0,8},{8,0},{16,24},{24,16},{1,9},{9,1},{17,25},{25,17},{2,10},{10... | collective-permute-start | bytes 1966088 | tf_op jit(solution)/shard_map/ppermute | solution.py:494
  130.9 20.4 %collective-permute-start.16 = (bf16[128,2048]{1,0:T(8,128)(2,1)S(1)}, bf16[128,2048]{1,0:T(8,128)(2,1)S(1)}, u32[]{:S(2)}, u32[]{:S(2)}) collective-permute-start(bf16[128,2048]{1,0:T(8,128)(2,1)S(1)} %get-tuple-element.109), channel_id=1, source_target_pairs={{0,2},{2,4},{4,6},{6,7},{7,5},{5,3},{3,1},{1,0},{8,10},{10,12},{12... | collective-permute-start | bytes 1572872 | tf_op jit(solution)/shard_map/ppermute | solution.py:401
  132.6 20.4 %collective-permute-start.17 = (bf16[128,2048]{1,0:T(8,128)(2,1)S(1)}, bf16[128,2048]{1,0:T(8,128)(2,1)S(1)}, u32[]{:S(2)}, u32[]{:S(2)}) collective-permute-start(bf16[128,2048]{1,0:T(8,128)(2,1)S(1)} %get-tuple-element.111), channel_id=1, source_target_pairs={{2,0},{4,2},{6,4},{7,6},{5,7},{3,5},{1,3},{0,1},{10,8},{12,10},{14... | collective-permute-start | bytes 1572872 | tf_op jit(solution)/shard_map/ppermute | solution.py:402
  143.4 22.6 %collective-permute-start.49 = (bf16[4,160,512]{2,1,0:T(8,128)(2,1)S(1)}, bf16[4,160,512]{2,1,0:T(8,128)(2,1)S(1)}, u32[]{:S(2)}, u32[]{:S(2)}) collective-permute-start(bf16[4,160,512]{2,1,0:T(8,128)(2,1)S(1)} %get-tuple-element.147), channel_id=1, source_target_pairs={{0,16},{8,24},{16,0},{24,8},{1,17},{9,25},{17,1},{25,9},{2,18},{10... | collective-permute-start | bytes 1966088 | tf_op jit(solution)/shard_map/ppermute | solution.py:494
  159.6 26.3 %collective-permute-start.18 = (bf16[128,2048]{1,0:T(8,128)(2,1)S(1)}, bf16[128,2048]{1,0:T(8,128)(2,1)S(1)}, u32[]{:S(2)}, u32[]{:S(2)}) collective-permute-start(bf16[128,2048]{1,0:T(8,128)(2,1)S(1)} %get-tuple-element.112), channel_id=1, source_target_pairs={{0,2},{2,4},{4,6},{6,7},{7,5},{5,3},{3,1},{1,0},{8,10},{10,12},{12... | collective-permute-start | bytes 1572872 | tf_op jit(solution)/shard_map/ppermute | solution.py:401
  163.3 23.5 %collective-permute-start.19 = (bf16[128,2048]{1,0:T(8,128)(2,1)S(1)}, bf16[128,2048]{1,0:T(8,128)(2,1)S(1)}, u32[]{:S(2)}, u32[]{:S(2)}) collective-permute-start(bf16[128,2048]{1,0:T(8,128)(2,1)S(1)} %get-tuple-element.114), channel_id=1, source_target_pairs={{2,0},{4,2},{6,4},{7,6},{5,7},{3,5},{1,3},{0,1},{10,8},{12,10},{14... | collective-permute-start | bytes 1572872 | tf_op jit(solution)/shard_map/ppermute | solution.py:402
  165.0 20.8 %collective-permute-start.39 = (bf16[64,2048]{1,0:T(8,128)(2,1)S(1)}, bf16[64,2048]{1,0:T(8,128)(2,1)S(1)}, u32[]{:S(2)}, u32[]{:S(2)}) collective-permute-start(bf16[64,2048]{1,0:T(8,128)(2,1)S(1)} %get-tuple-element.137), channel_id=1, source_target_pairs={{2,0},{4,2},{6,4},{7,6},{5,7},{3,5},{1,3},{0,1},{10,8},{12,10},{14... | collective-permute-start | bytes 786440 | tf_op jit(solution)/shard_map/ppermute | solution.py:422
  166.0 21.5 %collective-permute-start.33 = (bf16[64,2048]{1,0:T(8,128)(2,1)S(1)}, bf16[64,2048]{1,0:T(8,128)(2,1)S(1)}, u32[]{:S(2)}, u32[]{:S(2)}) collective-permute-start(bf16[64,2048]{1,0:T(8,128)(2,1)S(1)} %get-tuple-element.131), channel_id=1, source_target_pairs={{0,2},{2,4},{4,6},{6,7},{7,5},{5,3},{3,1},{1,0},{8,10},{10,12},{12... | collective-permute-start | bytes 786440 | tf_op jit(solution)/shard_map/ppermute | solution.py:419
  185.8 60.6 %collective-permute-start.56 = (bf16[2,2,384,512]{3,2,1,0:T(8,128)(2,1)S(1)}, bf16[2,2,384,512]{3,2,1,0:T(8,128)(2,1)S(1)}, u32[]{:S(2)}, u32[]{:S(2)}) collective-permute-start(bf16[2,2,384,512]{3,2,1,0:T(8,128)(2,1)S(1)} %get-tuple-element.155), channel_id=1, source_target_pairs={{0,8},{8,0},{16,24},{24,16},{1,9},{9,1},{17,25},{25,17},{2,10},{10... | collective-permute-start | bytes 4718600 | tf_op jit(solution)/shard_map/ppermute | solution.py:515
  185.9 61.9 %collective-permute-start.58 = (bf16[2,2,384,512]{3,2,1,0:T(8,128)(2,1)S(1)}, bf16[2,2,384,512]{3,2,1,0:T(8,128)(2,1)S(1)}, u32[]{:S(2)}, u32[]{:S(2)}) collective-permute-start(bf16[2,2,384,512]{3,2,1,0:T(8,128)(2,1)S(1)} %get-tuple-element.157), channel_id=1, source_target_pairs={{0,8},{8,0},{16,24},{24,16},{1,9},{9,1},{17,25},{25,17},{2,10},{10... | collective-permute-start | bytes 4718600 | tf_op jit(solution)/shard_map/ppermute | solution.py:515
  188.9 24.6 %collective-permute-start.50 = (bf16[2,320,768]{2,1,0:T(8,128)(2,1)S(1)}, bf16[2,320,768]{2,1,0:T(8,128)(2,1)S(1)}, u32[]{:S(2)}, u32[]{:S(2)}) collective-permute-start(bf16[2,320,768]{2,1,0:T(8,128)(2,1)S(1)} %get-tuple-element.150.refs_11_), channel_id=1, source_target_pairs={{0,16},{8,24},{16,0},{24,8},{1,17},{9,25},{17,1},{25,9},{2,18},{10... | collective-permute-start | bytes 2949128 | tf_op jit(solution)/shard_map/ppermute | solution.py:510
  195.2 38.0 %collective-permute-start.53 = (bf16[2,320,768]{2,1,0:T(8,128)(2,1)S(1)}, bf16[2,320,768]{2,1,0:T(8,128)(2,1)S(1)}, u32[]{:S(2)}, u32[]{:S(2)}) collective-permute-start(bf16[2,320,768]{2,1,0:T(8,128)(2,1)S(1)} %get-tuple-element.151.refs_11_), channel_id=1, source_target_pairs={{0,16},{8,24},{16,0},{24,8},{1,17},{9,25},{17,1},{25,9},{2,18},{10... | collective-permute-start | bytes 2949128 | tf_op jit(solution)/shard_map/ppermute | solution.py:510
  195.7 39.5 %collective-permute-start.55 = (bf16[2,320,768]{2,1,0:T(8,128)(2,1)S(1)}, bf16[2,320,768]{2,1,0:T(8,128)(2,1)S(1)}, u32[]{:S(2)}, u32[]{:S(2)}) collective-permute-start(bf16[2,320,768]{2,1,0:T(8,128)(2,1)S(1)} %get-tuple-element.151.refs_11_), channel_id=1, source_target_pairs={{0,8},{8,0},{16,24},{24,16},{1,9},{9,1},{17,25},{25,17},{2,10},{10... | collective-permute-start | bytes 2949128 | tf_op jit(solution)/shard_map/ppermute | solution.py:511
  213.6 22.2 %collective-permute-start.35 = (bf16[64,2048]{1,0:T(8,128)(2,1)S(1)}, bf16[64,2048]{1,0:T(8,128)(2,1)S(1)}, u32[]{:S(2)}, u32[]{:S(2)}) collective-permute-start(bf16[64,2048]{1,0:T(8,128)(2,1)S(1)} %get-tuple-element.133), channel_id=1, source_target_pairs={{0,2},{2,4},{4,6},{6,7},{7,5},{5,3},{3,1},{1,0},{8,10},{10,12},{12... | collective-permute-start | bytes 786440 | tf_op jit(solution)/shard_map/ppermute | solution.py:419
  242.9 22.2 %collective-permute-start.52 = (bf16[2,320,768]{2,1,0:T(8,128)(2,1)S(1)}, bf16[2,320,768]{2,1,0:T(8,128)(2,1)S(1)}, u32[]{:S(2)}, u32[]{:S(2)}) collective-permute-start(bf16[2,320,768]{2,1,0:T(8,128)(2,1)S(1)} %get-tuple-element.150.refs_11_), channel_id=1, source_target_pairs={{0,8},{8,0},{16,24},{24,16},{1,9},{9,1},{17,25},{25,17},{2,10},{10... | collective-permute-start | bytes 2949128 | tf_op jit(solution)/shard_map/ppermute | solution.py:511
  257.3 20.4 %collective-permute-start.57 = (bf16[2,384,512]{2,1,0:T(8,128)(2,1)S(1)}, bf16[2,384,512]{2,1,0:T(8,128)(2,1)S(1)}, u32[]{:S(2)}, u32[]{:S(2)}) collective-permute-start(bf16[2,384,512]{2,1,0:T(8,128)(2,1)S(1)} %fusion), channel_id=1, source_target_pairs={{0,16},{8,24},{16,0},{24,8},{1,17},{9,25},{17,1},{25,9},{2,18},{10... | collective-permute-start | bytes 2359304 | tf_op jit(solution)/shard_map/ppermute | solution.py:516
  257.8 32.8 %collective-permute-start.59 = (bf16[2,384,512]{2,1,0:T(8,128)(2,1)S(1)}, bf16[2,384,512]{2,1,0:T(8,128)(2,1)S(1)}, u32[]{:S(2)}, u32[]{:S(2)}) collective-permute-start(bf16[2,384,512]{2,1,0:T(8,128)(2,1)S(1)} %fusion.1), channel_id=1, source_target_pairs={{0,16},{8,24},{16,0},{24,8},{1,17},{9,25},{17,1},{25,9},{2,18},{10... | collective-permute-start | bytes 2359304 | tf_op jit(solution)/shard_map/ppermute | solution.py:516
  (43 other events, 787.8 us)

commit v4 on v3

--- a/solution.py
+++ b/solution.py
@@ -50,7 +50,7 @@
 def pack_rows(tokens, expert_ids, gate_fixed):
     rows, width = tokens.shape
     top, half = expert_ids.shape[1], rows // 2
-    expert_ids, gate_fixed = expert_ids.T, gate_fixed.T
+    tokens, expert_ids, gate_fixed = in_hbm(tokens), in_hbm(expert_ids.T), in_hbm(gate_fixed.T)
 
     def kernel(x_ref, ids_ref, gate_ref, low_ref, high_ref):
         lane = lax.broadcasted_iota(jnp.int32, (top, LANES), 1)
@@ -280,15 +280,12 @@
     )(order, *ds, *acts)
 
 
-def finish(pieces):
-    arrays = [a for piece in pieces for a in piece]
-    here, hidden, part = pieces[0][2].shape
-    shape = jax.ShapeDtypeStruct((here * len(pieces), hidden, part), BF16)
-
-    def kernel(*refs):
-        for i in range(len(pieces)):
-            keep, got, away = refs[3 * i : 3 * i + 3]
-            refs[-1][i * here : (i + 1) * here] = narrow(wide(keep[0]) + wide(got[0]) + wide(away[...]))
+def finish(piece, index, slots, into):
+    here, hidden, part = piece[2].shape
+    shape = jax.ShapeDtypeStruct((slots, hidden, part), BF16)
+
+    def kernel(keep, got, away, *refs):
+        refs[-1][...] = narrow(wide(keep[0]) + wide(got[0]) + wide(away[...]))
 
     own = pl.BlockSpec((1, here, hidden, part), lambda *_: (1, 0, 0, 0))
     return call(
@@ -296,10 +293,11 @@
         3 * here * hidden * part,
         8 * here * hidden * part,
         grid=(1,),
-        in_specs=[own, own, full(pieces[0][2])] * len(pieces),
-        out_specs=full(shape),
+        in_specs=[own, own, full(piece[2])] + ([] if into is None else [pl.BlockSpec(memory_space=pl.ANY)]),
+        out_specs=pl.BlockSpec((here, hidden, part), lambda *_: (index, 0, 0)),
         out_shape=shape,
-    )(*arrays)
+        input_output_aliases={} if into is None else {3: 0},
+    )(*piece, *([] if into is None else [into]))
 
 
 def in_gradients(xs, d_pres, first, last, into):
@@ -515,7 +513,9 @@
         got = lax.ppermute(give, "dp", core_pairs)
         away = lax.ppermute(narrow(wide(keep[0]) + wide(got[0])), "dp", chip_pairs)
         grads.append((keep, got, away))
-    grad_out = finish(grads)
+    grad_out = None
+    for i, piece in enumerate(grads):
+        grad_out = finish(piece, i, slots, grad_out)
     rows_by_group = [columns[i][j] for j in range(parts) for i in range(2)]
     grad_in = None
     for low, d_lean in zip(lows, leans):

time: 293 us -> 281 us (0.959)
  waiting for transfers between devices: 159 us -> 145 us
  starting transfers between devices: 60.9 us -> 64.4 us
    ppermute x4, waiting for transfers between devices: 0.01 us -> 10.2 us  [ring_scatter(): g = lax.ppermute(g, 'expert', back)]
    ppermute x2, waiting for transfers between devices: 22.2 us -> 12.7 us  [body(): away = lax.ppermute(narrow(wide(keep[0]) + wide(got[0])), 'dp', chip_pairs)]
    ppermute x4, waiting for transfers between devices: 9.15 us -> 0.01 us  [ring_scatter(): f = lax.ppermute(f, 'expert', ahead)]
    ppermute x3, waiting for transfers between devices: 8.71 us -> 0.01 us  [ring_gather(): f = lax.ppermute(f, 'expert', ahead)]
    ppermute x3, waiting for transfers between devices: 10.8 us -> 18.6 us  [ring_gather_halves(): lf = lax.ppermute(lf, 'expert', ahead)]
    ppermute x6, waiting for transfers between devices: 3.68 us -> 8.59 us  [body(): lax.ppermute(cols[j], 'dp', routes[j])]
    ppermute x1, waiting for transfers between devices: 5.39 us -> 1.55 us  [ring_gather_halves(): high = lax.ppermute(hg, 'expert', back)]
    ppermute x3, waiting for transfers between devices: 3.47 us -> 0.01 us  [ring_gather_halves(): lg = lax.ppermute(lg, 'expert', back)]
  transfers between devices with their start and end apart: 60 -> 60, of which waited for: 23 -> 23; matrix products, arithmetic and copies ran while one was open for 0% -> 0% of each run, Pallas kernels for 22% -> 24%
where the time goes in v4:
time: 281 us
  waiting for transfers between devices  145 us (52%)
  Pallas kernels  68.8 us (24%)
  starting transfers between devices  64.4 us (23%)
    ppermute x2, waiting for transfers between devices, body(): across = lax.ppermute(mine, 'dp', chip_pairs)  35.8 us
    ppermute x3, waiting for transfers between devices, ring_gather_halves(): hf = lax.ppermute(hf, 'expert', ahead)  21 us
    pallas_call x2, Pallas kernels, forward(): call(kernel, 2 * slots * total * width * (both + hidden), 2 * slots * wid...  20.1 us
    ppermute x3, waiting for transfers between devices, ring_gather_halves(): lf = lax.ppermute(lf, 'expert', ahead)  18.6 us
    ppermute x3, waiting for transfers between devices, ring_scatter_halves(): hf = None if hf is None else lax.ppermute(hf, 'expert', ahead)  16.8 us
    ppermute x2, waiting for transfers between devices, body(): away = lax.ppermute(narrow(wide(keep[0]) + wide(got[0])), 'dp', chip_pairs)  12.7 us
    ppermute x4, waiting for transfers between devices, ring_scatter(): g = lax.ppermute(g, 'expert', back)  10.2 us
    pallas_call x2, Pallas kernels, rows_back(): call(kernel, 2 * total * width * here * both, 2 * width * here * (total +...  9.53 us
  transfers between devices with their start and end apart: 60, of which 23 were waited for; matrix products, arithmetic and copies ran while one was open for 0% of the time, Pallas kernels for 24%

profile of v4, /device:TPU:0, one launch (start us, length us, event | category | flops | bytes accessed | tf_op | source)
XLA Modules:
  0.0 280.7 jit_solution(2370475183821147109)
XLA Ops:
  2.0 3.1 %collective-permute-start = (bf16[64,2176]{1,0:T(8,128)(2,1)S(1)}, bf16[64,2176]{1,0:T(8,128)(2,1)S(1)}, u32[]{:S(2)}, u32[]{:S(2)}) collective-permute-start(bf16[64,2176]{1,0:T(8,128)(2,1)S(1)} %get-tuple-element.81.refs_2_), channel_id=1, source_target_pairs={{0,2},{2,4},{4,6},{6,7},{7,5},{5,3},{3,1},{1,0},{8,10},{10,12},{12... | collective-permute-start | bytes 835592 | tf_op jit(solution)/shard_map/ppermute | solution.py:453
  9.1 3.4 %collective-permute-done.refs_4_ = bf16[64,2176]{1,0:T(8,128)(2,1)S(1)} collective-permute-done((bf16[64,2176]{1,0:T(8,128)(2,1)S(1)}, bf16[64,2176]{1,0:T(8,128)(2,1)S(1)}, u32[]{:S(2)}, u32[]{:S(2)}) %collective-permute-start) | collective-permute-done | bytes 278560 | tf_op jit(solution)/shard_map/ppermute | solution.py:453
  12.5 2.0 collective-permute-start.3
  14.5 14.3 %collective-permute-done.1.refs_5_ = bf16[64,2176]{1,0:T(8,128)(2,1)S(1)} collective-permute-done((bf16[64,2176]{1,0:T(8,128)(2,1)S(1)}, bf16[64,2176]{1,0:T(8,128)(2,1)S(1)}, u32[]{:S(2)}, u32[]{:S(2)}) %collective-permute-start.1) | collective-permute-done | bytes 278560 | tf_op jit(solution)/shard_map/ppermute | solution.py:455
  35.7 2.7 collective-permute-done.4.refs_8_
  40.1 4.2 %collective-permute-done.5.refs_9_ = bf16[64,2176]{1,0:T(8,128)(2,1)S(1)} collective-permute-done((bf16[64,2176]{1,0:T(8,128)(2,1)S(1)}, bf16[64,2176]{1,0:T(8,128)(2,1)S(1)}, u32[]{:S(2)}, u32[]{:S(2)}) %collective-permute-start.5) | collective-permute-done | bytes 278560 | tf_op jit(solution)/shard_map/ppermute | solution.py:455
  49.2 12.5 %collective-permute-done.8.refs_4_ = bf16[64,2176]{1,0:T(8,128)(2,1)} collective-permute-done((bf16[64,2176]{1,0:T(8,128)(2,1)S(1)}, bf16[64,2176]{1,0:T(8,128)(2,1)}, u32[]{:S(2)}, u32[]{:S(2)}) %collective-permute-start.8) | collective-permute-done | bytes 278560 | tf_op jit(solution)/shard_map/ppermute | solution.py:453
  63.4 2.4 collective-permute-done.9.refs_5_
  70.7 3.3 %shard_map.103 = (bf16[4,48,2048]{2,1,0:T(8,128)(2,1)S(1)}, bf16[192,128]{1,0:T(8,128)(2,1)S(1)}, f32[4,48,128]{2,1,0:T(8,128)S(1)}, bf16[4,48,2048]{2,1,0:T(8,1...) custom-call(s32[32]{0:T(128)S(1)} %copy-done.3, ...), custom_call_target="tpu_custom_call" | custom-call | flops 402653184 | bytes 8388608 | tf_op jit(solution)/shard_map/pallas_call | solution.py:135
  77.2 3.3 %shard_map.105 = (bf16[4,48,2048]{2,1,0:T(8,128)(2,1)S(1)}, bf16[192,128]{1,0:T(8,128)(2,1)S(1)}, f32[4,48,128]{2,1,0:T(8,128)S(1)}, bf16[4,48,2048]{2,1,0:T(8,1...) custom-call(s32[32]{0:T(128)S(1)} %copy-done.4, ...), custom_call_target="tpu_custom_call" | custom-call | flops 402653184 | bytes 8388608 | tf_op jit(solution)/shard_map/pallas_call | solution.py:135
  80.5 10.0 %shard_map.106 = (bf16[4,4,48,2048]{3,2,1,0:T(8,128)(2,1)S(1)}, bf16[4,192,384]{2,1,0:T(8,128)(2,1)S(1)}, f32[4,192,768]{2,1,0:T(8,128)S(1)}) custom-call(bf16[4,48,2048]{2,1,0:T(8,128)(2,1)S(1)} %get-tuple-element.94.refs_0_, bf16[4,48,2048]{2,1,0:T(8,128)(2,1)S(1)} %get-tuple-element.95.refs_1_, bf16[4,48,2048]{2,1,0:T(8,128)(2,1)S(1)} %get-tuple-element.96.refs_2_, ...), custom_call_target="tpu_custom_call" | custom-call | flops 3623878656 | bytes 25165824 | tf_op jit(solution)/shard_map/pallas_call | solution.py:200
  95.2 10.1 %shard_map.104 = (bf16[4,4,48,2048]{3,2,1,0:T(8,128)(2,1)S(1)}, bf16[4,192,384]{2,1,0:T(8,128)(2,1)S(1)}, f32[4,192,768]{2,1,0:T(8,128)S(1)}) custom-call(bf16[4,48,2048]{2,1,0:T(8,128)(2,1)S(1)} %get-tuple-element.83.refs_0_, bf16[4,48,2048]{2,1,0:T(8,128)(2,1)S(1)} %get-tuple-element.84.refs_1_, bf16[4,48,2048]{2,1,0:T(8,128)(2,1)S(1)} %get-tuple-element.85.refs_2_, ...), custom_call_target="tpu_custom_call" | custom-call | flops 3623878656 | bytes 25165824 | tf_op jit(solution)/shard_map/pallas_call | solution.py:200
  111.6 3.5 %shard_map.115 = (bf16[2,384,768]{2,1,0:T(8,128)(2,1)S(1)}, bf16[2,320,768]{2,1,0:T(8,128)(2,1)S(1)}) custom-call(bf16[4,48,2048]{2,1,0:T(8,128)(2,1)S(1)} %get-tuple-element.117.refs_0_.refs_1_, bf16[4,48,2048]{2,1,0:T(8,128)(2,1)S(1)} %get-tuple-element.118.refs_1_.refs_2_, bf16[4,48,2048]{2,1,0:T(8,128)(2,1)S(1)} %get-tuple-element.119.refs_2_.refs_3_, ...), custom_call_target="tpu_custom_call" | custom-call | flops 1207959552 | bytes 6291456 | tf_op jit(solution)/shard_map/pallas_call | solution.py:233
  115.1 4.8 %shard_map.116.refs_0_.refs_4_.refs_3_ = bf16[2,8,48,2048]{3,2,1,0:T(8,128)(2,1)S(1)} custom-call(bf16[2,384,768]{2,1,0:T(8,128)(2,1)S(1)} %get-tuple-element.126.d_ref, bf16[4,2048,768]{2,1,0:T(8,128)(2,1)} %w_ref.3), custom_call_target="tpu_custom_call" | custom-call | flops 2415919104 | bytes 9437184 | tf_op jit(solution)/shard_map/pallas_call | solution.py:335
  119.9 3.5 %shard_map.117 = (bf16[2,384,768]{2,1,0:T(8,128)(2,1)S(1)}, bf16[2,320,768]{2,1,0:T(8,128)(2,1)S(1)}) custom-call(bf16[4,48,2048]{2,1,0:T(8,128)(2,1)S(1)} %get-tuple-element.117.refs_0_.refs_1_, bf16[4,48,2048]{2,1,0:T(8,128)(2,1)S(1)} %get-tuple-element.118.refs_1_.refs_2_, bf16[4,48,2048]{2,1,0:T(8,128)(2,1)S(1)} %get-tuple-element.119.refs_2_.refs_3_, ...), custom_call_target="tpu_custom_call" | custom-call | flops 1207959552 | bytes 6291456 | tf_op jit(solution)/shard_map/pallas_call | solution.py:233
  123.3 4.8 %shard_map.118.refs_1_.refs_5_.refs_4_ = bf16[2,8,48,2048]{3,2,1,0:T(8,128)(2,1)S(1)} custom-call(bf16[2,384,768]{2,1,0:T(8,128)(2,1)S(1)} %get-tuple-element.127.d_ref, bf16[4,2048,768]{2,1,0:T(8,128)(2,1)} %w_ref.3), custom_call_target="tpu_custom_call" | custom-call | flops 2415919104 | bytes 9437184 | tf_op jit(solution)/shard_map/pallas_call | solution.py:335
  130.1 6.2 %collective-permute-done.30.refs_3_ = bf16[64,2048]{1,0:T(8,128)(2,1)S(1)} collective-permute-done((bf16[64,2048]{1,0:T(8,128)(2,1)S(1)}, bf16[64,2048]{1,0:T(8,128)(2,1)S(1)}, u32[]{:S(2)}, u32[]{:S(2)}) %collective-permute-start.30) | collective-permute-done | bytes 262176 | tf_op jit(solution)/shard_map/ppermute | solution.py:417
  140.4 5.1 %collective-permute-done.37.refs_6_ = bf16[64,2048]{1,0:T(8,128)(2,1)S(1)} collective-permute-done((bf16[64,2048]{1,0:T(8,128)(2,1)S(1)}, bf16[64,2048]{1,0:T(8,128)(2,1)S(1)}, u32[]{:S(2)}, u32[]{:S(2)}) %collective-permute-start.37) | collective-permute-done | bytes 262176 | tf_op jit(solution)/shard_map/ppermute | solution.py:420
  150.5 4.3 %collective-permute-done.38.refs_3_ = bf16[64,2048]{1,0:T(8,128)(2,1)S(1)} collective-permute-done((bf16[64,2048]{1,0:T(8,128)(2,1)S(1)}, bf16[64,2048]{1,0:T(8,128)(2,1)S(1)}, u32[]{:S(2)}, u32[]{:S(2)}) %collective-permute-start.38) | collective-permute-done | bytes 262176 | tf_op jit(solution)/shard_map/ppermute | solution.py:419
  154.8 2.5 collective-permute-start.18
  158.2 2.1 collective-permute-start.33
  160.3 8.6 %collective-permute-done.49.refs_5_ = bf16[4,160,512]{2,1,0:T(8,128)(2,1)S(1)} collective-permute-done((bf16[4,160,512]{2,1,0:T(8,128)(2,1)S(1)}, bf16[4,160,512]{2,1,0:T(8,128)(2,1)S(1)}, u32[]{:S(2)}, u32[]{:S(2)}) %collective-permute-start.49) | collective-permute-done | bytes 655392 | tf_op jit(solution)/shard_map/ppermute | solution.py:492
  170.1 3.0 %shard_map.130 = (bf16[2,2,384,512]{3,2,1,0:T(8,128)(2,1)S(1)}, bf16[2,2,384,512]{3,2,1,0:T(8,128)(2,1)S(1)}) custom-call(s32[4]{0:T(128)S(1)} %pad_add_fusion.refs_0_, bf16[4,48,2048]{2,1,0:T(8,128)(2,1)S(1)} %get-tuple-element.117.refs_0_.refs_1_, bf16[4,48,2048]{2,1,0:T(8,128)(2,1)S(1)} %get-tuple-element.118.refs_1_.refs_2_, ...), custom_call_target="tpu_custom_call" | custom-call | flops 1207959552 | bytes 6291456 | tf_op jit(solution)/shard_map/pallas_call | solution.py:267
  178.2 3.0 %shard_map.129 = (bf16[2,2,384,512]{3,2,1,0:T(8,128)(2,1)S(1)}, bf16[2,2,384,512]{3,2,1,0:T(8,128)(2,1)S(1)}) custom-call(s32[4]{0:T(128)S(1)} %pad_add_fusion.refs_0_, bf16[4,48,2048]{2,1,0:T(8,128)(2,1)S(1)} %get-tuple-element.117.refs_0_.refs_1_, bf16[4,48,2048]{2,1,0:T(8,128)(2,1)S(1)} %get-tuple-element.118.refs_1_.refs_2_, ...), custom_call_target="tpu_custom_call" | custom-call | flops 1207959552 | bytes 6291456 | tf_op jit(solution)/shard_map/pallas_call | solution.py:267
  182.8 16.8 %collective-permute-done.50.refs_10_ = bf16[2,320,768]{2,1,0:T(8,128)(2,1)S(1)} collective-permute-done((bf16[2,320,768]{2,1,0:T(8,128)(2,1)S(1)}, bf16[2,320,768]{2,1,0:T(8,128)(2,1)S(1)}, u32[]{:S(2)}, u32[]{:S(2)}) %collective-permute-start.50) | collective-permute-done | bytes 983072 | tf_op jit(solution)/shard_map/ppermute | solution.py:508
  200.7 19.1 %collective-permute-done.53.refs_10_ = bf16[2,320,768]{2,1,0:T(8,128)(2,1)S(1)} collective-permute-done((bf16[2,320,768]{2,1,0:T(8,128)(2,1)S(1)}, bf16[2,320,768]{2,1,0:T(8,128)(2,1)S(1)}, u32[]{:S(2)}, u32[]{:S(2)}) %collective-permute-start.53) | collective-permute-done | bytes 983072 | tf_op jit(solution)/shard_map/ppermute | solution.py:508
  224.0 3.2 %collective-permute-done.36.refs_4_ = bf16[64,2048]{1,0:T(8,128)(2,1)S(1)} collective-permute-done((bf16[64,2048]{1,0:T(8,128)(2,1)S(1)}, bf16[64,2048]{1,0:T(8,128)(2,1)S(1)}, u32[]{:S(2)}, u32[]{:S(2)}) %collective-permute-start.36) | collective-permute-done | bytes 262176 | tf_op jit(solution)/shard_map/ppermute | solution.py:418
  228.8 11.5 %collective-permute-done.42.refs_5_ = bf16[64,2048]{1,0:T(8,128)(2,1)S(1)} collective-permute-done((bf16[64,2048]{1,0:T(8,128)(2,1)S(1)}, bf16[64,2048]{1,0:T(8,128)(2,1)S(1)}, u32[]{:S(2)}, u32[]{:S(2)}) %collective-permute-start.42) | collective-permute-done | bytes 262176 | tf_op jit(solution)/shard_map/ppermute | solution.py:419
  244.7 10.2 %collective-permute-done.21.refs_3_ = bf16[128,2048]{1,0:T(8,128)(2,1)S(1)} collective-permute-done((bf16[128,2048]{1,0:T(8,128)(2,1)S(1)}, bf16[128,2048]{1,0:T(8,128)(2,1)S(1)}, u32[]{:S(2)}, u32[]{:S(2)}) %collective-permute-start.21) | collective-permute-done | bytes 524320 | tf_op jit(solution)/shard_map/ppermute | solution.py:405
  259.0 3.4 %shard_map.127.refs_12_ = bf16[4,512,768]{2,1,0:T(8,128)(2,1)} custom-call(bf16[4,160,512]{2,1,0:T(8,128)(2,1)S(1)} %collective-permute-done.44.refs_0_, bf16[4,160,512]{2,1,0:T(8,128)(2,1)S(1)} %collective-permute-done.45.refs_1_, bf16[4,160,512]{2,1,0:T(8,128)(2,1)S(1)} %collective-permute-done.46.refs_2_, ...), custom_call_target="tpu_custom_call" | custom-call | flops 2013265920 | bytes 6553600 | tf_op jit(solution)/shard_map/pallas_call | solution.py:314
  262.3 3.4 %shard_map.128 = bf16[4,512,768]{2,1,0:T(8,128)(2,1)} custom-call(bf16[4,160,512]{2,1,0:T(8,128)(2,1)S(1)} %collective-permute-done.44.refs_0_, bf16[4,160,512]{2,1,0:T(8,128)(2,1)S(1)} %collective-permute-done.45.refs_1_, bf16[4,160,512]{2,1,0:T(8,128)(2,1)S(1)} %collective-permute-done.46.refs_2_, ...), custom_call_target="tpu_custom_call", output_to_operand_aliasing={{}: (12, {})} | custom-call | flops 2013265920 | bytes 6553600 | tf_op jit(solution)/shard_map/pallas_call | solution.py:314
  266.9 12.7 %collective-permute-done.57.away = bf16[2,384,512]{2,1,0:T(8,128)(2,1)S(1)} collective-permute-done((bf16[2,384,512]{2,1,0:T(8,128)(2,1)S(1)}, bf16[2,384,512]{2,1,0:T(8,128)(2,1)S(1)}, u32[]{:S(2)}, u32[]{:S(2)}) %collective-permute-start.57) | collective-permute-done | bytes 786464 | tf_op jit(solution)/shard_map/ppermute | solution.py:514
  (151 shorter events, 76.8 us)
Async XLA Ops:
  5.1 28.6 %collective-permute-start.22 = (bf16[128,2048]{1,0:T(8,128)(2,1)}, bf16[128,2048]{1,0:T(8,128)(2,1)S(1)}, u32[]{:S(2)}, u32[]{:S(2)}) collective-permute-start(bf16[128,2048]{1,0:T(8,128)(2,1)} %refs_0_.5), channel_id=1, source_target_pairs={{0,2},{2,4},{4,6},{6,7},{7,5},{5,3},{3,1},{1,0},{8,10},{10,12},{12... | collective-permute-start | bytes 1572872 | tf_op jit(solution)/shard_map/ppermute | solution.py:439
  6.7 22.2 %collective-permute-start.1 = (bf16[64,2176]{1,0:T(8,128)(2,1)S(1)}, bf16[64,2176]{1,0:T(8,128)(2,1)S(1)}, u32[]{:S(2)}, u32[]{:S(2)}) collective-permute-start(bf16[64,2176]{1,0:T(8,128)(2,1)S(1)} %get-tuple-element.82.refs_3_), channel_id=1, source_target_pairs={{0,2},{2,4},{4,6},{6,7},{7,5},{5,3},{3,1},{1,0},{8,10},{10,12},{12... | collective-permute-start | bytes 835592 | tf_op jit(solution)/shard_map/ppermute | solution.py:455
  8.2 25.9 %collective-permute-start.23 = (bf16[128,2048]{1,0:T(8,128)(2,1)}, bf16[128,2048]{1,0:T(8,128)(2,1)S(1)}, u32[]{:S(2)}, u32[]{:S(2)}) collective-permute-start(bf16[128,2048]{1,0:T(8,128)(2,1)} %refs_0_.5), channel_id=1, source_target_pairs={{2,0},{4,2},{6,4},{7,6},{5,7},{3,5},{1,3},{0,1},{10,8},{12,10},{14... | collective-permute-start | bytes 1572872 | tf_op jit(solution)/shard_map/ppermute | solution.py:440
  8.7 22.0 %collective-permute-start.2 = (bf16[64,2176]{1,0:T(8,128)(2,1)S(1)}, bf16[64,2176]{1,0:T(8,128)(2,1)S(1)}, u32[]{:S(2)}, u32[]{:S(2)}) collective-permute-start(bf16[64,2176]{1,0:T(8,128)(2,1)S(1)} %get-tuple-element.81.refs_2_), channel_id=1, source_target_pairs={{2,0},{4,2},{6,4},{7,6},{5,7},{3,5},{1,3},{0,1},{10,8},{12,10},{14... | collective-permute-start | bytes 835592 | tf_op jit(solution)/shard_map/ppermute | solution.py:454
  12.5 20.7 %collective-permute-start.3 = (bf16[64,2176]{1,0:T(8,128)(2,1)S(1)}, bf16[64,2176]{1,0:T(8,128)(2,1)S(1)}, u32[]{:S(2)}, u32[]{:S(2)}) collective-permute-start(bf16[64,2176]{1,0:T(8,128)(2,1)S(1)} %get-tuple-element.82.refs_3_), channel_id=1, source_target_pairs={{2,0},{4,2},{6,4},{7,6},{5,7},{3,5},{1,3},{0,1},{10,8},{12,10},{14... | collective-permute-start | bytes 835592 | tf_op jit(solution)/shard_map/ppermute | solution.py:456
  34.1 33.7 %collective-permute-start.24 = (bf16[128,2048]{1,0:T(8,128)(2,1)S(1)}, bf16[128,2048]{1,0:T(8,128)(2,1)S(1)}, u32[]{:S(2)}, u32[]{:S(2)}) collective-permute-start(bf16[128,2048]{1,0:T(8,128)(2,1)S(1)} %collective-permute-done.22.refs_1_), channel_id=1, source_target_pairs={{0,2},{2,4},{4,6},{6,7},{7,5},{5,3},{3,1},{1,0},{8,10},{10,12},{12... | collective-permute-start | bytes 1572872 | tf_op jit(solution)/shard_map/ppermute | solution.py:439
  38.4 31.0 %collective-permute-start.25 = (bf16[128,2048]{1,0:T(8,128)(2,1)S(1)}, bf16[128,2048]{1,0:T(8,128)(2,1)S(1)}, u32[]{:S(2)}, u32[]{:S(2)}) collective-permute-start(bf16[128,2048]{1,0:T(8,128)(2,1)S(1)} %collective-permute-done.23.refs_2_), channel_id=1, source_target_pairs={{2,0},{4,2},{6,4},{7,6},{5,7},{3,5},{1,3},{0,1},{10,8},{12,10},{14... | collective-permute-start | bytes 1572872 | tf_op jit(solution)/shard_map/ppermute | solution.py:440
  46.2 19.6 %collective-permute-start.9 = (bf16[64,2176]{1,0:T(8,128)(2,1)S(1)}, bf16[64,2176]{1,0:T(8,128)(2,1)S(1)}, u32[]{:S(2)}, u32[]{:S(2)}) collective-permute-start(bf16[64,2176]{1,0:T(8,128)(2,1)S(1)} %collective-permute-done.5.refs_9_), channel_id=1, source_target_pairs={{0,2},{2,4},{4,6},{6,7},{7,5},{5,3},{3,1},{1,0},{8,10},{10,12},{12... | collective-permute-start | bytes 835592 | tf_op jit(solution)/shard_map/ppermute | solution.py:455
  48.7 18.7 %collective-permute-start.11 = (bf16[64,2176]{1,0:T(8,128)(2,1)S(1)}, bf16[64,2176]{1,0:T(8,128)(2,1)}, u32[]{:S(2)}, u32[]{:S(2)}) collective-permute-start(bf16[64,2176]{1,0:T(8,128)(2,1)S(1)} %collective-permute-done.7.refs_3_), channel_id=1, source_target_pairs={{2,0},{4,2},{6,4},{7,6},{5,7},{3,5},{1,3},{0,1},{10,8},{12,10},{14... | collective-permute-start | bytes 835592 | tf_op jit(solution)/shard_map/ppermute | solution.py:456
  67.9 25.1 %collective-permute-start.26 = (bf16[128,2048]{1,0:T(8,128)(2,1)S(1)}, bf16[128,2048]{1,0:T(8,128)(2,1)S(1)}, u32[]{:S(2)}, u32[]{:S(2)}) collective-permute-start(bf16[128,2048]{1,0:T(8,128)(2,1)S(1)} %collective-permute-done.24.refs_3_), channel_id=1, source_target_pairs={{0,2},{2,4},{4,6},{6,7},{7,5},{5,3},{3,1},{1,0},{8,10},{10,12},{12... | collective-permute-start | bytes 1572872 | tf_op jit(solution)/shard_map/ppermute | solution.py:439
  69.4 25.2 %collective-permute-start.27 = (bf16[128,2048]{1,0:T(8,128)(2,1)S(1)}, bf16[128,2048]{1,0:T(8,128)(2,1)S(1)}, u32[]{:S(2)}, u32[]{:S(2)}) collective-permute-start(bf16[128,2048]{1,0:T(8,128)(2,1)S(1)} %collective-permute-done.25.refs_0_), channel_id=1, source_target_pairs={{2,0},{4,2},{6,4},{7,6},{5,7},{3,5},{1,3},{0,1},{10,8},{12,10},{14... | collective-permute-start | bytes 1572872 | tf_op jit(solution)/shard_map/ppermute | solution.py:440
  74.1 54.4 %collective-permute-start.44 = (bf16[4,160,512]{2,1,0:T(8,128)(2,1)S(1)}, bf16[4,160,512]{2,1,0:T(8,128)(2,1)S(1)}, u32[]{:S(2)}, u32[]{:S(2)}) collective-permute-start(bf16[4,160,512]{2,1,0:T(8,128)(2,1)S(1)} %get-tuple-element.142), channel_id=1, source_target_pairs={{0,24},{8,16},{16,8},{24,0},{1,25},{9,17},{17,9},{25,1},{2,26},{10... | collective-permute-start | bytes 1966088 | tf_op jit(solution)/shard_map/ppermute | solution.py:492
  106.3 31.4 %collective-permute-start.46 = (bf16[4,160,512]{2,1,0:T(8,128)(2,1)S(1)}, bf16[4,160,512]{2,1,0:T(8,128)(2,1)S(1)}, u32[]{:S(2)}, u32[]{:S(2)}) collective-permute-start(bf16[4,160,512]{2,1,0:T(8,128)(2,1)S(1)} %get-tuple-element.144), channel_id=1, source_target_pairs={{0,8},{8,0},{16,24},{24,16},{1,9},{9,1},{17,25},{25,17},{2,10},{10... | collective-permute-start | bytes 1966088 | tf_op jit(solution)/shard_map/ppermute | solution.py:492
  106.3 32.5 %collective-permute-start.48 = (bf16[4,160,512]{2,1,0:T(8,128)(2,1)S(1)}, bf16[4,160,512]{2,1,0:T(8,128)(2,1)S(1)}, u32[]{:S(2)}, u32[]{:S(2)}) collective-permute-start(bf16[4,160,512]{2,1,0:T(8,128)(2,1)S(1)} %get-tuple-element.146), channel_id=1, source_target_pairs={{0,16},{8,24},{16,0},{24,8},{1,17},{9,25},{17,1},{25,9},{2,18},{10... | collective-permute-start | bytes 1966088 | tf_op jit(solution)/shard_map/ppermute | solution.py:492
  109.2 30.6 %collective-permute-start.16 = (bf16[128,2048]{1,0:T(8,128)(2,1)S(1)}, bf16[128,2048]{1,0:T(8,128)(2,1)S(1)}, u32[]{:S(2)}, u32[]{:S(2)}) collective-permute-start(bf16[128,2048]{1,0:T(8,128)(2,1)S(1)} %get-tuple-element.109), channel_id=1, source_target_pairs={{0,2},{2,4},{4,6},{6,7},{7,5},{5,3},{3,1},{1,0},{8,10},{10,12},{12... | collective-permute-start | bytes 1572872 | tf_op jit(solution)/shard_map/ppermute | solution.py:399
  110.8 28.9 %collective-permute-start.17 = (bf16[128,2048]{1,0:T(8,128)(2,1)S(1)}, bf16[128,2048]{1,0:T(8,128)(2,1)S(1)}, u32[]{:S(2)}, u32[]{:S(2)}) collective-permute-start(bf16[128,2048]{1,0:T(8,128)(2,1)S(1)} %get-tuple-element.111), channel_id=1, source_target_pairs={{2,0},{4,2},{6,4},{7,6},{5,7},{3,5},{1,3},{0,1},{10,8},{12,10},{14... | collective-permute-start | bytes 1572872 | tf_op jit(solution)/shard_map/ppermute | solution.py:400
  139.7 18.5 %collective-permute-start.45 = (bf16[4,160,512]{2,1,0:T(8,128)(2,1)S(1)}, bf16[4,160,512]{2,1,0:T(8,128)(2,1)S(1)}, u32[]{:S(2)}, u32[]{:S(2)}) collective-permute-start(bf16[4,160,512]{2,1,0:T(8,128)(2,1)S(1)} %get-tuple-element.143), channel_id=1, source_target_pairs={{0,24},{8,16},{16,8},{24,0},{1,25},{9,17},{17,9},{25,1},{2,26},{10... | collective-permute-start | bytes 1966088 | tf_op jit(solution)/shard_map/ppermute | solution.py:492
  139.8 20.6 %collective-permute-start.47 = (bf16[4,160,512]{2,1,0:T(8,128)(2,1)S(1)}, bf16[4,160,512]{2,1,0:T(8,128)(2,1)S(1)}, u32[]{:S(2)}, u32[]{:S(2)}) collective-permute-start(bf16[4,160,512]{2,1,0:T(8,128)(2,1)S(1)} %get-tuple-element.145), channel_id=1, source_target_pairs={{0,8},{8,0},{16,24},{24,16},{1,9},{9,1},{17,25},{25,17},{2,10},{10... | collective-permute-start | bytes 1966088 | tf_op jit(solution)/shard_map/ppermute | solution.py:492
  145.5 23.4 %collective-permute-start.49 = (bf16[4,160,512]{2,1,0:T(8,128)(2,1)S(1)}, bf16[4,160,512]{2,1,0:T(8,128)(2,1)S(1)}, u32[]{:S(2)}, u32[]{:S(2)}) collective-permute-start(bf16[4,160,512]{2,1,0:T(8,128)(2,1)S(1)} %get-tuple-element.147), channel_id=1, source_target_pairs={{0,16},{8,24},{16,0},{24,8},{1,17},{9,25},{17,1},{25,9},{2,18},{10... | collective-permute-start | bytes 1966088 | tf_op jit(solution)/shard_map/ppermute | solution.py:492
  154.8 18.4 %collective-permute-start.18 = (bf16[128,2048]{1,0:T(8,128)(2,1)S(1)}, bf16[128,2048]{1,0:T(8,128)(2,1)S(1)}, u32[]{:S(2)}, u32[]{:S(2)}) collective-permute-start(bf16[128,2048]{1,0:T(8,128)(2,1)S(1)} %get-tuple-element.112), channel_id=1, source_target_pairs={{0,2},{2,4},{4,6},{6,7},{7,5},{5,3},{3,1},{1,0},{8,10},{10,12},{12... | collective-permute-start | bytes 1572872 | tf_op jit(solution)/shard_map/ppermute | solution.py:399
  173.2 69.2 %collective-permute-start.58 = (bf16[2,2,384,512]{3,2,1,0:T(8,128)(2,1)S(1)}, bf16[2,2,384,512]{3,2,1,0:T(8,128)(2,1)S(1)}, u32[]{:S(2)}, u32[]{:S(2)}) collective-permute-start(bf16[2,2,384,512]{3,2,1,0:T(8,128)(2,1)S(1)} %get-tuple-element.157), channel_id=1, source_target_pairs={{0,8},{8,0},{16,24},{24,16},{1,9},{9,1},{17,25},{25,17},{2,10},{10... | collective-permute-start | bytes 4718600 | tf_op jit(solution)/shard_map/ppermute | solution.py:513
  174.9 24.6 %collective-permute-start.50 = (bf16[2,320,768]{2,1,0:T(8,128)(2,1)S(1)}, bf16[2,320,768]{2,1,0:T(8,128)(2,1)S(1)}, u32[]{:S(2)}, u32[]{:S(2)}) collective-permute-start(bf16[2,320,768]{2,1,0:T(8,128)(2,1)S(1)} %get-tuple-element.150.refs_11_), channel_id=1, source_target_pairs={{0,16},{8,24},{16,0},{24,8},{1,17},{9,25},{17,1},{25,9},{2,18},{10... | collective-permute-start | bytes 2949128 | tf_op jit(solution)/shard_map/ppermute | solution.py:508
  176.6 43.1 %collective-permute-start.53 = (bf16[2,320,768]{2,1,0:T(8,128)(2,1)S(1)}, bf16[2,320,768]{2,1,0:T(8,128)(2,1)S(1)}, u32[]{:S(2)}, u32[]{:S(2)}) collective-permute-start(bf16[2,320,768]{2,1,0:T(8,128)(2,1)S(1)} %get-tuple-element.151.refs_11_), channel_id=1, source_target_pairs={{0,16},{8,24},{16,0},{24,8},{1,17},{9,25},{17,1},{25,9},{2,18},{10... | collective-permute-start | bytes 2949128 | tf_op jit(solution)/shard_map/ppermute | solution.py:508
  178.0 43.8 %collective-permute-start.55 = (bf16[2,320,768]{2,1,0:T(8,128)(2,1)S(1)}, bf16[2,320,768]{2,1,0:T(8,128)(2,1)S(1)}, u32[]{:S(2)}, u32[]{:S(2)}) collective-permute-start(bf16[2,320,768]{2,1,0:T(8,128)(2,1)S(1)} %get-tuple-element.151.refs_11_), channel_id=1, source_target_pairs={{0,8},{8,0},{16,24},{24,16},{1,9},{9,1},{17,25},{25,17},{2,10},{10... | collective-permute-start | bytes 2949128 | tf_op jit(solution)/shard_map/ppermute | solution.py:509
  182.3 60.3 %collective-permute-start.56 = (bf16[2,2,384,512]{3,2,1,0:T(8,128)(2,1)S(1)}, bf16[2,2,384,512]{3,2,1,0:T(8,128)(2,1)S(1)}, u32[]{:S(2)}, u32[]{:S(2)}) collective-permute-start(bf16[2,2,384,512]{3,2,1,0:T(8,128)(2,1)S(1)} %get-tuple-element.155), channel_id=1, source_target_pairs={{0,8},{8,0},{16,24},{24,16},{1,9},{9,1},{17,25},{25,17},{2,10},{10... | collective-permute-start | bytes 4718600 | tf_op jit(solution)/shard_map/ppermute | solution.py:513
  199.6 23.2 %collective-permute-start.35 = (bf16[64,2048]{1,0:T(8,128)(2,1)S(1)}, bf16[64,2048]{1,0:T(8,128)(2,1)S(1)}, u32[]{:S(2)}, u32[]{:S(2)}) collective-permute-start(bf16[64,2048]{1,0:T(8,128)(2,1)S(1)} %get-tuple-element.133), channel_id=1, source_target_pairs={{0,2},{2,4},{4,6},{6,7},{7,5},{5,3},{3,1},{1,0},{8,10},{10,12},{12... | collective-permute-start | bytes 786440 | tf_op jit(solution)/shard_map/ppermute | solution.py:417
  221.8 19.0 %collective-permute-start.20 = (bf16[128,2048]{1,0:T(8,128)(2,1)S(1)}, bf16[128,2048]{1,0:T(8,128)(2,1)S(1)}, u32[]{:S(2)}, u32[]{:S(2)}) collective-permute-start(bf16[128,2048]{1,0:T(8,128)(2,1)S(1)} %get-tuple-element.115), channel_id=1, source_target_pairs={{0,2},{2,4},{4,6},{6,7},{7,5},{5,3},{3,1},{1,0},{8,10},{10,12},{12... | collective-permute-start | bytes 1572872 | tf_op jit(solution)/shard_map/ppermute | solution.py:404
  240.3 18.7 %collective-permute-start.54 = (bf16[2,320,768]{2,1,0:T(8,128)(2,1)S(1)}, bf16[2,320,768]{2,1,0:T(8,128)(2,1)S(1)}, u32[]{:S(2)}, u32[]{:S(2)}) collective-permute-start(bf16[2,320,768]{2,1,0:T(8,128)(2,1)S(1)} %collective-permute-done.53.refs_10_), channel_id=1, source_target_pairs={{0,8},{8,0},{16,24},{24,16},{1,9},{9,1},{17,25},{25,17},{2,10},{10... | collective-permute-start | bytes 2949128 | tf_op jit(solution)/shard_map/ppermute | solution.py:510
  240.3 22.1 %collective-permute-start.52 = (bf16[2,320,768]{2,1,0:T(8,128)(2,1)S(1)}, bf16[2,320,768]{2,1,0:T(8,128)(2,1)S(1)}, u32[]{:S(2)}, u32[]{:S(2)}) collective-permute-start(bf16[2,320,768]{2,1,0:T(8,128)(2,1)S(1)} %get-tuple-element.150.refs_11_), channel_id=1, source_target_pairs={{0,8},{8,0},{16,24},{24,16},{1,9},{9,1},{17,25},{25,17},{2,10},{10... | collective-permute-start | bytes 2949128 | tf_op jit(solution)/shard_map/ppermute | solution.py:509
  242.4 19.9 %collective-permute-start.51 = (bf16[2,320,768]{2,1,0:T(8,128)(2,1)S(1)}, bf16[2,320,768]{2,1,0:T(8,128)(2,1)S(1)}, u32[]{:S(2)}, u32[]{:S(2)}) collective-permute-start(bf16[2,320,768]{2,1,0:T(8,128)(2,1)S(1)} %collective-permute-done.50.refs_10_), channel_id=1, source_target_pairs={{0,8},{8,0},{16,24},{24,16},{1,9},{9,1},{17,25},{25,17},{2,10},{10... | collective-permute-start | bytes 2949128 | tf_op jit(solution)/shard_map/ppermute | solution.py:510
  242.6 23.1 %collective-permute-start.59 = (bf16[2,384,512]{2,1,0:T(8,128)(2,1)S(1)}, bf16[2,384,512]{2,1,0:T(8,128)(2,1)S(1)}, u32[]{:S(2)}, u32[]{:S(2)}) collective-permute-start(bf16[2,384,512]{2,1,0:T(8,128)(2,1)S(1)} %fusion.1), channel_id=1, source_target_pairs={{0,16},{8,24},{16,0},{24,8},{1,17},{9,25},{17,1},{25,9},{2,18},{10... | collective-permute-start | bytes 2359304 | tf_op jit(solution)/shard_map/ppermute | solution.py:514
  254.9 24.7 %collective-permute-start.57 = (bf16[2,384,512]{2,1,0:T(8,128)(2,1)S(1)}, bf16[2,384,512]{2,1,0:T(8,128)(2,1)S(1)}, u32[]{:S(2)}, u32[]{:S(2)}) collective-permute-start(bf16[2,384,512]{2,1,0:T(8,128)(2,1)S(1)} %fusion), channel_id=1, source_target_pairs={{0,16},{8,24},{16,0},{24,8},{1,17},{9,25},{17,1},{25,9},{2,18},{10... | collective-permute-start | bytes 2359304 | tf_op jit(solution)/shard_map/ppermute | solution.py:514
  (41 other events, 788.1 us)
